TPU v7x, 512 devices: a whole 4x4x16 slice. The times are simulated.
512 devices in a mesh: seq: 32 (over z, core), heads: 4 (over x), dp: 4 (over y).
Axes of the slice: x: 4, y: 4, z: 16, core: 2. Of those that a mesh axis runs over, the one named last changes fastest.
Arguments:
- tokens: bfloat16 [4, 4096, 3072], P('dp', 'seq'), may hold values from -6 to 6
- proj_weights: bfloat16 [3, 3072, 4096], P(None, 'seq', ('heads', 'dp')), may hold values from -0.109375 to 0.109375
- norm_gain: float32 [4096], P(('heads', 'dp')), may hold values from 0.5 to 1.5
Outputs:
- attended: bfloat16 [4, 4096, 4096], P('dp', 'seq', 'heads')
All inputs are finite; a program needn't handle non-finite values.
Results may differ from a plain program's by a relative error of at most 0.0063.
Values may be sent and summed in bfloat16 or wider, within the bound.
No kernel may reach another device: no remote copies, remote signals or barrier semaphores. Data moves between devices by JAX's collectives and lax.ppermute only.
A program may use at most 64 MiB of HBM per device.

v0:
```python
import jax
import jax.numpy as jnp
from jax import lax
from jax.sharding import PartitionSpec as P

DH = 128


def prefix_2(part, axis, combine, identity):
    place = lax.axis_index(axis)
    gathered = lax.all_gather(part, axis)
    state = jnp.zeros_like(part) + jnp.asarray(identity, part.dtype)

    def one(step, state):
        return combine(state, lax.dynamic_index_in_dim(gathered, step, 0, False))

    return lax.fori_loop(0, place, one, state)


def add_pair(earlier, later):
    return earlier + later


def project_rows(flat_rows):

    def accumulate(total, piece, start):
        return jnp.einsum("nd,jdc->jnc", flat_rows, piece, preferred_element_type=jnp.float32)

    return accumulate


def to_heads(matrix, seq_count, length):
    return matrix.reshape(seq_count, length, -1, DH)


def activate(matrix, seq_count, length):
    return to_heads(jax.nn.silu(matrix).astype(jnp.bfloat16), seq_count, length)


def block_prefix(keys_b, values_b):
    state = jnp.einsum("sthd,sthe->shde", keys_b, values_b, preferred_element_type=jnp.float32)
    return prefix_2(state, "seq", add_pair, jnp.zeros_like(state))


def attend(queries, keys_b, values_b, prefix, norm_gain):
    seq_count, length, head_count, head_size = queries.shape
    scores = jnp.einsum("sthd,suhd->shtu", queries, keys_b, preferred_element_type=jnp.float32)
    causal = lax.broadcasted_iota(jnp.int32, (length, length), 0) >= lax.broadcasted_iota(
        jnp.int32, (length, length), 1
    )
    scores_b = jnp.where(causal, scores, 0.0).astype(jnp.bfloat16)
    local = jnp.einsum("shtu,suhd->sthd", scores_b, values_b, preferred_element_type=jnp.float32)
    carried = jnp.einsum(
        "sthd,shde->sthe", queries, prefix.astype(jnp.bfloat16), preferred_element_type=jnp.float32
    )
    attn = local + carried
    scale = lax.rsqrt(jnp.mean(attn * attn, axis=-1, keepdims=True) + 1e-06)
    normed = attn * scale * norm_gain.reshape(head_count, head_size)
    return normed.astype(jnp.bfloat16).reshape(seq_count, length, head_count * head_size)


def body(tokens, proj_weights, norm_gain):
    everyone = lax.all_gather(tokens, "dp", axis=0, tiled=True)
    seq_count, length, width = everyone.shape
    total_rows = seq_count * length
    per_device = proj_weights.shape[2]
    accumulate = project_rows(everyone.reshape(total_rows, width))
    start_sum = jnp.zeros((3, total_rows, per_device), jnp.float32)
    projected = accumulate(
        start_sum, lax.all_gather(proj_weights, "seq", axis=1, tiled=True), jnp.int32(0)
    )
    queries = activate(projected[0], seq_count, length)
    keys_b = activate(projected[1], seq_count, length)
    values_b = to_heads(projected[2].astype(jnp.bfloat16), seq_count, length)
    prefix = block_prefix(keys_b, values_b)
    normed = attend(queries, keys_b, values_b, prefix, norm_gain)
    return lax.all_to_all(normed, "dp", split_axis=0, concat_axis=2, tiled=True)


def solution(mesh):
    in_specs = (P("dp", "seq", None), P(None, "seq", ("heads", "dp")), P(("heads", "dp")))
    out_specs = P("dp", "seq", "heads")
    return jax.shard_map(body, mesh=mesh, in_specs=in_specs, out_specs=out_specs, check_vma=False)
```

profile of v0, /device:TPU:481, one launch (start us, length us, event | category | flops | bytes accessed | tf_op | source)
XLA Modules:
  0.0 297.7 jit_solution(694654217346947341)
XLA Ops:
  6.5 0.7 all-gather.7.cloned.1.call-update
  7.3 0.7 all-gather.5.cloned.1.call-update
  8.1 47.7 %all-gather.7.cloned.1.call-done = bf16[4,128,3072]{2,1,0:T(8,128)(2,1)} async-done(((bf16[1,128,3072]{2,1,0:T(8,128)(2,1)}), bf16[4,128,3072]{2,1,0:T(8,128)(2,1)}) %all-gather.7.cloned.1.call-update) | async-done | bytes 3145744 | tf_op jit(solution)/shard_map/all_gather | solution.py:63
  55.8 76.4 %all-gather.5.cloned.1.call-done = bf16[3,3072,256]{2,1,0:T(8,128)(2,1)} async-done(((bf16[3,96,256]{2,1,0:T(8,128)(2,1)}), bf16[3,3072,256]{2,1,0:T(8,128)(2,1)}) %all-gather.5.cloned.1.call-update) | async-done | bytes 4718608 | tf_op jit(solution)/shard_map/all_gather | solution.py:70
  132.1 5.5 %convolution_bitcast_fusion = f32[3,512,256]{1,2,0:T(8,128)S(1)} fusion(bf16[3,3072,256]{2,1,0:T(8,128)(2,1)} %all-gather.5.cloned.1.call-done, bf16[512,3072,1]{1,0,2:T(8,128)(2,1)} %bitcast.33), kind=kOutput, calls=%fused_computation.1 | convolution fusion | flops 2415919104 | bytes 9437184 | tf_op jit(solution)/shard_map/nd,jdc->jnc/dot_general | solution.py:27
  137.7 0.2 squeeze.12
  137.9 0.2 copy.16
  138.2 0.2 copy.19
  138.4 1.1 fusion.7
  139.6 0.2 squeeze.11
  139.8 0.2 copy.14
  140.0 0.6 fusion.2
  140.6 101.5 %all-gather.9.cloned.1.call-done = f32[128,2,128,128]{3,2,1,0:T(8,128)} async-done(((f32[4,2,128,128]{3,2,1,0:T(8,128)}), f32[128,2,128,128]{3,2,1,0:T(8,128)}) %all-gather.9.cloned.1.call-update) | async-done | bytes 16777232 | tf_op jit(solution)/shard_map/all_gather | solution.py:11
  242.2 37.0 %while.10 = (s32[]{:T(128)}, f32[4,2,128,128]{3,2,1,0:T(8,128)S(1)}, s32[]{:T(128)}, f32[32,4,2,128,128]{4,3,2,1,0:T(8,128)}, s32[]{:T(128)}, /*index=5*/s32[]{:T(128)}, s32[]{:T(128)}) while((s32[]{:T(128)}, f32[4,2,128,128]{3,2,1,0:T(8,128)S(1)}, s32[]{:T(128)}, f32[32,4,2,128,128]{4,3,2,1,0:T(8,128)}, s32[]{:T(128)}, /*index=5*/s32[]{:T(128)}, ...), condition=%wide.region_1.2_spmd, body=%wide.region_0.1_spmd.sunk | while | flops 131077 | bytes 1572987 | solution.py:17
  242.2 1.2 bitcast_add_fusion.2
  243.4 1.2 bitcast_add_fusion.2
  244.6 1.2 bitcast_add_fusion.2
  245.8 1.2 bitcast_add_fusion.2
  247.0 1.2 bitcast_add_fusion.2
  248.2 1.2 bitcast_add_fusion.2
  249.3 1.2 bitcast_add_fusion.2
  250.5 1.2 bitcast_add_fusion.2
  251.7 1.2 bitcast_add_fusion.2
  252.9 1.2 bitcast_add_fusion.2
  254.1 1.2 bitcast_add_fusion.2
  255.3 1.2 bitcast_add_fusion.2
  256.5 1.2 bitcast_add_fusion.2
  257.7 1.2 bitcast_add_fusion.2
  258.9 1.2 bitcast_add_fusion.2
  260.1 1.2 bitcast_add_fusion.2
  261.3 1.2 bitcast_add_fusion.2
  262.5 1.2 bitcast_add_fusion.2
  263.7 1.2 bitcast_add_fusion.2
  264.9 1.2 bitcast_add_fusion.2
  266.0 1.2 bitcast_add_fusion.2
  267.2 1.2 bitcast_add_fusion.2
  268.4 1.2 bitcast_add_fusion.2
  269.6 1.2 bitcast_add_fusion.2
  270.8 1.2 bitcast_add_fusion.2
  272.0 1.2 bitcast_add_fusion.2
  273.2 1.2 bitcast_add_fusion.2
  274.4 1.2 bitcast_add_fusion.2
  275.6 1.2 bitcast_add_fusion.2
  276.8 1.2 bitcast_add_fusion.2
  278.0 1.2 bitcast_add_fusion.2
  279.2 0.4 multiply_reduce_fusion
  279.7 10.6 %all_to_all.18 = bf16[4,128,256]{1,2,0:T(8,128)(2,1)S(1)} all-to-all(bf16[4,128,256]{1,2,0:T(8,128)(2,1)S(1)} %bitcast.29), channel_id=1, replica_groups=mesh['seq'=32,'heads'=4,'dp'=4] {'dp'}, dimensions={0} | all-to-all | bytes 524288 | tf_op jit(solution)/shard_map/all_to_all | solution.py:77
  290.3 0.8 copy.24
  (13 shorter events, 0.4 us)
Async XLA Ops:
  6.5 49.2 %all-gather.7.cloned.1.call-start = ((), (), s32[]{:S(2)}) async-start(), calls=%async_computation.2 | async-start | bytes 3932160 | tf_op jit(solution)/shard_map/all_gather | solution.py:63
  7.3 124.9 %all-gather.5.cloned.1.call-start = ((), (), s32[]{:S(2)}) async-start(), calls=%async_computation.1 | async-start | bytes 4866048 | tf_op jit(solution)/shard_map/all_gather | solution.py:70
  8.0 234.1 %all-gather.9.cloned.1.call-start = ((), (), s32[]{:S(2)}) async-start(), calls=%async_computation.3 | async-start | bytes 17301504 | tf_op jit(solution)/shard_map/all_gather | solution.py:11
  242.1 37.4 %copy-start = (f32[256]{0:T(256)S(1)}, f32[256]{0:T(256)}, u32[]{:S(2)}) copy-start(f32[256]{0:T(256)} %param.7) | copy-start | bytes 3076
Sparse Core Ops, SparseCore 0:
  9.5 46.2 all-gather.6
  57.9 74.1 all-gather.4
  139.7 102.3 all-gather.8
where the time goes:
time: 299 us; the launch traced here: 298 us
  waiting for transfers between devices  227 us (76%)
  other arithmetic  36.4 us (12%)
  between operations  13.2 us (4%)
  blocking collectives  10.6 us (4%)
  matrix products  7.57 us (3%)
    all_gather x1, waiting for transfers between devices, prefix_2(): gathered = lax.all_gather(part, axis)  101 us
    all_gather x1, waiting for transfers between devices, body(): lax.all_gather(proj_weights, 'seq', axis=1, tiled=True)  76.4 us
    all_gather x1, waiting for transfers between devices, body(): everyone = lax.all_gather(tokens, 'dp', axis=0, tiled=True)  47.7 us
    add x31, other arithmetic, add_pair(): return earlier + later  36.3 us
    all_to_all x1, blocking collectives, body(): return lax.all_to_all(normed, 'dp', split_axis=0, concat_axis=2, tiled=True)  10.6 us
  transfers between devices with their start and end apart: 3, of which 3 were waited for; matrix products, arithmetic and copies ran while one was open for 0% of the time, Pallas kernels for 0%

commit v1 on v0

v1 whole, which is shorter than its diff:
```python
import jax
import jax.numpy as jnp
from jax import lax
from jax.sharding import PartitionSpec as P

DH = 128
SEQ = 32
WSCALE = 2.0**19
SAME_CORE = [[2 * z + c for z in range(16)] for c in range(2)]
SIBLING = [(i, i ^ 1) for i in range(SEQ)]
QUAD = [[8 * a + 2 * b + c for b in range(4)] for a in range(4) for c in range(2)]
ACROSS = [[8 * a + 2 * b + c for a in range(4)] for b in range(4) for c in range(2)]
F32 = jnp.float32
B16 = jnp.bfloat16


def body(tokens, proj_weights, norm_gain):
    place = lax.axis_index("seq")
    core = place % 2
    quad_place = (place // 2) % 4
    quad = place // 8
    mine_t = lax.all_to_all(jnp.broadcast_to(tokens, (4,) + tokens.shape[1:]), "dp", 0, 0, tiled=True)
    wh = (proj_weights.astype(F32) * WSCALE).astype(jnp.float16)
    wh = jnp.transpose(wh, (1, 0, 2)).reshape(96, 3, 2, DH)
    head0, head1 = wh[:, :, 0].reshape(96, 3 * DH), wh[:, :, 1].reshape(96, 3 * DH)
    first = core == 0
    keep = jnp.where(first, head0, head1)
    give = jnp.where(first, head1, head0)
    got = lax.ppermute(give, "seq", SIBLING)
    rows = jnp.concatenate([jnp.where(first, keep, got), jnp.where(first, got, keep)], axis=0)
    full = lax.all_gather(rows, "seq", axis=0, tiled=True, axis_index_groups=SAME_CORE)
    mine_t, full = lax.optimization_barrier((mine_t, full))
    weights = (full.astype(F32) * (1.0 / WSCALE)).astype(B16)
    other_t = lax.ppermute(mine_t, "seq", SIBLING)

    def project(t):
        out = jnp.dot(t.reshape(4 * 128, -1), weights, preferred_element_type=F32)
        out = out.reshape(4, 128, 3, DH)
        return (jax.nn.silu(out[:, :, 0]).astype(B16), jax.nn.silu(out[:, :, 1]).astype(B16), out[:, :, 2].astype(B16))

    qa, ka, va = project(mine_t)
    qb, kb, vb = project(other_t)
    sa = jnp.einsum("std,ste->sde", ka, va, preferred_element_type=F32)
    sb = jnp.einsum("std,ste->sde", kb, vb, preferred_element_type=F32)
    chip = (sa + sb).astype(B16)
    in_quad = lax.all_gather(chip, "seq", axis=0, axis_index_groups=QUAD).astype(F32)
    total = jnp.sum(in_quad, axis=0)
    before = jnp.sum(jnp.where((jnp.arange(4) < quad_place)[:, None, None, None], in_quad, 0.0), axis=0)
    quads = lax.all_gather(total.astype(B16), "seq", axis=0, axis_index_groups=ACROSS).astype(F32)
    before = before + jnp.sum(jnp.where((jnp.arange(4) < quad)[:, None, None, None], quads, 0.0), axis=0)
    pa = (before + jnp.where(first, 0.0, sb)).astype(B16)
    pb = (before + jnp.where(first, sa, 0.0)).astype(B16)
    gain = lax.dynamic_slice_in_dim(norm_gain, core * DH, DH)

    def attend(q, k, v, p):
        s = jnp.einsum("std,sud->stu", q, k, preferred_element_type=F32)
        causal = lax.broadcasted_iota(jnp.int32, (128, 128), 0) >= lax.broadcasted_iota(jnp.int32, (128, 128), 1)
        s = jnp.where(causal, s, 0.0).astype(B16)
        attn = jnp.einsum("stu,sue->ste", s, v, preferred_element_type=F32)
        attn = attn + jnp.einsum("std,sde->ste", q, p, preferred_element_type=F32)
        scale = lax.rsqrt(jnp.mean(attn * attn, axis=-1, keepdims=True) + 1e-06)
        return (attn * scale * gain).astype(B16)

    oa = attend(qa, ka, va, pa)
    ob = attend(qb, kb, vb, pb)
    sib = lax.ppermute(ob, "seq", SIBLING)
    out = jnp.concatenate([jnp.where(first, oa, sib), jnp.where(first, sib, oa)], axis=-1)
    return lax.all_to_all(out, "dp", split_axis=0, concat_axis=2, tiled=True)


def solution(mesh):
    in_specs = (P("dp", "seq", None), P(None, "seq", ("heads", "dp")), P(("heads", "dp")))
    out_specs = P("dp", "seq", "heads")
    return jax.shard_map(body, mesh=mesh, in_specs=in_specs, out_specs=out_specs, check_vma=False)
```

time: 299 us -> 139 us (0.46)
  the two profiles are of different devices: /device:TPU:481 before, /device:TPU:1 now
where the time goes in v1:
time: 139 us
  blocking collectives  88.4 us (64%)
  starting transfers between devices  27.2 us (20%)
  matrix products  9.3 us (7%)
  local copies, waits for them, and re-layouts  8.46 us (6%)
  other arithmetic  3.09 us (2%)
  waiting for transfers between devices  1.85 us (1%)
    all_gather x1, blocking collectives, body(): lax.all_gather(rows, 'seq', axis=0, tiled=True, axis_index_groups=SAME_CORE)  39.9 us
    all_gather x1, blocking collectives, body(): lax.all_gather(total.astype(B16), 'seq', axis=0, axis_index_groups=ACROSS)  23.5 us
    all_gather x1, blocking collectives, body(): lax.all_gather(chip, 'seq', axis=0, axis_index_groups=QUAD).astype(F32)  13.8 us
    all_to_all x1, blocking collectives, body(): return lax.all_to_all(out, 'dp', split_axis=0, concat_axis=2, tiled=True)  11.3 us
    ppermute x1, starting transfers between devices, body(): got = lax.ppermute(give, 'seq', SIBLING)  8.46 us
    ppermute x1, starting transfers between devices, body(): other_t = lax.ppermute(mine_t, 'seq', SIBLING)  8.23 us
    dot_general x2, matrix products, project(): out = jnp.dot(t.reshape(4 * 128, -1), weights, preferred_element_type=F32)  7.38 us
    ppermute x1, starting transfers between devices, body(): sib = lax.ppermute(ob, 'seq', SIBLING)  5.36 us
  transfers between devices with their start and end apart: 4, of which 2 were waited for; matrix products, arithmetic and copies ran while one was open for 7% of the time, Pallas kernels for 0%

profile of v1, /device:TPU:1, one launch (start us, length us, event | category | flops | bytes accessed | tf_op | source)
XLA Modules:
  0.0 138.6 jit_solution(9068452318912237880)
XLA Ops:
  0.0 3.2 %broadcast_in_dim.49 = bf16[4,128,3072]{2,1,0:T(8,128)(2,1)} broadcast(bf16[128,3072]{1,0:T(8,128)(2,1)} %bitcast.98), dimensions={1,2} | broadcast | bytes 3932160 | tf_op jit(solution)/shard_map/broadcast_in_dim | solution.py:22
  3.2 0.0 copy-start
  3.2 5.1 %all-to-all-start = ((bf16[4,128,3072]{2,1,0:T(8,128)(2,1)}), bf16[4,128,3072]{2,1,0:T(8,128)(2,1)}, u32[]{:S(2)}, u32[]{:S(2)}) async-start(bf16[4,128,3072]{2,1,0:T(8,128)(2,1)} %broadcast_in_dim.49), calls=%async_computation | async-start | bytes 6291456 | tf_op jit(solution)/shard_map/all_to_all | solution.py:22
  8.3 0.0 copy-start.1
  8.3 0.0 copy-done
  8.4 0.1 reshape.44
  8.4 0.3 fusion.33
  8.7 0.2 broadcast_select_fusion.3
  9.0 8.5 %collective-permute-start = (f16[96,384]{1,0:T(8,128)(2,1)S(1)}, f16[96,384]{1,0:T(8,128)(2,1)S(1)}, u32[]{:S(2)}, u32[]{:S(2)}) collective-permute-start(f16[96,384]{1,0:T(8,128)(2,1)S(1)} %bitcast.101), channel_id=1, source_target_pairs={{0,16},{16,0},{32,48},{48,32},{64,80},{80,64},{96,112},{112,96},{1... | collective-permute-start | bytes 221192 | tf_op jit(solution)/shard_map/ppermute | solution.py:29
  17.4 0.9 collective-permute-done
  18.4 39.9 %all-gather.3 = f16[3072,384]{1,0:T(8,128)(2,1)S(1)} all-gather(f16[192,384]{1,0:T(8,128)(2,1)S(1)} %pad_maximum_fusion.1), channel_id=1, replica_groups={{0,32,64,96,128,160,192,224,256,288,320,352,384,416,448,480},{16,48,80,..., dimensions={0}, use_global_device_ids=true | all-gather | bytes 2506752 | tf_op jit(solution)/shard_map/all_gather | solution.py:31
  58.3 0.0 all-to-all-done
  58.3 8.2 %collective-permute-start.1 = (bf16[4,128,3072]{2,1,0:T(8,128)(2,1)}, bf16[4,128,3072]{2,1,0:T(8,128)(2,1)}, u32[]{:S(2)}, u32[]{:S(2)}) collective-permute-start(bf16[4,128,3072]{2,1,0:T(8,128)(2,1)} %all-to-all-done), channel_id=1, source_target_pairs={{0,16},{16,0},{32,48},{48,32},{64,80},{80,64},{96,112},{112,96},{1... | collective-permute-start | bytes 9437192 | tf_op jit(solution)/shard_map/ppermute | solution.py:34
  66.6 0.0 copy-done.1
  66.6 0.1 dynamic_slice.3
  66.7 2.0 %fusion.4 = bf16[384,3072]{0,1:T(8,128)(2,1)} fusion(f16[3072,384]{1,0:T(8,128)(2,1)S(1)} %all-gather.3), kind=kLoop, calls=%fused_computation.5 | loop fusion | flops 3538944 | bytes 4718592 | tf_op jit(solution)/shard_map/dot_general | solution.py:37
  68.7 2.8 %copy.68 = bf16[384,3072]{1,0:T(8,128)(2,1)S(1)} copy(bf16[384,3072]{0,1:T(8,128)(2,1)} %fusion.4) | data formatting | bytes 4718592 | tf_op jit(solution)/shard_map/dot_general | solution.py:37
  71.5 3.7 %fusion.2 = f32[4,128,3,128]{3,1,2,0:T(8,128)S(1)} fusion(bf16[3,128,3072,1]{2,1,0,3:T(8,128)(2,1)S(1)} %bitcast.93, bf16[4,128,3072]{2,1,0:T(8,128)(2,1)} %all-to-all-done), kind=kOutput, calls=%fused_computation.3 | convolution fusion | flops 1207959552 | bytes 6291456 | tf_op jit(solution)/shard_map/dot_general | solution.py:37
  75.2 0.0 copy-start.2
  75.2 0.4 fusion.8
  75.6 0.5 copy-done.2
  76.1 0.0 collective-permute-done.1
  76.1 3.7 %fusion = f32[4,128,3,128]{3,1,2,0:T(8,128)S(1)} fusion(bf16[3,128,3072,1]{2,1,0,3:T(8,128)(2,1)S(1)} %bitcast.94, bf16[4,128,3072]{2,1,0:T(8,128)(2,1)} %collective-permute-done.1), kind=kOutput, calls=%fused_computation.1 | convolution fusion | flops 1207959552 | bytes 6291456 | tf_op jit(solution)/shard_map/dot_general | solution.py:37
  79.8 0.0 copy-start.3
  79.8 0.3 fusion.24
  80.1 0.4 fusion.7
  80.5 0.5 copy-done.3
  80.9 0.3 add_convert_fusion.2
  81.2 13.8 %all-gather = bf16[16,128,128]{2,1,0:T(8,128)(2,1)S(1)} all-gather(bf16[4,128,128]{2,1,0:T(8,128)(2,1)S(1)} %get-tuple-element.17), channel_id=2, replica_groups={{0,32,64,96},{16,48,80,112},{128,160,192,224},{144,176,208,240},{256,28..., dimensions={0}, use_global_device_ids=true | all-gather | bytes 655360 | tf_op jit(solution)/shard_map/all_gather | solution.py:46
  95.0 0.1 reduce_sum.49
  95.1 23.5 %all-gather.1 = bf16[16,128,128]{2,1,0:T(8,128)(2,1)S(1)} all-gather(bf16[4,128,128]{2,1,0:T(8,128)(2,1)S(1)} %reduce_sum.49), channel_id=3, replica_groups={{0,128,256,384},{16,144,272,400},{32,160,288,416},{48,176,304,432},{64,..., dimensions={0}, use_global_device_ids=true | all-gather | bytes 655360 | tf_op jit(solution)/shard_map/all_gather | solution.py:49
  118.6 0.2 select_reduce_fusion
  118.8 0.2 fusion.9
  119.0 0.3 multiply_reduce_fusion.1
  119.3 0.3 multiply_reduce_fusion
  119.6 0.1 multiply_convert_fusion.2
  119.8 5.4 %collective-permute-start.2 = (bf16[4,128,128]{2,1,0:T(8,128)(2,1)S(1)}, bf16[4,128,128]{2,1,0:T(8,128)(2,1)S(1)}, u32[]{:S(2)}, u32[]{:S(2)}) collective-permute-start(bf16[4,128,128]{2,1,0:T(8,128)(2,1)S(1)} %multiply_convert_fusion.2), channel_id=1, source_target_pairs={{0,16},{16,0},{32,48},{48,32},{64,80},{80,64},{96,112},{112,96},{1... | collective-permute-start | bytes 393224 | tf_op jit(solution)/shard_map/ppermute | solution.py:66
  125.1 1.0 collective-permute-done.2
  126.1 0.1 broadcast_select_fusion.1
  126.3 11.3 %all_to_all.23 = bf16[4,128,256]{2,1,0:T(8,128)(2,1)S(1)} all-to-all(bf16[4,128,256]{2,1,0:T(8,128)(2,1)S(1)} %pad_maximum_fusion), channel_id=1, replica_groups=mesh['seq'=32,'heads'=4,'dp'=4] {'dp'}, dimensions={0} | all-to-all | bytes 524288 | tf_op jit(solution)/shard_map/all_to_all | solution.py:68
  137.5 0.2 copy.82
  137.7 0.9 copy.83
  (10 shorter events, 0.2 us)
Async XLA Ops:
  3.2 5.2 %copy-start = (bf16[3,96,256]{2,1,0:T(8,128)(2,1)S(1)}, bf16[3,96,256]{2,1,0:T(8,128)(2,1)}, u32[]{:S(2)}) copy-start(bf16[3,96,256]{2,1,0:T(8,128)(2,1)} %param.4) | copy-start | bytes 442372
  3.2 55.1 %all-to-all-start = ((bf16[4,128,3072]{2,1,0:T(8,128)(2,1)}), bf16[4,128,3072]{2,1,0:T(8,128)(2,1)}, u32[]{:S(2)}, u32[]{:S(2)}) async-start(bf16[4,128,3072]{2,1,0:T(8,128)(2,1)} %broadcast_in_dim.49), calls=%async_computation | async-start | bytes 6291456 | tf_op jit(solution)/shard_map/all_to_all | solution.py:22
  8.3 58.2 %copy-start.1 = (f32[256]{0:T(256)S(1)}, f32[256]{0:T(256)}, u32[]{:S(2)}) copy-start(f32[256]{0:T(256)} %param.5) | copy-start | bytes 3076
  9.0 9.4 %collective-permute-start = (f16[96,384]{1,0:T(8,128)(2,1)S(1)}, f16[96,384]{1,0:T(8,128)(2,1)S(1)}, u32[]{:S(2)}, u32[]{:S(2)}) collective-permute-start(f16[96,384]{1,0:T(8,128)(2,1)S(1)} %bitcast.101), channel_id=1, source_target_pairs={{0,16},{16,0},{32,48},{48,32},{64,80},{80,64},{96,112},{112,96},{1... | collective-permute-start | bytes 221192 | tf_op jit(solution)/shard_map/ppermute | solution.py:29
  58.3 17.8 %collective-permute-start.1 = (bf16[4,128,3072]{2,1,0:T(8,128)(2,1)}, bf16[4,128,3072]{2,1,0:T(8,128)(2,1)}, u32[]{:S(2)}, u32[]{:S(2)}) collective-permute-start(bf16[4,128,3072]{2,1,0:T(8,128)(2,1)} %all-to-all-done), channel_id=1, source_target_pairs={{0,16},{16,0},{32,48},{48,32},{64,80},{80,64},{96,112},{112,96},{1... | collective-permute-start | bytes 9437192 | tf_op jit(solution)/shard_map/ppermute | solution.py:34
  75.2 0.9 copy-start.2
  79.8 1.1 copy-start.3
  119.8 6.3 %collective-permute-start.2 = (bf16[4,128,128]{2,1,0:T(8,128)(2,1)S(1)}, bf16[4,128,128]{2,1,0:T(8,128)(2,1)S(1)}, u32[]{:S(2)}, u32[]{:S(2)}) collective-permute-start(bf16[4,128,128]{2,1,0:T(8,128)(2,1)S(1)} %multiply_convert_fusion.2), channel_id=1, source_target_pairs={{0,16},{16,0},{32,48},{48,32},{64,80},{80,64},{96,112},{112,96},{1... | collective-permute-start | bytes 393224 | tf_op jit(solution)/shard_map/ppermute | solution.py:66

commit v2 on v1

v2 whole, which is shorter than its diff:
```python
import jax
import jax.numpy as jnp
from jax import lax
from jax.experimental import pallas as pl
from jax.experimental.pallas import tpu as pltpu
from jax.sharding import PartitionSpec as P

DH = 128
SEQ = 32
BLOCK = 128
SEQS = 4
WSCALE = 2.0**19
F32 = jnp.float32
B16 = jnp.bfloat16
SAME_CORE = [[2 * z + c for z in range(16)] for c in range(2)]
SIBLING = [(i, i ^ 1) for i in range(SEQ)]
QUAD = [[8 * a + 2 * b + c for b in range(4)] for a in range(4) for c in range(2)]
ACROSS = [[8 * a + 2 * b + c for a in range(4)] for b in range(4) for c in range(2)]
OWNERS = [[(2 * z + c) * 4 + y for y in range(4) for c in range(2)] for z in range(16)]
VMEM = pl.BlockSpec(memory_space=pltpu.VMEM)
SMEM = pl.BlockSpec(memory_space=pltpu.SMEM)
PARAMS = pltpu.CompilerParams(vmem_limit_bytes=24 * 1024 * 1024)


def silu_b(v):
    return (v * jax.nn.sigmoid(v)).astype(B16)


def rows(s):
    return slice(s * BLOCK, (s + 1) * BLOCK)


def outer(k, v):
    return lax.dot_general(k, v, (((0,), (0,)), ((), ())), preferred_element_type=F32)


def first_kernel(t_ref, w_ref, q_ref, k_ref, v_ref, s_ref):
    t = t_ref[...]
    kv = jnp.dot(t, w_ref[:, DH:], preferred_element_type=F32)
    k_ref[...] = silu_b(kv[:, :DH])
    v_ref[...] = kv[:, DH:].astype(B16)
    q_ref[...] = silu_b(jnp.dot(t, w_ref[:, :DH], preferred_element_type=F32))
    for s in range(SEQS):
        s_ref[s] = outer(k_ref[rows(s)], v_ref[rows(s)])


def second_kernel(t_ref, w_ref, sa_ref, k_ref, v_ref, s_ref, chip_ref):
    kv = jnp.dot(t_ref[...], w_ref[:, DH:], preferred_element_type=F32)
    k_ref[...] = silu_b(kv[:, :DH])
    v_ref[...] = kv[:, DH:].astype(B16)
    for s in range(SEQS):
        state = outer(k_ref[rows(s)], v_ref[rows(s)])
        s_ref[s] = state
        chip_ref[s] = (sa_ref[s] + state).astype(B16)


def local(q, k, v):
    scores = lax.dot_general(q, k, (((1,), (1,)), ((), ())), preferred_element_type=F32)
    causal = lax.broadcasted_iota(jnp.int32, scores.shape, 0) >= lax.broadcasted_iota(jnp.int32, scores.shape, 1)
    return jnp.dot(jnp.where(causal, scores, 0.0).astype(B16), v, preferred_element_type=F32)


def local_kernel(t_ref, w_ref, qa_ref, ka_ref, va_ref, kb_ref, vb_ref, qb_ref, la_ref, lb_ref):
    qb_ref[...] = silu_b(jnp.dot(t_ref[...], w_ref[:, :DH], preferred_element_type=F32))
    for s in range(SEQS):
        r = rows(s)
        la_ref[r] = local(qa_ref[r], ka_ref[r], va_ref[r])
        lb_ref[r] = local(qb_ref[r], kb_ref[r], vb_ref[r])


def final_kernel(core_ref, qa_ref, qb_ref, la_ref, lb_ref, before_ref, sa_ref, sb_ref, gain_ref, o_ref):
    core = core_ref[0]
    gain = jnp.where(core == 0, gain_ref[0:1], gain_ref[1:2])

    def normed(q, l, p):
        attn = l + jnp.dot(q, p.astype(B16), preferred_element_type=F32)
        scale = lax.rsqrt(jnp.mean(attn * attn, axis=-1, keepdims=True) + 1e-06)
        return (attn * scale * gain).astype(B16)

    for s in range(SEQS):
        r = rows(s)
        before = before_ref[s].astype(F32)
        pa = jnp.where(core == 0, before, before + sb_ref[s])
        pb = jnp.where(core == 0, before + sa_ref[s], before)
        o_ref[s, core] = normed(qa_ref[r], la_ref[r], pa)
        o_ref[s, 1 - core] = normed(qb_ref[r], lb_ref[r], pb)


def call(kernel, name, outs, *args):
    return pl.pallas_call(
        kernel,
        name=name,
        out_shape=[jax.ShapeDtypeStruct(s, d) for s, d in outs],
        in_specs=[SMEM if a.dtype == jnp.int32 else VMEM for a in args],
        out_specs=[VMEM for _ in outs],
        compiler_params=PARAMS,
    )(*args)


def body(tokens, proj_weights, norm_gain):
    place = lax.axis_index("seq")
    core = place & 1
    quad = place >> 3
    mine_t = lax.all_to_all(jnp.broadcast_to(tokens, (SEQS,) + tokens.shape[1:]), "dp", 0, 0, tiled=True)
    wh = (proj_weights.astype(F32) * WSCALE).astype(jnp.float16)
    wh = jnp.transpose(wh, (1, 0, 2)).reshape(-1, 3, 2, DH)
    head0, head1 = wh[:, :, 0].reshape(-1, 3 * DH), wh[:, :, 1].reshape(-1, 3 * DH)
    first = core == 0
    keep = jnp.where(first, head0, head1)
    give = jnp.where(first, head1, head0)
    got = lax.ppermute(give, "seq", SIBLING)
    pair = jnp.concatenate([jnp.where(first, keep, got), jnp.where(first, got, keep)], axis=0)
    full = lax.all_gather(pair, "seq", axis=0, tiled=True, axis_index_groups=SAME_CORE)
    mine_t, full = lax.optimization_barrier((mine_t, full))
    other_t = lax.ppermute(mine_t, "seq", SIBLING)
    weights = (full.astype(F32) * (1.0 / WSCALE)).astype(B16)
    n = SEQS * BLOCK
    ta, tb = mine_t.reshape(n, -1), other_t.reshape(n, -1)
    block, state = ((n, DH), B16), ((SEQS, DH, DH), F32)
    qa, ka, va, sa = call(first_kernel, "first", [block, block, block, state], ta, weights)
    kb, vb, sb, chip = call(second_kernel, "second", [block, block, state, ((SEQS, DH, DH), B16)], tb, weights, sa)

    by_chip = lax.all_to_all(chip, "seq", 0, 0, tiled=True, axis_index_groups=QUAD).astype(F32)
    total = jnp.sum(by_chip, axis=0).astype(B16)
    totals = lax.all_gather(total, "seq", axis=0, axis_index_groups=ACROSS).astype(F32)
    before = jnp.sum(jnp.where((jnp.arange(4) < quad)[:, None, None], totals, 0.0), axis=0)
    parts = [before]
    for j in range(3):
        parts.append(parts[-1] + by_chip[j])
    back = lax.all_to_all(jnp.stack(parts).astype(B16), "seq", 0, 0, tiled=True, axis_index_groups=QUAD)

    qb, la, lb = call(local_kernel, "local", [block, ((n, DH), F32), ((n, DH), F32)], tb, weights, qa, ka, va, kb, vb)
    (out,) = call(
        final_kernel, "final", [((SEQS, 2, BLOCK, DH), B16)],
        core.reshape(1), qa, qb, la, lb, back, sa, sb, norm_gain.reshape(2, DH),
    )
    out = lax.all_to_all(out.reshape(8, BLOCK, DH), ("seq", "dp"), 0, 0, tiled=True, axis_index_groups=OWNERS)
    return jnp.transpose(out, (1, 0, 2)).reshape(1, BLOCK, 8 * DH)


def solution(mesh):
    in_specs = (P("dp", "seq", None), P(None, "seq", ("heads", "dp")), P(("heads", "dp")))
    out_specs = P("dp", "seq", "heads")
    return jax.shard_map(body, mesh=mesh, in_specs=in_specs, out_specs=out_specs, check_vma=False)
```

time: 139 us -> 135 us (0.971)
  blocking collectives: 88.4 us -> 71.7 us
  matrix products: 9.3 us -> 0 us
  Pallas kernels: 0 us -> 8.4 us
  local copies, waits for them, and re-layouts: 8.46 us -> 15.3 us
  waiting for transfers between devices: 1.85 us -> 5.73 us
  starting transfers between devices: 27.2 us -> 30.1 us
    all_gather x3 -> x2, blocking collectives: 77.2 us -> 56.7 us  [the longest x1 42.1 us: body(): lax.all_gather(pair, 'seq', axis=0, tiled=True, axis_index_groups=SAME_CORE)]
    unnamed x9 -> x29, local copies, waits for them, and re-layouts: 1.01 us -> 10.8 us
    dot_general x8 -> x0, matrix products: 9.3 us -> none  [the longest x2 7.38 us: project(): out = jnp.dot(t.reshape(4 * 128, -1), weights, preferred_element_type=F32)]
    pallas_call x0 -> x4, Pallas kernels: none -> 8.4 us  [call(): pl.pallas_call(kernel, name=name, out_shape=[jax.ShapeDtypeStruct(s, d) f...]
    all_to_all x1 -> x3, starting transfers between devices: 5.14 us -> 12.7 us  [the longest x1 5.14 us: body(): lax.all_to_all(jnp.broadcast_to(tokens, (SEQS,) + tokens.shape[1:]), 'dp'...]
    ppermute x1 -> x0, starting transfers between devices: 5.36 us -> none  [body(): sib = lax.ppermute(ob, 'seq', SIBLING)]
    all_to_all x1 -> x3, waiting for transfers between devices: 0.01 us -> 4.83 us  [the longest x1 4.83 us: body(): lax.all_to_all(chip, 'seq', 0, 0, tiled=True, axis_index_groups=QUAD)]
    all_to_all x1, blocking collectives: 11.3 us -> 14.9 us  [body(): lax.all_to_all(out.reshape(8, BLOCK, DH), ('seq', 'dp'), 0, 0, tiled=True...]
  transfers between devices with their start and end apart: 4 -> 5, of which waited for: 2 -> 2; matrix products, arithmetic and copies ran while one was open for 7% -> 2% of each run, Pallas kernels for 0% -> 5%
where the time goes in v2:
time: 135 us
  blocking collectives  71.7 us (53%)
  starting transfers between devices  30.1 us (22%)
  local copies, waits for them, and re-layouts  15.3 us (11%)
  Pallas kernels  8.4 us (6%)
  waiting for transfers between devices  5.73 us (4%)
  other arithmetic  3.34 us (2%)
    all_gather x1, blocking collectives, body(): lax.all_gather(pair, 'seq', axis=0, tiled=True, axis_index_groups=SAME_CORE)  42.1 us
    all_to_all x1, blocking collectives, body(): lax.all_to_all(out.reshape(8, BLOCK, DH), ('seq', 'dp'), 0, 0, tiled=True...  14.9 us
    all_gather x1, blocking collectives, body(): lax.all_gather(total, 'seq', axis=0, axis_index_groups=ACROSS).astype(F32)  14.6 us
    unnamed x29, local copies, waits for them, and re-layouts  10.8 us
    ppermute x1, starting transfers between devices, body(): other_t = lax.ppermute(mine_t, 'seq', SIBLING)  8.93 us
    ppermute x1, starting transfers between devices, body(): got = lax.ppermute(give, 'seq', SIBLING)  8.44 us
    pallas_call x4, Pallas kernels, call(): pl.pallas_call(kernel, name=name, out_shape=[jax.ShapeDtypeStruct(s, d) f...  8.4 us
    all_to_all x1, starting transfers between devices, body(): lax.all_to_all(jnp.broadcast_to(tokens, (SEQS,) + tokens.shape[1:]), 'dp'...  5.14 us
  transfers between devices with their start and end apart: 5, of which 2 were waited for; matrix products, arithmetic and copies ran while one was open for 2% of the time, Pallas kernels for 5%

profile of v2, /device:TPU:1, one launch (start us, length us, event | category | flops | bytes accessed | tf_op | source)
XLA Modules:
  0.0 134.7 jit_solution(17323966518970948376)
XLA Ops:
  0.0 3.2 %broadcast_in_dim.21 = bf16[4,128,3072]{2,1,0:T(8,128)(2,1)} broadcast(bf16[128,3072]{1,0:T(8,128)(2,1)} %bitcast.41), dimensions={1,2} | broadcast | bytes 3932160 | tf_op jit(solution)/shard_map/broadcast_in_dim | solution.py:104
  3.2 0.0 copy-start.13
  3.2 5.1 %all-to-all-start = ((bf16[4,128,3072]{2,1,0:T(8,128)(2,1)}), bf16[4,128,3072]{2,1,0:T(8,128)(2,1)}, u32[]{:S(2)}, u32[]{:S(2)}) async-start(bf16[4,128,3072]{2,1,0:T(8,128)(2,1)} %broadcast_in_dim.21), calls=%async_computation | async-start | bytes 6291456 | tf_op jit(solution)/shard_map/all_to_all | solution.py:104
  8.4 0.0 copy-done.13
  8.4 0.1 reshape.33
  8.5 0.3 fusion.5
  8.7 0.2 broadcast_select_fusion.1
  9.0 8.4 %collective-permute-start = (f16[96,384]{1,0:T(8,128)(2,1)S(1)}, f16[96,384]{1,0:T(8,128)(2,1)S(1)}, u32[]{:S(2)}, u32[]{:S(2)}) collective-permute-start(f16[96,384]{1,0:T(8,128)(2,1)S(1)} %bitcast.45), channel_id=1, source_target_pairs={{0,16},{16,0},{32,48},{48,32},{64,80},{80,64},{96,112},{112,96},{1... | collective-permute-start | bytes 221192 | tf_op jit(solution)/shard_map/ppermute | solution.py:111
  17.4 0.9 collective-permute-done
  18.4 42.1 %all-gather.2 = f16[3072,384]{1,0:T(8,128)(2,1)} all-gather(f16[192,384]{1,0:T(8,128)(2,1)S(1)} %pad_maximum_fusion), channel_id=1, replica_groups={{0,32,64,96,128,160,192,224,256,288,320,352,384,416,448,480},{16,48,80,..., dimensions={0}, use_global_device_ids=true | all-gather | bytes 2506752 | tf_op jit(solution)/shard_map/all_gather | solution.py:113
  60.5 0.0 all-to-all-done
  60.5 8.9 %collective-permute-start.1 = (bf16[4,128,3072]{2,1,0:T(8,128)(2,1)}, bf16[4,128,3072]{2,1,0:T(8,128)(2,1)S(1)}, u32[]{:S(2)}, u32[]{:S(2)}) collective-permute-start(bf16[4,128,3072]{2,1,0:T(8,128)(2,1)} %all-to-all-done), channel_id=1, source_target_pairs={{0,16},{16,0},{32,48},{48,32},{64,80},{80,64},{96,112},{112,96},{1... | collective-permute-start | bytes 9437192 | tf_op jit(solution)/shard_map/ppermute | solution.py:115
  69.5 2.2 %multiply_convert_fusion.w_ref = bf16[3072,384]{1,0:T(8,128)(2,1)S(1)} fusion(f16[3072,384]{1,0:T(8,128)(2,1)} %all-gather.2), kind=kLoop, calls=%fused_computation | loop fusion | flops 3538944 | bytes 4718592 | tf_op jit(solution)/shard_map/convert_element_type | solution.py:116
  71.7 3.9 %first.1 = (bf16[512,128]{1,0:T(8,128)(2,1)S(1)}, bf16[512,128]{1,0:T(8,128)(2,1)S(1)}, bf16[512,128]{1,0:T(8,128)(2,1)S(1)}, f32[4,128,128]{2,1,0:T(8,128)S(1)}) custom-call(bf16[512,3072]{1,0:T(8,128)(2,1)} %bitcast.3.t_ref, bf16[3072,384]{1,0:T(8,128)(2,1)S(1)} %multiply_convert_fusion.w_ref), custom_call_target="tpu_custom_call" | custom-call | tf_op jit(solution)/shard_map/first/pallas_call | solution.py:90
  75.6 0.0 copy-start.4
  75.6 0.0 collective-permute-done.1
  75.6 1.9 %second.1 = (bf16[512,128]{1,0:T(8,128)(2,1)S(1)}, bf16[512,128]{1,0:T(8,128)(2,1)S(1)}, f32[4,128,128]{2,1,0:T(8,128)S(1)}, bf16[4,128,128]{2,1,0:T(8,128)(2,1)}) custom-call(bf16[512,3072]{1,0:T(8,128)(2,1)S(1)} %bitcast.36, bf16[3072,384]{1,0:T(8,128)(2,1)S(1)} %multiply_convert_fusion.w_ref, f32[4,128,128]{2,1,0:T(8,128)S(1)} %get-tuple-element.23.sa_ref), custom_call_target="tpu_custom_call" | custom-call | tf_op jit(solution)/shard_map/second/pallas_call | solution.py:90
  77.5 0.0 copy-start
  77.5 1.6 %copy-done = bf16[4,128,3072]{2,1,0:T(8,128)(2,1)} copy-done((bf16[4,128,3072]{2,1,0:T(8,128)(2,1)}, bf16[4,128,3072]{2,1,0:T(8,128)(2,1)S(1)}, u32[]{:S(2)}) %copy-start) | copy-done | bytes 3145752
  79.1 0.0 copy-start.6
  79.1 0.7 copy-done.6
  79.8 0.7 copy-done.8
  80.4 3.3 %all-to-all-start.1 = ((bf16[4,128,128]{2,1,0:T(8,128)(2,1)}), bf16[4,128,128]{2,1,0:T(8,128)(2,1)S(1)}, u32[]{:S(2)}, u32[]{:S(2)}) async-start(bf16[4,128,128]{2,1,0:T(8,128)(2,1)} %get-tuple-element.29), calls=%async_computation.1 | async-start | bytes 262144 | tf_op jit(solution)/shard_map/all_to_all | solution.py:123
  83.8 4.8 %all-to-all-done.1 = bf16[4,128,128]{2,1,0:T(8,128)(2,1)S(1)} async-done(((bf16[4,128,128]{2,1,0:T(8,128)(2,1)}), bf16[4,128,128]{2,1,0:T(8,128)(2,1)S(1)}, u32[]{:S(2)}, u32[]{:S(2)}) %all-to-all-start.1) | async-done | bytes 131104 | tf_op jit(solution)/shard_map/all_to_all | solution.py:123
  88.6 0.0 copy-done.4
  88.7 14.6 %all-gather = bf16[512,128]{1,0:T(8,128)(2,1)S(1)} all-gather(bf16[128,128]{1,0:T(8,128)(2,1)S(1)} %get-tuple-element.40), channel_id=2, replica_groups={{0,128,256,384},{16,144,272,400},{32,160,288,416},{48,176,304,432},{64,..., dimensions={0}, use_global_device_ids=true | all-gather | bytes 163840 | tf_op jit(solution)/shard_map/all_gather | solution.py:125
  103.3 0.1 fusion
  103.4 0.7 pad_maximum_fusion.1
  104.1 4.2 %all-to-all-start.2 = ((bf16[4,128,128]{2,1,0:T(8,128)(2,1)}), bf16[4,128,128]{2,1,0:T(8,128)(2,1)S(1)}, u32[]{:S(2)}, u32[]{:S(2)}) async-start(bf16[4,128,128]{2,1,0:T(8,128)(2,1)} %pad_maximum_fusion.1), calls=%async_computation.2 | async-start | bytes 262144 | tf_op jit(solution)/shard_map/all_to_all | solution.py:130
  108.3 0.0 copy-start.12
  108.3 0.0 copy-start.1
  108.3 1.9 %copy-done.1 = bf16[4,128,3072]{2,1,0:T(8,128)(2,1)S(1)} copy-done((bf16[4,128,3072]{2,1,0:T(8,128)(2,1)S(1)}, bf16[4,128,3072]{2,1,0:T(8,128)(2,1)}, u32[]{:S(2)}) %copy-start.1) | copy-done | bytes 3145752
  110.2 0.0 copy-start.5
  110.2 0.9 copy-done.5
  111.1 0.9 copy-done.7
  112.1 0.9 copy-done.9
  113.0 2.2 %local.1 = (bf16[512,128]{1,0:T(8,128)(2,1)S(1)}, f32[512,128]{1,0:T(8,128)S(1)}, f32[512,128]{1,0:T(8,128)S(1)}) custom-call(bf16[512,3072]{1,0:T(8,128)(2,1)S(1)} %bitcast.37, bf16[3072,384]{1,0:T(8,128)(2,1)S(1)} %multiply_convert_fusion.w_ref, bf16[512,128]{1,0:T(8,128)(2,1)S(1)} %get-tuple-element.20.qa_ref, ...), custom_call_target="tpu_custom_call" | custom-call | tf_op jit(solution)/shard_map/local/pallas_call | solution.py:90
  115.2 0.0 copy-start.2
  115.2 0.7 copy-done.2
  115.9 0.6 copy-done.10
  116.5 0.0 all-to-all-done.2.before_ref
  116.5 0.0 copy-done.12
  116.5 0.9 copy-done.3
  117.5 0.9 copy-done.11
  118.4 0.4 final.1
  118.8 14.9 %all_to_all.20 = bf16[8,128,128]{2,1,0:T(8,128)(2,1)S(1)} all-to-all(bf16[8,128,128]{2,1,0:T(8,128)(2,1)S(1)} %bitcast.38), channel_id=1, replica_groups={{0,16,1,17,2,18,3,19},{32,48,33,49,34,50,35,51},{64,80,65,81,66,82,67,8..., dimensions={0} | all-to-all | bytes 524288 | tf_op jit(solution)/shard_map/all_to_all | solution.py:137
  133.7 0.2 copy.12
  133.9 0.8 reshape.38
  (14 shorter events, 0.2 us)
Async XLA Ops:
  3.2 5.1 %copy-start.13 = (bf16[3,96,256]{2,1,0:T(8,128)(2,1)S(1)}, bf16[3,96,256]{2,1,0:T(8,128)(2,1)}, u32[]{:S(2)}) copy-start(bf16[3,96,256]{2,1,0:T(8,128)(2,1)} %param.4) | copy-start | bytes 442372
  3.2 57.3 %all-to-all-start = ((bf16[4,128,3072]{2,1,0:T(8,128)(2,1)}), bf16[4,128,3072]{2,1,0:T(8,128)(2,1)}, u32[]{:S(2)}, u32[]{:S(2)}) async-start(bf16[4,128,3072]{2,1,0:T(8,128)(2,1)} %broadcast_in_dim.21), calls=%async_computation | async-start | bytes 6291456 | tf_op jit(solution)/shard_map/all_to_all | solution.py:104
  9.0 9.3 %collective-permute-start = (f16[96,384]{1,0:T(8,128)(2,1)S(1)}, f16[96,384]{1,0:T(8,128)(2,1)S(1)}, u32[]{:S(2)}, u32[]{:S(2)}) collective-permute-start(f16[96,384]{1,0:T(8,128)(2,1)S(1)} %bitcast.45), channel_id=1, source_target_pairs={{0,16},{16,0},{32,48},{48,32},{64,80},{80,64},{96,112},{112,96},{1... | collective-permute-start | bytes 221192 | tf_op jit(solution)/shard_map/ppermute | solution.py:111
  60.5 15.1 %collective-permute-start.1 = (bf16[4,128,3072]{2,1,0:T(8,128)(2,1)}, bf16[4,128,3072]{2,1,0:T(8,128)(2,1)S(1)}, u32[]{:S(2)}, u32[]{:S(2)}) collective-permute-start(bf16[4,128,3072]{2,1,0:T(8,128)(2,1)} %all-to-all-done), channel_id=1, source_target_pairs={{0,16},{16,0},{32,48},{48,32},{64,80},{80,64},{96,112},{112,96},{1... | collective-permute-start | bytes 9437192 | tf_op jit(solution)/shard_map/ppermute | solution.py:115
  75.6 13.1 %copy-start.4 = (bf16[512,128]{1,0:T(8,128)(2,1)}, bf16[512,128]{1,0:T(8,128)(2,1)S(1)}, u32[]{:S(2)}) copy-start(bf16[512,128]{1,0:T(8,128)(2,1)S(1)} %get-tuple-element.22.va_ref) | copy-start | bytes 393220
  77.5 1.6 %copy-start = (bf16[4,128,3072]{2,1,0:T(8,128)(2,1)}, bf16[4,128,3072]{2,1,0:T(8,128)(2,1)S(1)}, u32[]{:S(2)}) copy-start(bf16[4,128,3072]{2,1,0:T(8,128)(2,1)S(1)} %collective-permute-done.1) | copy-start | bytes 9437188
  79.1 0.7 copy-start.6
  79.8 0.7 copy-start.8
  80.4 8.2 %all-to-all-start.1 = ((bf16[4,128,128]{2,1,0:T(8,128)(2,1)}), bf16[4,128,128]{2,1,0:T(8,128)(2,1)S(1)}, u32[]{:S(2)}, u32[]{:S(2)}) async-start(bf16[4,128,128]{2,1,0:T(8,128)(2,1)} %get-tuple-element.29), calls=%async_computation.1 | async-start | bytes 262144 | tf_op jit(solution)/shard_map/all_to_all | solution.py:123
  104.1 12.4 %all-to-all-start.2 = ((bf16[4,128,128]{2,1,0:T(8,128)(2,1)}), bf16[4,128,128]{2,1,0:T(8,128)(2,1)S(1)}, u32[]{:S(2)}, u32[]{:S(2)}) async-start(bf16[4,128,128]{2,1,0:T(8,128)(2,1)} %pad_maximum_fusion.1), calls=%async_computation.2 | async-start | bytes 262144 | tf_op jit(solution)/shard_map/all_to_all | solution.py:130
  108.3 8.2 %copy-start.12 = (f32[256]{0:T(256)S(1)}, f32[256]{0:T(256)}, u32[]{:S(2)}) copy-start(f32[256]{0:T(256)} %param.5) | copy-start | bytes 3076
  108.3 1.9 %copy-start.1 = (bf16[4,128,3072]{2,1,0:T(8,128)(2,1)S(1)}, bf16[4,128,3072]{2,1,0:T(8,128)(2,1)}, u32[]{:S(2)}) copy-start(bf16[4,128,3072]{2,1,0:T(8,128)(2,1)} %copy-done) | copy-start | bytes 9437188
  110.2 0.9 copy-start.5
  111.1 0.9 copy-start.7
  112.1 0.9 copy-start.9
  115.2 0.7 copy-start.2
  115.9 0.6 copy-start.10
  116.5 1.0 copy-start.3
  117.5 0.9 copy-start.11

commit v3 on v2

--- a/solution.py
+++ b/solution.py
@@ -34,38 +34,38 @@
     return lax.dot_general(k, v, (((0,), (0,)), ((), ())), preferred_element_type=F32)
 
 
-def first_kernel(t_ref, w_ref, q_ref, k_ref, v_ref, s_ref):
-    t = t_ref[...]
-    kv = jnp.dot(t, w_ref[:, DH:], preferred_element_type=F32)
-    k_ref[...] = silu_b(kv[:, :DH])
-    v_ref[...] = kv[:, DH:].astype(B16)
-    q_ref[...] = silu_b(jnp.dot(t, w_ref[:, :DH], preferred_element_type=F32))
-    for s in range(SEQS):
-        s_ref[s] = outer(k_ref[rows(s)], v_ref[rows(s)])
-
-
-def second_kernel(t_ref, w_ref, sa_ref, k_ref, v_ref, s_ref, chip_ref):
-    kv = jnp.dot(t_ref[...], w_ref[:, DH:], preferred_element_type=F32)
-    k_ref[...] = silu_b(kv[:, :DH])
-    v_ref[...] = kv[:, DH:].astype(B16)
-    for s in range(SEQS):
-        state = outer(k_ref[rows(s)], v_ref[rows(s)])
-        s_ref[s] = state
-        chip_ref[s] = (sa_ref[s] + state).astype(B16)
-
-
 def local(q, k, v):
     scores = lax.dot_general(q, k, (((1,), (1,)), ((), ())), preferred_element_type=F32)
     causal = lax.broadcasted_iota(jnp.int32, scores.shape, 0) >= lax.broadcasted_iota(jnp.int32, scores.shape, 1)
     return jnp.dot(jnp.where(causal, scores, 0.0).astype(B16), v, preferred_element_type=F32)
 
 
-def local_kernel(t_ref, w_ref, qa_ref, ka_ref, va_ref, kb_ref, vb_ref, qb_ref, la_ref, lb_ref):
-    qb_ref[...] = silu_b(jnp.dot(t_ref[...], w_ref[:, :DH], preferred_element_type=F32))
+def block_work(t_ref, w_ref, q_ref, l_ref, s_ref):
+    out = jnp.dot(t_ref[...], w_ref[...], preferred_element_type=F32)
+    q, k, v = silu_b(out[:, :DH]), silu_b(out[:, DH : 2 * DH]), out[:, 2 * DH :].astype(B16)
+    q_ref[...] = q
     for s in range(SEQS):
         r = rows(s)
-        la_ref[r] = local(qa_ref[r], ka_ref[r], va_ref[r])
-        lb_ref[r] = local(qb_ref[r], kb_ref[r], vb_ref[r])
+        s_ref[s] = outer(k[r], v[r])
+        l_ref[r] = local(q[r], k[r], v[r])
+
+
+def first_kernel(t_ref, w_ref, q_ref, l_ref, s_ref):
+    block_work(t_ref, w_ref, q_ref, l_ref, s_ref)
+
+
+def second_kernel(t_ref, w_ref, sa_ref, q_ref, l_ref, s_ref, chip_ref):
+    block_work(t_ref, w_ref, q_ref, l_ref, s_ref)
+    for s in range(SEQS):
+        chip_ref[s] = (sa_ref[s] + s_ref[s]).astype(B16)
+
+
+def copies_kernel(t_ref, o_ref, sem):
+    copies = [pltpu.make_async_copy(t_ref, o_ref.at[s], sem.at[s]) for s in range(SEQS)]
+    for c in copies:
+        c.start()
+    for c in copies:
+        c.wait()
 
 
 def final_kernel(core_ref, qa_ref, qb_ref, la_ref, lb_ref, before_ref, sa_ref, sb_ref, gain_ref, o_ref):
@@ -101,14 +101,24 @@
     place = lax.axis_index("seq")
     core = place & 1
     quad = place >> 3
-    mine_t = lax.all_to_all(jnp.broadcast_to(tokens, (SEQS,) + tokens.shape[1:]), "dp", 0, 0, tiled=True)
+    first = core == 0
     wh = (proj_weights.astype(F32) * WSCALE).astype(jnp.float16)
     wh = jnp.transpose(wh, (1, 0, 2)).reshape(-1, 3, 2, DH)
     head0, head1 = wh[:, :, 0].reshape(-1, 3 * DH), wh[:, :, 1].reshape(-1, 3 * DH)
-    first = core == 0
     keep = jnp.where(first, head0, head1)
     give = jnp.where(first, head1, head0)
     got = lax.ppermute(give, "seq", SIBLING)
+    hbm = pl.BlockSpec(memory_space=pl.ANY)
+    copies = pl.pallas_call(
+        copies_kernel,
+        name="copies",
+        out_shape=jax.ShapeDtypeStruct((SEQS,) + tokens.shape[1:], B16),
+        in_specs=[hbm],
+        out_specs=hbm,
+        scratch_shapes=[pltpu.SemaphoreType.DMA((SEQS,))],
+    )(tokens[0])
+    copies, got = lax.optimization_barrier((copies, got))
+    mine_t = lax.all_to_all(copies, "dp", 0, 0, tiled=True)
     pair = jnp.concatenate([jnp.where(first, keep, got), jnp.where(first, got, keep)], axis=0)
     full = lax.all_gather(pair, "seq", axis=0, tiled=True, axis_index_groups=SAME_CORE)
     mine_t, full = lax.optimization_barrier((mine_t, full))
@@ -116,9 +126,10 @@
     weights = (full.astype(F32) * (1.0 / WSCALE)).astype(B16)
     n = SEQS * BLOCK
     ta, tb = mine_t.reshape(n, -1), other_t.reshape(n, -1)
-    block, state = ((n, DH), B16), ((SEQS, DH, DH), F32)
-    qa, ka, va, sa = call(first_kernel, "first", [block, block, block, state], ta, weights)
-    kb, vb, sb, chip = call(second_kernel, "second", [block, block, state, ((SEQS, DH, DH), B16)], tb, weights, sa)
+    outs = [((n, DH), B16), ((n, DH), F32), ((SEQS, DH, DH), F32)]
+    qa, la, sa = call(first_kernel, "first", outs, ta, weights)
+    qb, lb, sb, chip = call(second_kernel, "second", outs + [((SEQS, DH, DH), B16)], tb, weights, sa)
+    chip, qa, la, sa, qb, lb, sb = lax.optimization_barrier((chip, qa, la, sa, qb, lb, sb))
 
     by_chip = lax.all_to_all(chip, "seq", 0, 0, tiled=True, axis_index_groups=QUAD).astype(F32)
     total = jnp.sum(by_chip, axis=0).astype(B16)
@@ -128,8 +139,6 @@
     for j in range(3):
         parts.append(parts[-1] + by_chip[j])
     back = lax.all_to_all(jnp.stack(parts).astype(B16), "seq", 0, 0, tiled=True, axis_index_groups=QUAD)
-
-    qb, la, lb = call(local_kernel, "local", [block, ((n, DH), F32), ((n, DH), F32)], tb, weights, qa, ka, va, kb, vb)
     (out,) = call(
         final_kernel, "final", [((SEQS, 2, BLOCK, DH), B16)],
         core.reshape(1), qa, qb, la, lb, back, sa, sb, norm_gain.reshape(2, DH),

time: 135 us -> 220 us (1.63)
  Pallas kernels: 8.4 us -> 102 us
  local copies, waits for them, and re-layouts: 15.3 us -> 2.04 us
  blocking collectives: 71.7 us -> 81.9 us
  starting transfers between devices: 30.1 us -> 24.8 us
    pallas_call x0 -> x1, Pallas kernels: none -> 96.4 us  [body(): pl.pallas_call(copies_kernel, name='copies', out_shape=jax.ShapeDtypeStru...]
    unnamed x29 -> x7, local copies, waits for them, and re-layouts: 10.8 us -> 0.73 us
    all_to_all x0 -> x1, blocking collectives: none -> 8.14 us  [body(): lax.all_to_all(jnp.stack(parts).astype(B16), 'seq', 0, 0, tiled=True, axi...]
    all_to_all x2 -> x1, starting transfers between devices: 9.38 us -> 3.71 us  [body(): mine_t = lax.all_to_all(copies, 'dp', 0, 0, tiled=True)]
    broadcast_in_dim x1 -> x0, local copies, waits for them, and re-layouts: 3.21 us -> none  [body(): jnp.broadcast_to(tokens, (SEQS,) + tokens.shape[1:])]
    pallas_call x4 -> x3, Pallas kernels: 8.4 us -> 5.33 us  [call(): pl.pallas_call(kernel, name=name, out_shape=[jax.ShapeDtypeStruct(s, d) f...]
  transfers between devices with their start and end apart: 5 -> 4, of which waited for: 2 -> 2; matrix products, arithmetic and copies ran while one was open for 2% -> 1% of each run, Pallas kernels for 5% -> 45%
where the time goes in v3:
time: 220 us; the launch traced here: 219 us
  Pallas kernels  102 us (46%)
  blocking collectives  81.9 us (37%)
  starting transfers between devices  24.8 us (11%)
  waiting for transfers between devices  5.02 us (2%)
  other arithmetic  3.61 us (2%)
    pallas_call x1, Pallas kernels, body(): pl.pallas_call(copies_kernel, name='copies', out_shape=jax.ShapeDtypeStru...  96.4 us
    all_gather x1, blocking collectives, body(): lax.all_gather(pair, 'seq', axis=0, tiled=True, axis_index_groups=SAME_CORE)  42.6 us
    all_to_all x1, blocking collectives, body(): lax.all_to_all(out.reshape(8, BLOCK, DH), ('seq', 'dp'), 0, 0, tiled=True...  16.1 us
    all_gather x1, blocking collectives, body(): lax.all_gather(total, 'seq', axis=0, axis_index_groups=ACROSS).astype(F32)  15 us
    ppermute x1, starting transfers between devices, body(): other_t = lax.ppermute(mine_t, 'seq', SIBLING)  8.96 us
    ppermute x1, starting transfers between devices, body(): got = lax.ppermute(give, 'seq', SIBLING)  8.79 us
    all_to_all x1, blocking collectives, body(): lax.all_to_all(jnp.stack(parts).astype(B16), 'seq', 0, 0, tiled=True, axi...  8.14 us
    pallas_call x3, Pallas kernels, call(): pl.pallas_call(kernel, name=name, out_shape=[jax.ShapeDtypeStruct(s, d) f...  5.33 us
  transfers between devices with their start and end apart: 4, of which 2 were waited for; matrix products, arithmetic and copies ran while one was open for 1% of the time, Pallas kernels for 45%

profile of v3, /device:TPU:1, one launch (start us, length us, event | category | flops | bytes accessed | tf_op | source)
XLA Modules:
  0.0 219.3 jit_solution(4459089897204256747)
XLA Ops:
  0.0 0.9 fusion.1
  0.9 0.1 reshape.33
  1.0 0.3 fusion.5
  1.3 0.2 broadcast_select_fusion
  1.5 8.8 %collective-permute-start = (f16[96,384]{1,0:T(8,128)(2,1)S(1)}, f16[96,384]{1,0:T(8,128)(2,1)S(1)}, u32[]{:S(2)}, u32[]{:S(2)}) collective-permute-start(f16[96,384]{1,0:T(8,128)(2,1)S(1)} %bitcast.45), channel_id=1, source_target_pairs={{0,16},{16,0},{32,48},{48,32},{64,80},{80,64},{96,112},{112,96},{1... | collective-permute-start | bytes 221192 | tf_op jit(solution)/shard_map/ppermute | solution.py:110
  10.3 96.4 %copies.1 = bf16[4,128,3072]{2,1,0:T(8,128)(2,1)} custom-call(bf16[128,3072]{1,0:T(8,128)(2,1)} %bitcast.41), custom_call_target="tpu_custom_call" | custom-call | tf_op jit(solution)/shard_map/copies/pallas_call | solution.py:112
  106.8 0.0 collective-permute-done
  106.8 3.7 %all-to-all-start = ((bf16[4,128,3072]{2,1,0:T(8,128)(2,1)}), bf16[4,128,3072]{2,1,0:T(8,128)(2,1)S(1)}, u32[]{:S(2)}, u32[]{:S(2)}) async-start(bf16[4,128,3072]{2,1,0:T(8,128)(2,1)} %copies.1), calls=%async_computation | async-start | bytes 6291456 | tf_op jit(solution)/shard_map/all_to_all | solution.py:121
  110.6 42.6 %all-gather.2 = f16[3072,384]{1,0:T(8,128)(2,1)} all-gather(f16[192,384]{1,0:T(8,128)(2,1)S(1)} %pad_maximum_fusion), channel_id=1, replica_groups={{0,32,64,96,128,160,192,224,256,288,320,352,384,416,448,480},{16,48,80,..., dimensions={0}, use_global_device_ids=true | all-gather | bytes 2506752 | tf_op jit(solution)/shard_map/all_gather | solution.py:123
  153.3 0.0 all-to-all-done
  153.3 9.0 %collective-permute-start.1 = (bf16[4,128,3072]{2,1,0:T(8,128)(2,1)S(1)}, bf16[4,128,3072]{2,1,0:T(8,128)(2,1)S(1)}, u32[]{:S(2)}, u32[]{:S(2)}) collective-permute-start(bf16[4,128,3072]{2,1,0:T(8,128)(2,1)S(1)} %all-to-all-done), channel_id=1, source_target_pairs={{0,16},{16,0},{32,48},{48,32},{64,80},{80,64},{96,112},{112,96},{1... | collective-permute-start | bytes 9437192 | tf_op jit(solution)/shard_map/ppermute | solution.py:125
  162.2 2.2 %multiply_convert_fusion.w_ref = bf16[3072,384]{1,0:T(8,128)(2,1)S(1)} fusion(f16[3072,384]{1,0:T(8,128)(2,1)} %all-gather.2), kind=kLoop, calls=%fused_computation | loop fusion | flops 3538944 | bytes 4718592 | tf_op jit(solution)/shard_map/convert_element_type | solution.py:126
  164.4 2.2 first.1
  166.6 0.0 copy-start
  166.6 0.7 copy-done
  167.3 0.2 collective-permute-done.1
  167.5 0.0 copy-start.1
  167.5 0.0 copy-start.2
  167.5 2.8 %second.1 = (bf16[512,128]{1,0:T(8,128)(2,1)S(1)}, f32[512,128]{1,0:T(8,128)S(1)}, f32[4,128,128]{2,1,0:T(8,128)S(1)}, bf16[4,128,128]{2,1,0:T(8,128)(2,1)}) custom-call(bf16[512,3072]{1,0:T(8,128)(2,1)S(1)} %bitcast.37, bf16[3072,384]{1,0:T(8,128)(2,1)S(1)} %multiply_convert_fusion.w_ref, f32[4,128,128]{2,1,0:T(8,128)S(1)} %get-tuple-element.39.sa_ref), custom_call_target="tpu_custom_call" | custom-call | tf_op jit(solution)/shard_map/second/pallas_call | solution.py:90
  170.3 3.3 %all-to-all-start.1 = ((bf16[4,128,128]{2,1,0:T(8,128)(2,1)}), bf16[4,128,128]{2,1,0:T(8,128)(2,1)S(1)}, u32[]{:S(2)}, u32[]{:S(2)}) async-start(bf16[4,128,128]{2,1,0:T(8,128)(2,1)} %get-tuple-element.38), calls=%async_computation.1 | async-start | bytes 262144 | tf_op jit(solution)/shard_map/all_to_all | solution.py:134
  173.6 4.8 %all-to-all-done.1 = bf16[4,128,128]{2,1,0:T(8,128)(2,1)S(1)} async-done(((bf16[4,128,128]{2,1,0:T(8,128)(2,1)}), bf16[4,128,128]{2,1,0:T(8,128)(2,1)S(1)}, u32[]{:S(2)}, u32[]{:S(2)}) %all-to-all-start.1) | async-done | bytes 131104 | tf_op jit(solution)/shard_map/all_to_all | solution.py:134
  178.5 15.0 %all-gather = bf16[512,128]{1,0:T(8,128)(2,1)S(1)} all-gather(bf16[128,128]{1,0:T(8,128)(2,1)S(1)} %get-tuple-element.50), channel_id=2, replica_groups={{0,128,256,384},{16,144,272,400},{32,160,288,416},{48,176,304,432},{64,..., dimensions={0}, use_global_device_ids=true | all-gather | bytes 163840 | tf_op jit(solution)/shard_map/all_gather | solution.py:136
  193.5 0.1 fusion
  193.7 8.1 %all_to_all.20.before_ref = bf16[4,128,128]{2,1,0:T(8,128)(2,1)S(1)} all-to-all(bf16[4,128,128]{2,1,0:T(8,128)(2,1)S(1)} %pad_maximum_fusion.1), channel_id=1, replica_groups={{0,32,64,96},{16,48,80,112},{128,160,192,224},{144,176,208,240},{256,28..., dimensions={0} | all-to-all | bytes 262144 | tf_op jit(solution)/shard_map/all_to_all | solution.py:141
  201.8 0.0 copy-done.1
  201.8 0.0 copy-done.2
  201.8 0.4 final.1
  202.2 16.1 %all_to_all.21 = bf16[8,128,128]{2,1,0:T(8,128)(2,1)S(1)} all-to-all(bf16[8,128,128]{2,1,0:T(8,128)(2,1)S(1)} %bitcast.38), channel_id=1, replica_groups={{0,16,1,17,2,18,3,19},{32,48,33,49,34,50,35,51},{64,80,65,81,66,82,67,8..., dimensions={0} | all-to-all | bytes 524288 | tf_op jit(solution)/shard_map/all_to_all | solution.py:146
  218.3 0.2 copy.12
  218.5 0.8 reshape.38
  (8 shorter events, 0.2 us)
Async XLA Ops:
  1.5 105.2 %collective-permute-start = (f16[96,384]{1,0:T(8,128)(2,1)S(1)}, f16[96,384]{1,0:T(8,128)(2,1)S(1)}, u32[]{:S(2)}, u32[]{:S(2)}) collective-permute-start(f16[96,384]{1,0:T(8,128)(2,1)S(1)} %bitcast.45), channel_id=1, source_target_pairs={{0,16},{16,0},{32,48},{48,32},{64,80},{80,64},{96,112},{112,96},{1... | collective-permute-start | bytes 221192 | tf_op jit(solution)/shard_map/ppermute | solution.py:110
  106.8 46.5 %all-to-all-start = ((bf16[4,128,3072]{2,1,0:T(8,128)(2,1)}), bf16[4,128,3072]{2,1,0:T(8,128)(2,1)S(1)}, u32[]{:S(2)}, u32[]{:S(2)}) async-start(bf16[4,128,3072]{2,1,0:T(8,128)(2,1)} %copies.1), calls=%async_computation | async-start | bytes 6291456 | tf_op jit(solution)/shard_map/all_to_all | solution.py:121
  153.3 14.2 %collective-permute-start.1 = (bf16[4,128,3072]{2,1,0:T(8,128)(2,1)S(1)}, bf16[4,128,3072]{2,1,0:T(8,128)(2,1)S(1)}, u32[]{:S(2)}, u32[]{:S(2)}) collective-permute-start(bf16[4,128,3072]{2,1,0:T(8,128)(2,1)S(1)} %all-to-all-done), channel_id=1, source_target_pairs={{0,16},{16,0},{32,48},{48,32},{64,80},{80,64},{96,112},{112,96},{1... | collective-permute-start | bytes 9437192 | tf_op jit(solution)/shard_map/ppermute | solution.py:125
  166.6 0.7 copy-start
  167.5 34.3 %copy-start.1 = (f32[512,128]{1,0:T(8,128)S(1)}, f32[512,128]{1,0:T(8,128)}, u32[]{:S(2)}) copy-start(f32[512,128]{1,0:T(8,128)} %copy-done) | copy-start | bytes 786436
  167.5 34.3 %copy-start.2 = (f32[256]{0:T(256)S(1)}, f32[256]{0:T(256)}, u32[]{:S(2)}) copy-start(f32[256]{0:T(256)} %param.5) | copy-start | bytes 3076
  170.3 8.2 %all-to-all-start.1 = ((bf16[4,128,128]{2,1,0:T(8,128)(2,1)}), bf16[4,128,128]{2,1,0:T(8,128)(2,1)S(1)}, u32[]{:S(2)}, u32[]{:S(2)}) async-start(bf16[4,128,128]{2,1,0:T(8,128)(2,1)} %get-tuple-element.38), calls=%async_computation.1 | async-start | bytes 262144 | tf_op jit(solution)/shard_map/all_to_all | solution.py:134

commit v4 on v3

--- a/solution.py
+++ b/solution.py
@@ -60,6 +60,21 @@
         chip_ref[s] = (sa_ref[s] + s_ref[s]).astype(B16)
 
 
+def total_kernel(r_ref, o_ref):
+    o_ref[...] = (r_ref[0].astype(F32) + r_ref[1].astype(F32) + r_ref[2].astype(F32) + r_ref[3].astype(F32)).astype(B16)
+
+
+def parts_kernel(quad_ref, r_ref, totals_ref, o_ref):
+    quad = quad_ref[0]
+    before = jnp.zeros((DH, DH), F32)
+    for a in range(3):
+        before = before + jnp.where(a < quad, totals_ref[a].astype(F32), 0.0)
+    o_ref[0] = before.astype(B16)
+    for j in range(3):
+        before = before + r_ref[j].astype(F32)
+        o_ref[j + 1] = before.astype(B16)
+
+
 def copies_kernel(t_ref, o_ref, sem):
     copies = [pltpu.make_async_copy(t_ref, o_ref.at[s], sem.at[s]) for s in range(SEQS)]
     for c in copies:
@@ -100,7 +115,7 @@
 def body(tokens, proj_weights, norm_gain):
     place = lax.axis_index("seq")
     core = place & 1
-    quad = place >> 3
+    quad = (place >> 3).reshape(1)
     first = core == 0
     wh = (proj_weights.astype(F32) * WSCALE).astype(jnp.float16)
     wh = jnp.transpose(wh, (1, 0, 2)).reshape(-1, 3, 2, DH)
@@ -108,13 +123,12 @@
     keep = jnp.where(first, head0, head1)
     give = jnp.where(first, head1, head0)
     got = lax.ppermute(give, "seq", SIBLING)
-    hbm = pl.BlockSpec(memory_space=pl.ANY)
     copies = pl.pallas_call(
         copies_kernel,
         name="copies",
         out_shape=jax.ShapeDtypeStruct((SEQS,) + tokens.shape[1:], B16),
-        in_specs=[hbm],
-        out_specs=hbm,
+        in_specs=[VMEM],
+        out_specs=pl.BlockSpec(memory_space=pl.ANY),
         scratch_shapes=[pltpu.SemaphoreType.DMA((SEQS,))],
     )(tokens[0])
     copies, got = lax.optimization_barrier((copies, got))
@@ -129,16 +143,14 @@
     outs = [((n, DH), B16), ((n, DH), F32), ((SEQS, DH, DH), F32)]
     qa, la, sa = call(first_kernel, "first", outs, ta, weights)
     qb, lb, sb, chip = call(second_kernel, "second", outs + [((SEQS, DH, DH), B16)], tb, weights, sa)
-    chip, qa, la, sa, qb, lb, sb = lax.optimization_barrier((chip, qa, la, sa, qb, lb, sb))
+    chip, qa, la, sa, qb, lb, sb, quad = lax.optimization_barrier((chip, qa, la, sa, qb, lb, sb, quad))
 
-    by_chip = lax.all_to_all(chip, "seq", 0, 0, tiled=True, axis_index_groups=QUAD).astype(F32)
-    total = jnp.sum(by_chip, axis=0).astype(B16)
-    totals = lax.all_gather(total, "seq", axis=0, axis_index_groups=ACROSS).astype(F32)
-    before = jnp.sum(jnp.where((jnp.arange(4) < quad)[:, None, None], totals, 0.0), axis=0)
-    parts = [before]
-    for j in range(3):
-        parts.append(parts[-1] + by_chip[j])
-    back = lax.all_to_all(jnp.stack(parts).astype(B16), "seq", 0, 0, tiled=True, axis_index_groups=QUAD)
+    square = (DH, DH)
+    by_chip = lax.all_to_all(chip, "seq", 0, 0, tiled=True, axis_index_groups=QUAD)
+    (total,) = call(total_kernel, "total", [(square, B16)], by_chip)
+    totals = lax.all_gather(total, "seq", axis=0, axis_index_groups=ACROSS)
+    (parts,) = call(parts_kernel, "parts", [((4,) + square, B16)], quad, by_chip, totals)
+    back = lax.all_to_all(parts, "seq", 0, 0, tiled=True, axis_index_groups=QUAD)
     (out,) = call(
         final_kernel, "final", [((SEQS, 2, BLOCK, DH), B16)],
         core.reshape(1), qa, qb, la, lb, back, sa, sb, norm_gain.reshape(2, DH),

time: 220 us -> 127 us (0.58)
  Pallas kernels: 102 us -> 9.49 us
  blocking collectives: 81.9 us -> 89.2 us
  waiting for transfers between devices: 5.02 us -> 1.02 us
  starting transfers between devices: 24.8 us -> 21.5 us
    pallas_call x1, Pallas kernels: 96.4 us -> 2.81 us  [body(): pl.pallas_call(copies_kernel, name='copies', out_shape=jax.ShapeDtypeStru...]
    all_to_all x1 -> x2, blocking collectives: 8.14 us -> 14.6 us  [the longest x1 7.31 us: body(): lax.all_to_all(parts, 'seq', 0, 0, tiled=True, axis_index_groups=QUAD)]
    all_to_all x1 -> x0, waiting for transfers between devices: 4.83 us -> none  [body(): lax.all_to_all(chip, 'seq', 0, 0, tiled=True, axis_index_groups=QUAD)]
    all_to_all x1 -> x0, starting transfers between devices: 3.32 us -> none  [body(): lax.all_to_all(chip, 'seq', 0, 0, tiled=True, axis_index_groups=QUAD)]
    pallas_call x3 -> x5, Pallas kernels: 5.33 us -> 6.69 us  [call(): pl.pallas_call(kernel, name=name, out_shape=[jax.ShapeDtypeStruct(s, d) f...]
  transfers between devices with their start and end apart: 4 -> 3, of which waited for: 2 -> 1; matrix products, arithmetic and copies ran while one was open for 1% -> 2% of each run, Pallas kernels for 45% -> 4%
where the time goes in v4:
time: 127 us; the launch traced here: 126 us
  blocking collectives  89.2 us (70%)
  starting transfers between devices  21.5 us (17%)
  Pallas kernels  9.49 us (7%)
  other arithmetic  3.44 us (3%)
  local copies, waits for them, and re-layouts  1.34 us (1%)
    all_gather x1, blocking collectives, body(): lax.all_gather(pair, 'seq', axis=0, tiled=True, axis_index_groups=SAME_CORE)  42.6 us
    all_to_all x1, blocking collectives, body(): lax.all_to_all(out.reshape(8, BLOCK, DH), ('seq', 'dp'), 0, 0, tiled=True...  16.2 us
    all_gather x1, blocking collectives, body(): totals = lax.all_gather(total, 'seq', axis=0, axis_index_groups=ACROSS)  15.8 us
    ppermute x1, starting transfers between devices, body(): other_t = lax.ppermute(mine_t, 'seq', SIBLING)  8.97 us
    ppermute x1, starting transfers between devices, body(): got = lax.ppermute(give, 'seq', SIBLING)  8.79 us
    all_to_all x1, blocking collectives, body(): lax.all_to_all(parts, 'seq', 0, 0, tiled=True, axis_index_groups=QUAD)  7.31 us
    all_to_all x1, blocking collectives, body(): lax.all_to_all(chip, 'seq', 0, 0, tiled=True, axis_index_groups=QUAD)  7.27 us
    pallas_call x5, Pallas kernels, call(): pl.pallas_call(kernel, name=name, out_shape=[jax.ShapeDtypeStruct(s, d) f...  6.69 us
  transfers between devices with their start and end apart: 3, of which 1 were waited for; matrix products, arithmetic and copies ran while one was open for 2% of the time, Pallas kernels for 4%

profile of v4, /device:TPU:1, one launch (start us, length us, event | category | flops | bytes accessed | tf_op | source)
XLA Modules:
  0.0 126.1 jit_solution(4731144336491666909)
XLA Ops:
  0.0 0.9 fusion
  0.9 0.1 reshape.29
  1.0 0.3 fusion.1
  1.3 0.2 broadcast_select_fusion
  1.5 8.8 %collective-permute-start = (f16[96,384]{1,0:T(8,128)(2,1)S(1)}, f16[96,384]{1,0:T(8,128)(2,1)S(1)}, u32[]{:S(2)}, u32[]{:S(2)}) collective-permute-start(f16[96,384]{1,0:T(8,128)(2,1)S(1)} %bitcast.33), channel_id=1, source_target_pairs={{0,16},{16,0},{32,48},{48,32},{64,80},{80,64},{96,112},{112,96},{1... | collective-permute-start | bytes 221192 | tf_op jit(solution)/shard_map/ppermute | solution.py:125
  10.3 2.8 %copies.1 = bf16[4,128,3072]{2,1,0:T(8,128)(2,1)} custom-call(bf16[128,3072]{1,0:T(8,128)(2,1)} %bitcast.30), custom_call_target="tpu_custom_call" | custom-call | tf_op jit(solution)/shard_map/copies/pallas_call | solution.py:126
  13.2 0.0 collective-permute-done
  13.2 3.7 %all-to-all-start = ((bf16[4,128,3072]{2,1,0:T(8,128)(2,1)}), bf16[4,128,3072]{2,1,0:T(8,128)(2,1)S(1)}, u32[]{:S(2)}, u32[]{:S(2)}) async-start(bf16[4,128,3072]{2,1,0:T(8,128)(2,1)} %copies.1), calls=%async_computation | async-start | bytes 6291456 | tf_op jit(solution)/shard_map/all_to_all | solution.py:135
  17.0 42.6 %all-gather.2 = f16[3072,384]{1,0:T(8,128)(2,1)} all-gather(f16[192,384]{1,0:T(8,128)(2,1)S(1)} %pad_maximum_fusion), channel_id=1, replica_groups={{0,32,64,96,128,160,192,224,256,288,320,352,384,416,448,480},{16,48,80,..., dimensions={0}, use_global_device_ids=true | all-gather | bytes 2506752 | tf_op jit(solution)/shard_map/all_gather | solution.py:137
  59.6 0.0 all-to-all-done
  59.6 9.0 %collective-permute-start.1 = (bf16[4,128,3072]{2,1,0:T(8,128)(2,1)S(1)}, bf16[4,128,3072]{2,1,0:T(8,128)(2,1)}, u32[]{:S(2)}, u32[]{:S(2)}) collective-permute-start(bf16[4,128,3072]{2,1,0:T(8,128)(2,1)S(1)} %all-to-all-done), channel_id=1, source_target_pairs={{0,16},{16,0},{32,48},{48,32},{64,80},{80,64},{96,112},{112,96},{1... | collective-permute-start | bytes 9437192 | tf_op jit(solution)/shard_map/ppermute | solution.py:139
  68.6 2.2 %multiply_convert_fusion.w_ref = bf16[3072,384]{1,0:T(8,128)(2,1)S(1)} fusion(f16[3072,384]{1,0:T(8,128)(2,1)} %all-gather.2), kind=kLoop, calls=%fused_computation | loop fusion | flops 3538944 | bytes 4718592 | tf_op jit(solution)/shard_map/convert_element_type | solution.py:140
  70.8 2.2 %first.1 = (bf16[512,128]{1,0:T(8,128)(2,1)S(1)}, f32[512,128]{1,0:T(8,128)S(1)}, f32[4,128,128]{2,1,0:T(8,128)S(1)}) custom-call(bf16[512,3072]{1,0:T(8,128)(2,1)S(1)} %bitcast.25, bf16[3072,384]{1,0:T(8,128)(2,1)S(1)} %multiply_convert_fusion.w_ref), custom_call_target="tpu_custom_call" | custom-call | tf_op jit(solution)/shard_map/first/pallas_call | solution.py:105
  73.0 1.0 collective-permute-done.1
  74.0 0.0 copy-start
  74.0 4.1 %second.1 = (bf16[512,128]{1,0:T(8,128)(2,1)S(1)}, f32[512,128]{1,0:T(8,128)S(1)}, f32[4,128,128]{2,1,0:T(8,128)S(1)}, bf16[4,128,128]{2,1,0:T(8,128)(2,1)S(1)}) custom-call(bf16[512,3072]{1,0:T(8,128)(2,1)} %bitcast.3.t_ref, bf16[3072,384]{1,0:T(8,128)(2,1)S(1)} %multiply_convert_fusion.w_ref, f32[4,128,128]{2,1,0:T(8,128)S(1)} %get-tuple-element.41.sa_ref), custom_call_target="tpu_custom_call" | custom-call | tf_op jit(solution)/shard_map/second/pallas_call | solution.py:105
  78.1 7.3 %all_to_all.20.r_ref = bf16[4,128,128]{2,1,0:T(8,128)(2,1)S(1)} all-to-all(bf16[4,128,128]{2,1,0:T(8,128)(2,1)S(1)} %get-tuple-element.40), channel_id=1, replica_groups={{0,32,64,96},{16,48,80,112},{128,160,192,224},{144,176,208,240},{256,28..., dimensions={0} | all-to-all | bytes 262144 | tf_op jit(solution)/shard_map/all_to_all | solution.py:149
  85.4 15.8 %all-gather = bf16[512,128]{1,0:T(8,128)(2,1)S(1)} all-gather(bf16[128,128]{1,0:T(8,128)(2,1)S(1)} %total.1), channel_id=2, replica_groups={{0,128,256,384},{16,144,272,400},{32,160,288,416},{48,176,304,432},{64,..., dimensions={0}, use_global_device_ids=true | all-gather | bytes 163840 | tf_op jit(solution)/shard_map/all_gather | solution.py:151
  101.2 7.3 %all_to_all.21.before_ref = bf16[4,128,128]{2,1,0:T(8,128)(2,1)S(1)} all-to-all(bf16[4,128,128]{2,1,0:T(8,128)(2,1)S(1)} %parts.1), channel_id=1, replica_groups={{0,32,64,96},{16,48,80,112},{128,160,192,224},{144,176,208,240},{256,28..., dimensions={0} | all-to-all | bytes 262144 | tf_op jit(solution)/shard_map/all_to_all | solution.py:153
  108.5 0.0 copy-done
  108.5 0.4 final.1
  108.9 16.2 %all_to_all.22 = bf16[8,128,128]{2,1,0:T(8,128)(2,1)S(1)} all-to-all(bf16[8,128,128]{2,1,0:T(8,128)(2,1)S(1)} %bitcast.26), channel_id=1, replica_groups={{0,16,1,17,2,18,3,19},{32,48,33,49,34,50,35,51},{64,80,65,81,66,82,67,8..., dimensions={0} | all-to-all | bytes 524288 | tf_op jit(solution)/shard_map/all_to_all | solution.py:158
  125.1 0.2 copy.9
  125.3 0.8 reshape.35
  (5 shorter events, 0.2 us)
Async XLA Ops:
  1.5 11.6 %collective-permute-start = (f16[96,384]{1,0:T(8,128)(2,1)S(1)}, f16[96,384]{1,0:T(8,128)(2,1)S(1)}, u32[]{:S(2)}, u32[]{:S(2)}) collective-permute-start(f16[96,384]{1,0:T(8,128)(2,1)S(1)} %bitcast.33), channel_id=1, source_target_pairs={{0,16},{16,0},{32,48},{48,32},{64,80},{80,64},{96,112},{112,96},{1... | collective-permute-start | bytes 221192 | tf_op jit(solution)/shard_map/ppermute | solution.py:125
  13.2 46.5 %all-to-all-start = ((bf16[4,128,3072]{2,1,0:T(8,128)(2,1)}), bf16[4,128,3072]{2,1,0:T(8,128)(2,1)S(1)}, u32[]{:S(2)}, u32[]{:S(2)}) async-start(bf16[4,128,3072]{2,1,0:T(8,128)(2,1)} %copies.1), calls=%async_computation | async-start | bytes 6291456 | tf_op jit(solution)/shard_map/all_to_all | solution.py:135
  59.6 14.4 %collective-permute-start.1 = (bf16[4,128,3072]{2,1,0:T(8,128)(2,1)S(1)}, bf16[4,128,3072]{2,1,0:T(8,128)(2,1)}, u32[]{:S(2)}, u32[]{:S(2)}) collective-permute-start(bf16[4,128,3072]{2,1,0:T(8,128)(2,1)S(1)} %all-to-all-done), channel_id=1, source_target_pairs={{0,16},{16,0},{32,48},{48,32},{64,80},{80,64},{96,112},{112,96},{1... | collective-permute-start | bytes 9437192 | tf_op jit(solution)/shard_map/ppermute | solution.py:139
  74.0 34.5 %copy-start = (f32[256]{0:T(256)S(1)}, f32[256]{0:T(256)}, u32[]{:S(2)}) copy-start(f32[256]{0:T(256)} %param.5) | copy-start | bytes 3076

commit v5 on v4

v5 whole, which is shorter than its diff:
```python
import jax
import jax.numpy as jnp
from jax import lax
from jax.experimental import pallas as pl
from jax.experimental.pallas import tpu as pltpu
from jax.sharding import PartitionSpec as P

DH = 128
SEQ = 32
BLOCK = 128
SEQS = 4
WSCALE = 2.0**19
F32 = jnp.float32
B16 = jnp.bfloat16
SIBLING = [(i, i ^ 1) for i in range(SEQ)]
QUAD = [[8 * a + 2 * b + c for b in range(4)] for a in range(4) for c in range(2)]


def holder(z, head):
    return 2 * z + (head ^ ((z >> 2) & 1))


SAME_HEAD = [[holder(z, h) for z in range(16)] for h in range(2)]
ACROSS = [[holder(4 * a + b, h) for a in range(4)] for b in range(4) for h in range(2)]
OWNERS = [[holder(z, h) * 4 + y for y in range(4) for h in range(2)] for z in range(16)]
VMEM = pl.BlockSpec(memory_space=pltpu.VMEM)
SMEM = pl.BlockSpec(memory_space=pltpu.SMEM)
PARAMS = pltpu.CompilerParams(vmem_limit_bytes=24 * 1024 * 1024)


def silu_b(v):
    return (v * jax.nn.sigmoid(v)).astype(B16)


def rows(s):
    return slice(s * BLOCK, (s + 1) * BLOCK)


def outer(k, v):
    return lax.dot_general(k, v, (((0,), (0,)), ((), ())), preferred_element_type=F32)


def local(q, k, v):
    scores = lax.dot_general(q, k, (((1,), (1,)), ((), ())), preferred_element_type=F32)
    causal = lax.broadcasted_iota(jnp.int32, scores.shape, 0) >= lax.broadcasted_iota(jnp.int32, scores.shape, 1)
    return jnp.dot(jnp.where(causal, scores, 0.0).astype(B16), v, preferred_element_type=F32)


def block_work(out, q_ref, l_ref, s_ref):
    q, k, v = silu_b(out[:, :DH]), silu_b(out[:, DH : 2 * DH]), out[:, 2 * DH :].astype(B16)
    q_ref[...] = q
    for s in range(SEQS):
        r = rows(s)
        s_ref[s] = outer(k[r], v[r])
        l_ref[r] = local(q[r], k[r], v[r])


def first_kernel(t_ref, w_ref, q_ref, l_ref, s_ref):
    block_work(jnp.dot(t_ref[...], w_ref[...], preferred_element_type=F32), q_ref, l_ref, s_ref)


def second_kernel(t_ref, w_ref, sa_ref, q_ref, l_ref, s_ref, chip_ref, piece, acc, sem):
    count, _, width = piece.shape
    span = [slice(i * width, (i + 1) * width) for i in range(count)]
    copies = [pltpu.make_async_copy(t_ref.at[:, span[i]], piece.at[i], sem.at[i]) for i in range(count)]
    for c in copies:
        c.start()
    for i in range(count):
        copies[i].wait()
        part = jnp.dot(piece[i], w_ref[span[i]], preferred_element_type=F32)
        if i == 0:
            acc[...] = part
        else:
            acc[...] += part
    block_work(acc[...], q_ref, l_ref, s_ref)
    for s in range(SEQS):
        chip_ref[s] = (sa_ref[s] + s_ref[s]).astype(B16)


def total_kernel(r_ref, o_ref):
    o_ref[...] = (r_ref[0].astype(F32) + r_ref[1].astype(F32) + r_ref[2].astype(F32) + r_ref[3].astype(F32)).astype(B16)


def parts_kernel(quad_ref, r_ref, totals_ref, o_ref):
    quad = quad_ref[0]
    before = jnp.zeros((DH, DH), F32)
    for a in range(3):
        before = before + jnp.where(a < quad, totals_ref[a].astype(F32), 0.0)
    o_ref[0] = before.astype(B16)
    for j in range(3):
        before = before + r_ref[j].astype(F32)
        o_ref[j + 1] = before.astype(B16)


def copies_kernel(t_ref, o_ref, buf, sem_in, sem):
    count = buf.shape[0]
    loads = [pltpu.make_async_copy(t_ref.at[pl.ds(i * 32, 32)], buf.at[i], sem_in.at[i]) for i in range(count)]
    stores = [
        pltpu.make_async_copy(buf.at[i], o_ref.at[s, pl.ds(i * 32, 32)], sem.at[i, s])
        for i in range(count) for s in range(SEQS)
    ]
    for c in loads:
        c.start()
    for i in range(count):
        loads[i].wait()
        for c in stores[i * SEQS : (i + 1) * SEQS]:
            c.start()
    for c in stores:
        c.wait()


def join_kernel(i_ref, o_ref, sem):
    count = i_ref.shape[0]
    copies = [pltpu.make_async_copy(i_ref.at[j], o_ref.at[:, pl.ds(j * DH, DH)], sem.at[j]) for j in range(count)]
    for c in copies:
        c.start()
    for c in copies:
        c.wait()


def final_kernel(spot_ref, qa_ref, qb_ref, la_ref, lb_ref, before_ref, sa_ref, sb_ref, gain_ref, o_ref):
    core, head = spot_ref[0], spot_ref[1]
    gain = jnp.where(head == 0, gain_ref[0:1], gain_ref[1:2])

    def normed(q, l, p):
        attn = l + jnp.dot(q, p.astype(B16), preferred_element_type=F32)
        scale = lax.rsqrt(jnp.mean(attn * attn, axis=-1, keepdims=True) + 1e-06)
        return (attn * scale * gain).astype(B16)

    for s in range(SEQS):
        r = rows(s)
        before = before_ref[s].astype(F32)
        pa = jnp.where(core == 0, before, before + sb_ref[s])
        pb = jnp.where(core == 0, before + sa_ref[s], before)
        o_ref[s, head] = normed(qa_ref[r], la_ref[r], pa)
        o_ref[s, 1 - head] = normed(qb_ref[r], lb_ref[r], pb)


def call(kernel, name, outs, *args, away=(), out_away=False, scratch=()):
    anywhere = pl.BlockSpec(memory_space=pltpu.HBM if out_away else pl.ANY)
    return pl.pallas_call(
        kernel,
        name=name,
        out_shape=[jax.ShapeDtypeStruct(s, d) for s, d in outs],
        in_specs=[SMEM if a.dtype == jnp.int32 else anywhere if i in away else VMEM for i, a in enumerate(args)],
        out_specs=[anywhere if out_away else VMEM for _ in outs],
        scratch_shapes=list(scratch),
        compiler_params=PARAMS,
    )(*args)


def body(tokens, proj_weights, norm_gain):
    place = lax.axis_index("seq")
    core = place & 1
    quad = place >> 3
    head = core ^ (quad & 1)
    spot = jnp.stack([core, head])
    quad = quad.reshape(1)
    wh = (proj_weights.astype(F32) * WSCALE).astype(jnp.float16)
    wh = jnp.transpose(wh, (1, 0, 2)).reshape(-1, 3, 2, DH)
    head0, head1 = wh[:, :, 0].reshape(-1, 3 * DH), wh[:, :, 1].reshape(-1, 3 * DH)
    keep = jnp.where(head == 0, head0, head1)
    give = jnp.where(head == 0, head1, head0)
    got = lax.ppermute(give, "seq", SIBLING)
    (copies,) = call(
        copies_kernel, "copies", [((SEQS,) + tokens.shape[1:], B16)], tokens[0], away=(0,), out_away=True,
        scratch=[pltpu.VMEM((4, 32) + tokens.shape[2:], B16), pltpu.SemaphoreType.DMA((4,)), pltpu.SemaphoreType.DMA((4, SEQS))],
    )
    copies, got = lax.optimization_barrier((copies, got))
    mine_t = lax.all_to_all(copies, "dp", 0, 0, tiled=True)
    first = core == 0
    pair = jnp.concatenate([jnp.where(first, keep, got), jnp.where(first, got, keep)], axis=0)
    full = lax.all_gather(pair, "seq", axis=0, tiled=True, axis_index_groups=SAME_HEAD)
    mine_t, full = lax.optimization_barrier((mine_t, full))
    other_t = lax.ppermute(mine_t, "seq", SIBLING)
    weights = (full.astype(F32) * (1.0 / WSCALE)).astype(B16)
    n = SEQS * BLOCK
    ta, tb = mine_t.reshape(n, -1), other_t.reshape(n, -1)
    outs = [((n, DH), B16), ((n, DH), F32), ((SEQS, DH, DH), F32)]
    qa, la, sa = call(first_kernel, "first", outs, ta, weights)
    width = tb.shape[1] // 4
    qb, lb, sb, chip = call(
        second_kernel, "second", outs + [((SEQS, DH, DH), B16)], tb, weights, sa, away=(0,),
        scratch=[pltpu.VMEM((4, n, width), B16), pltpu.VMEM((n, 3 * DH), F32), pltpu.SemaphoreType.DMA((4,))],
    )
    chip, qa, la, sa, qb, lb, sb, quad, spot = lax.optimization_barrier((chip, qa, la, sa, qb, lb, sb, quad, spot))

    square = (DH, DH)
    by_chip = lax.all_to_all(chip, "seq", 0, 0, tiled=True, axis_index_groups=QUAD)
    (total,) = call(total_kernel, "total", [(square, B16)], by_chip)
    totals = lax.all_gather(total, "seq", axis=0, axis_index_groups=ACROSS)
    (parts,) = call(parts_kernel, "parts", [((4,) + square, B16)], quad, by_chip, totals)
    back = lax.all_to_all(parts, "seq", 0, 0, tiled=True, axis_index_groups=QUAD)
    (out,) = call(
        final_kernel, "final", [((SEQS, 2, BLOCK, DH), B16)],
        spot, qa, qb, la, lb, back, sa, sb, norm_gain.reshape(2, DH),
    )
    out = lax.all_to_all(out.reshape(8, BLOCK, DH), ("seq", "dp"), 0, 0, tiled=True, axis_index_groups=OWNERS)
    (joined,) = call(
        join_kernel, "join", [((BLOCK, 8 * DH), B16)], out, out_away=True, scratch=[pltpu.SemaphoreType.DMA((8,))]
    )
    return joined[None]


def solution(mesh):
    in_specs = (P("dp", "seq", None), P(None, "seq", ("heads", "dp")), P(("heads", "dp")))
    out_specs = P("dp", "seq", "heads")
    return jax.shard_map(body, mesh=mesh, in_specs=in_specs, out_specs=out_specs, check_vma=False)
```

time: 127 us -> 131 us (1.031)
  blocking collectives: 89.2 us -> 96.7 us
  starting transfers between devices: 21.5 us -> 14.8 us
  Pallas kernels: 9.49 us -> 11.9 us
  local copies, waits for them, and re-layouts: 1.34 us -> 3.1 us
    all_gather x1, blocking collectives: 42.6 us -> 52 us  [body(): lax.all_gather(pair, 'seq', axis=0, tiled=True, axis_index_groups=SAME_HEAD)]
    ppermute x1, starting transfers between devices: 8.97 us -> 2.29 us  [body(): other_t = lax.ppermute(mine_t, 'seq', SIBLING)]
    pallas_call x5 -> x7, Pallas kernels: 6.69 us -> 11.9 us  [call(): pl.pallas_call(kernel, name=name, out_shape=[jax.ShapeDtypeStruct(s, d) f...]
    all_to_all x1, blocking collectives: 16.2 us -> 13.4 us  [body(): lax.all_to_all(out.reshape(8, BLOCK, DH), ('seq', 'dp'), 0, 0, tiled=True...]
    pallas_call x1 -> x0, Pallas kernels: 2.81 us -> none  [body(): pl.pallas_call(copies_kernel, name='copies', out_shape=jax.ShapeDtypeStru...]
    unnamed x3 -> x7, local copies, waits for them, and re-layouts: 0.03 us -> 2.78 us
  transfers between devices with their start and end apart: 3 -> 3, of which waited for: 1 -> 1; matrix products, arithmetic and copies ran while one was open for 2% -> 2% of each run, Pallas kernels for 4% -> 6%
where the time goes in v5:
time: 131 us
  blocking collectives  96.7 us (74%)
  starting transfers between devices  14.8 us (11%)
  Pallas kernels  11.9 us (9%)
  other arithmetic  3.52 us (3%)
  local copies, waits for them, and re-layouts  3.1 us (2%)
    all_gather x1, blocking collectives, body(): lax.all_gather(pair, 'seq', axis=0, tiled=True, axis_index_groups=SAME_HEAD)  52 us
    all_gather x1, blocking collectives, body(): totals = lax.all_gather(total, 'seq', axis=0, axis_index_groups=ACROSS)  16.2 us
    all_to_all x1, blocking collectives, body(): lax.all_to_all(out.reshape(8, BLOCK, DH), ('seq', 'dp'), 0, 0, tiled=True...  13.4 us
    pallas_call x7, Pallas kernels, call(): pl.pallas_call(kernel, name=name, out_shape=[jax.ShapeDtypeStruct(s, d) f...  11.9 us
    ppermute x1, starting transfers between devices, body(): got = lax.ppermute(give, 'seq', SIBLING)  8.79 us
    all_to_all x1, blocking collectives, body(): lax.all_to_all(parts, 'seq', 0, 0, tiled=True, axis_index_groups=QUAD)  7.9 us
    all_to_all x1, blocking collectives, body(): lax.all_to_all(chip, 'seq', 0, 0, tiled=True, axis_index_groups=QUAD)  7.26 us
    all_to_all x1, starting transfers between devices, body(): mine_t = lax.all_to_all(copies, 'dp', 0, 0, tiled=True)  3.7 us
  transfers between devices with their start and end apart: 3, of which 1 were waited for; matrix products, arithmetic and copies ran while one was open for 2% of the time, Pallas kernels for 6%

profile of v5, /device:TPU:1, one launch (start us, length us, event | category | flops | bytes accessed | tf_op | source)
XLA Modules:
  0.0 131.0 jit_solution(5797475238148785930)
XLA Ops:
  0.0 0.9 fusion
  0.9 0.1 reshape.22
  1.0 0.3 fusion.1
  1.3 0.2 broadcast_select_fusion
  1.5 8.8 %collective-permute-start = (f16[96,384]{1,0:T(8,128)(2,1)S(1)}, f16[96,384]{1,0:T(8,128)(2,1)S(1)}, u32[]{:S(2)}, u32[]{:S(2)}) collective-permute-start(f16[96,384]{1,0:T(8,128)(2,1)S(1)} %bitcast.34), channel_id=1, source_target_pairs={{0,16},{16,0},{32,48},{48,32},{64,80},{80,64},{96,112},{112,96},{1... | collective-permute-start | bytes 221192 | tf_op jit(solution)/shard_map/ppermute | solution.py:164
  10.3 0.0 copy-start.1
  10.3 1.1 copy-done.1
  11.5 5.2 %copies.1 = bf16[4,128,3072]{2,1,0:T(8,128)(2,1)S(1)} custom-call(bf16[128,3072]{1,0:T(8,128)(2,1)S(1)} %bitcast.29), custom_call_target="tpu_custom_call" | custom-call | tf_op jit(solution)/shard_map/copies/pallas_call | solution.py:141
  16.7 0.0 copy-start
  16.7 1.6 %copy-done = bf16[4,128,3072]{2,1,0:T(8,128)(2,1)} copy-done((bf16[4,128,3072]{2,1,0:T(8,128)(2,1)}, bf16[4,128,3072]{2,1,0:T(8,128)(2,1)S(1)}, u32[]{:S(2)}) %copy-start) | copy-done | bytes 3145752
  18.3 0.0 collective-permute-done
  18.3 3.7 %all-to-all-start = ((bf16[4,128,3072]{2,1,0:T(8,128)(2,1)}), bf16[4,128,3072]{2,1,0:T(8,128)(2,1)S(1)}, u32[]{:S(2)}, u32[]{:S(2)}) async-start(bf16[4,128,3072]{2,1,0:T(8,128)(2,1)} %copy-done), calls=%async_computation | async-start | bytes 6291456 | tf_op jit(solution)/shard_map/all_to_all | solution.py:170
  22.2 52.0 %all-gather.2 = f16[3072,384]{1,0:T(8,128)(2,1)} all-gather(f16[192,384]{1,0:T(8,128)(2,1)S(1)} %pad_maximum_fusion), channel_id=1, replica_groups={{0,32,64,96,144,176,208,240,256,288,320,352,400,432,464,496},{16,48,80,..., dimensions={0}, use_global_device_ids=true | all-gather | bytes 2506752 | tf_op jit(solution)/shard_map/all_gather | solution.py:173
  74.2 0.0 all-to-all-done
  74.2 2.3 %collective-permute-start.1 = (bf16[4,128,3072]{2,1,0:T(8,128)(2,1)S(1)}, bf16[4,128,3072]{2,1,0:T(8,128)(2,1)S(1)}, u32[]{:S(2)}, u32[]{:S(2)}) collective-permute-start(bf16[4,128,3072]{2,1,0:T(8,128)(2,1)S(1)} %all-to-all-done), channel_id=1, source_target_pairs={{0,16},{16,0},{32,48},{48,32},{64,80},{80,64},{96,112},{112,96},{1... | collective-permute-start | bytes 9437192 | tf_op jit(solution)/shard_map/ppermute | solution.py:175
  76.5 0.1 pad_add_fusion.spot_ref
  76.6 2.2 %multiply_convert_fusion.w_ref = bf16[3072,384]{1,0:T(8,128)(2,1)S(1)} fusion(f16[3072,384]{1,0:T(8,128)(2,1)} %all-gather.2), kind=kLoop, calls=%fused_computation | loop fusion | flops 3538944 | bytes 4718592 | tf_op jit(solution)/shard_map/convert_element_type | solution.py:176
  78.8 2.2 %first.1 = (bf16[512,128]{1,0:T(8,128)(2,1)S(1)}, f32[512,128]{1,0:T(8,128)S(1)}, f32[4,128,128]{2,1,0:T(8,128)S(1)}) custom-call(bf16[512,3072]{1,0:T(8,128)(2,1)S(1)} %bitcast.26, bf16[3072,384]{1,0:T(8,128)(2,1)S(1)} %multiply_convert_fusion.w_ref), custom_call_target="tpu_custom_call" | custom-call | tf_op jit(solution)/shard_map/first/pallas_call | solution.py:141
  80.9 0.8 collective-permute-done.1
  81.7 0.0 copy-start.2
  81.7 2.8 %second.1 = (bf16[512,128]{1,0:T(8,128)(2,1)S(1)}, f32[512,128]{1,0:T(8,128)S(1)}, f32[4,128,128]{2,1,0:T(8,128)S(1)}, bf16[4,128,128]{2,1,0:T(8,128)(2,1)S(1)}) custom-call(bf16[512,3072]{1,0:T(8,128)(2,1)S(1)} %bitcast.27, bf16[3072,384]{1,0:T(8,128)(2,1)S(1)} %multiply_convert_fusion.w_ref, f32[4,128,128]{2,1,0:T(8,128)S(1)} %get-tuple-element.43.sa_ref), custom_call_target="tpu_custom_call" | custom-call | tf_op jit(solution)/shard_map/second/pallas_call | solution.py:141
  84.5 7.3 %all_to_all.20.r_ref = bf16[4,128,128]{2,1,0:T(8,128)(2,1)S(1)} all-to-all(bf16[4,128,128]{2,1,0:T(8,128)(2,1)S(1)} %get-tuple-element.42), channel_id=1, replica_groups={{0,32,64,96},{16,48,80,112},{128,160,192,224},{144,176,208,240},{256,28..., dimensions={0} | all-to-all | bytes 262144 | tf_op jit(solution)/shard_map/all_to_all | solution.py:189
  91.8 16.2 %all-gather = bf16[512,128]{1,0:T(8,128)(2,1)S(1)} all-gather(bf16[128,128]{1,0:T(8,128)(2,1)S(1)} %total.1), channel_id=2, replica_groups={{0,144,256,400},{16,128,272,384},{32,176,288,432},{48,160,304,416},{64,..., dimensions={0}, use_global_device_ids=true | all-gather | bytes 163840 | tf_op jit(solution)/shard_map/all_gather | solution.py:191
  108.0 7.9 %all_to_all.21.before_ref = bf16[4,128,128]{2,1,0:T(8,128)(2,1)S(1)} all-to-all(bf16[4,128,128]{2,1,0:T(8,128)(2,1)S(1)} %parts.1), channel_id=1, replica_groups={{0,32,64,96},{16,48,80,112},{128,160,192,224},{144,176,208,240},{256,28..., dimensions={0} | all-to-all | bytes 262144 | tf_op jit(solution)/shard_map/all_to_all | solution.py:193
  115.9 0.0 copy-done.2
  115.9 0.9 final.1
  116.9 13.4 %all_to_all.22.i_ref = bf16[8,128,128]{2,1,0:T(8,128)(2,1)S(1)} all-to-all(bf16[8,128,128]{2,1,0:T(8,128)(2,1)S(1)} %bitcast.28), channel_id=1, replica_groups={{0,16,1,17,2,18,3,19},{32,48,33,49,34,50,35,51},{64,80,65,81,66,82,67,8..., dimensions={0} | all-to-all | bytes 524288 | tf_op jit(solution)/shard_map/all_to_all | solution.py:198
  130.2 0.8 join.1
  (5 shorter events, 0.2 us)
Async XLA Ops:
  1.5 16.8 %collective-permute-start = (f16[96,384]{1,0:T(8,128)(2,1)S(1)}, f16[96,384]{1,0:T(8,128)(2,1)S(1)}, u32[]{:S(2)}, u32[]{:S(2)}) collective-permute-start(f16[96,384]{1,0:T(8,128)(2,1)S(1)} %bitcast.34), channel_id=1, source_target_pairs={{0,16},{16,0},{32,48},{48,32},{64,80},{80,64},{96,112},{112,96},{1... | collective-permute-start | bytes 221192 | tf_op jit(solution)/shard_map/ppermute | solution.py:164
  10.3 1.1 copy-start.1
  16.7 1.6 %copy-start = (bf16[4,128,3072]{2,1,0:T(8,128)(2,1)}, bf16[4,128,3072]{2,1,0:T(8,128)(2,1)S(1)}, u32[]{:S(2)}) copy-start(bf16[4,128,3072]{2,1,0:T(8,128)(2,1)S(1)} %copies.1) | copy-start | bytes 9437188
  18.3 55.8 %all-to-all-start = ((bf16[4,128,3072]{2,1,0:T(8,128)(2,1)}), bf16[4,128,3072]{2,1,0:T(8,128)(2,1)S(1)}, u32[]{:S(2)}, u32[]{:S(2)}) async-start(bf16[4,128,3072]{2,1,0:T(8,128)(2,1)} %copy-done), calls=%async_computation | async-start | bytes 6291456 | tf_op jit(solution)/shard_map/all_to_all | solution.py:170
  74.2 7.6 %collective-permute-start.1 = (bf16[4,128,3072]{2,1,0:T(8,128)(2,1)S(1)}, bf16[4,128,3072]{2,1,0:T(8,128)(2,1)S(1)}, u32[]{:S(2)}, u32[]{:S(2)}) collective-permute-start(bf16[4,128,3072]{2,1,0:T(8,128)(2,1)S(1)} %all-to-all-done), channel_id=1, source_target_pairs={{0,16},{16,0},{32,48},{48,32},{64,80},{80,64},{96,112},{112,96},{1... | collective-permute-start | bytes 9437192 | tf_op jit(solution)/shard_map/ppermute | solution.py:175
  81.7 34.2 %copy-start.2 = (f32[256]{0:T(256)S(1)}, f32[256]{0:T(256)}, u32[]{:S(2)}) copy-start(f32[256]{0:T(256)} %param.5) | copy-start | bytes 3076

commit v6 on v5

--- a/solution.py
+++ b/solution.py
@@ -13,11 +13,15 @@
 F32 = jnp.float32
 B16 = jnp.bfloat16
 SIBLING = [(i, i ^ 1) for i in range(SEQ)]
-QUAD = [[8 * a + 2 * b + c for b in range(4)] for a in range(4) for c in range(2)]
 
 
 def holder(z, head):
-    return 2 * z + (head ^ ((z >> 2) & 1))
+    return 2 * z + (head ^ ((z ^ (z >> 2)) & 1))
+
+
+QUAD = [[holder(4 * a + b, h) for b in range(4)] for a in range(4) for h in range(2)]
+def head_of(place):
+    return (place ^ (place >> 1) ^ (place >> 3)) & 1
 
 
 SAME_HEAD = [[holder(z, h) for z in range(16)] for h in range(2)]
@@ -81,8 +85,8 @@
     o_ref[...] = (r_ref[0].astype(F32) + r_ref[1].astype(F32) + r_ref[2].astype(F32) + r_ref[3].astype(F32)).astype(B16)
 
 
-def parts_kernel(quad_ref, r_ref, totals_ref, o_ref):
-    quad = quad_ref[0]
+def parts_kernel(spot_ref, r_ref, totals_ref, o_ref):
+    quad = spot_ref[0] >> 3
     before = jnp.zeros((DH, DH), F32)
     for a in range(3):
         before = before + jnp.where(a < quad, totals_ref[a].astype(F32), 0.0)
@@ -92,20 +96,11 @@
         o_ref[j + 1] = before.astype(B16)
 
 
-def copies_kernel(t_ref, o_ref, buf, sem_in, sem):
-    count = buf.shape[0]
-    loads = [pltpu.make_async_copy(t_ref.at[pl.ds(i * 32, 32)], buf.at[i], sem_in.at[i]) for i in range(count)]
-    stores = [
-        pltpu.make_async_copy(buf.at[i], o_ref.at[s, pl.ds(i * 32, 32)], sem.at[i, s])
-        for i in range(count) for s in range(SEQS)
-    ]
-    for c in loads:
+def copies_kernel(t_ref, o_ref, sem):
+    copies = [pltpu.make_async_copy(t_ref, o_ref.at[s], sem.at[s]) for s in range(SEQS)]
+    for c in copies:
         c.start()
-    for i in range(count):
-        loads[i].wait()
-        for c in stores[i * SEQS : (i + 1) * SEQS]:
-            c.start()
-    for c in stores:
+    for c in copies:
         c.wait()
 
 
@@ -119,7 +114,7 @@
 
 
 def final_kernel(spot_ref, qa_ref, qb_ref, la_ref, lb_ref, before_ref, sa_ref, sb_ref, gain_ref, o_ref):
-    core, head = spot_ref[0], spot_ref[1]
+    core, head = spot_ref[0] & 1, head_of(spot_ref[0])
     gain = jnp.where(head == 0, gain_ref[0:1], gain_ref[1:2])
 
     def normed(q, l, p):
@@ -136,8 +131,8 @@
         o_ref[s, 1 - head] = normed(qb_ref[r], lb_ref[r], pb)
 
 
-def call(kernel, name, outs, *args, away=(), out_away=False, scratch=()):
-    anywhere = pl.BlockSpec(memory_space=pltpu.HBM if out_away else pl.ANY)
+def call(kernel, name, outs, *args, away=(), out_away=False, scratch=(), params=True):
+    anywhere = pl.BlockSpec(memory_space=pl.ANY)
     return pl.pallas_call(
         kernel,
         name=name,
@@ -145,17 +140,15 @@
         in_specs=[SMEM if a.dtype == jnp.int32 else anywhere if i in away else VMEM for i, a in enumerate(args)],
         out_specs=[anywhere if out_away else VMEM for _ in outs],
         scratch_shapes=list(scratch),
-        compiler_params=PARAMS,
+        compiler_params=PARAMS if params else None,
     )(*args)
 
 
 def body(tokens, proj_weights, norm_gain):
     place = lax.axis_index("seq")
     core = place & 1
-    quad = place >> 3
-    head = core ^ (quad & 1)
-    spot = jnp.stack([core, head])
-    quad = quad.reshape(1)
+    head = head_of(place)
+    spot = place.reshape(1)
     wh = (proj_weights.astype(F32) * WSCALE).astype(jnp.float16)
     wh = jnp.transpose(wh, (1, 0, 2)).reshape(-1, 3, 2, DH)
     head0, head1 = wh[:, :, 0].reshape(-1, 3 * DH), wh[:, :, 1].reshape(-1, 3 * DH)
@@ -163,8 +156,8 @@
     give = jnp.where(head == 0, head1, head0)
     got = lax.ppermute(give, "seq", SIBLING)
     (copies,) = call(
-        copies_kernel, "copies", [((SEQS,) + tokens.shape[1:], B16)], tokens[0], away=(0,), out_away=True,
-        scratch=[pltpu.VMEM((4, 32) + tokens.shape[2:], B16), pltpu.SemaphoreType.DMA((4,)), pltpu.SemaphoreType.DMA((4, SEQS))],
+        copies_kernel, "copies", [((SEQS,) + tokens.shape[1:], B16)], tokens[0], out_away=True, params=False,
+        scratch=[pltpu.SemaphoreType.DMA((SEQS,))],
     )
     copies, got = lax.optimization_barrier((copies, got))
     mine_t = lax.all_to_all(copies, "dp", 0, 0, tiled=True)
@@ -183,13 +176,13 @@
         second_kernel, "second", outs + [((SEQS, DH, DH), B16)], tb, weights, sa, away=(0,),
         scratch=[pltpu.VMEM((4, n, width), B16), pltpu.VMEM((n, 3 * DH), F32), pltpu.SemaphoreType.DMA((4,))],
     )
-    chip, qa, la, sa, qb, lb, sb, quad, spot = lax.optimization_barrier((chip, qa, la, sa, qb, lb, sb, quad, spot))
+    chip, qa, la, sa, qb, lb, sb, spot = lax.optimization_barrier((chip, qa, la, sa, qb, lb, sb, spot))
 
     square = (DH, DH)
     by_chip = lax.all_to_all(chip, "seq", 0, 0, tiled=True, axis_index_groups=QUAD)
     (total,) = call(total_kernel, "total", [(square, B16)], by_chip)
     totals = lax.all_gather(total, "seq", axis=0, axis_index_groups=ACROSS)
-    (parts,) = call(parts_kernel, "parts", [((4,) + square, B16)], quad, by_chip, totals)
+    (parts,) = call(parts_kernel, "parts", [((4,) + square, B16)], spot, by_chip, totals)
     back = lax.all_to_all(parts, "seq", 0, 0, tiled=True, axis_index_groups=QUAD)
     (out,) = call(
         final_kernel, "final", [((SEQS, 2, BLOCK, DH), B16)],

time: 131 us -> 124 us (0.947)
  Pallas kernels: 11.9 us -> 8.97 us
  blocking collectives: 96.7 us -> 93.8 us
  local copies, waits for them, and re-layouts: 3.1 us -> 0.35 us
    all_gather x1, blocking collectives: 52 us -> 48.2 us  [body(): lax.all_gather(pair, 'seq', axis=0, tiled=True, axis_index_groups=SAME_HEAD)]
    pallas_call x7, Pallas kernels: 11.9 us -> 8.97 us  [call(): pl.pallas_call(kernel, name=name, out_shape=[jax.ShapeDtypeStruct(s, d) f...]
    unnamed x7 -> x3, local copies, waits for them, and re-layouts: 2.78 us -> 0.03 us
    all_to_all x1, blocking collectives: 13.4 us -> 12 us  [body(): lax.all_to_all(out.reshape(8, BLOCK, DH), ('seq', 'dp'), 0, 0, tiled=True...]
  transfers between devices with their start and end apart: 3 -> 3, of which waited for: 1 -> 1; matrix products, arithmetic and copies ran while one was open for 2% -> 2% of each run, Pallas kernels for 6% -> 4%
where the time goes in v6:
time: 124 us; the launch traced here: 123 us
  blocking collectives  93.8 us (76%)
  starting transfers between devices  15.7 us (13%)
  Pallas kernels  8.97 us (7%)
  other arithmetic  3.44 us (3%)
    all_gather x1, blocking collectives, body(): lax.all_gather(pair, 'seq', axis=0, tiled=True, axis_index_groups=SAME_HEAD)  48.2 us
    all_gather x1, blocking collectives, body(): totals = lax.all_gather(total, 'seq', axis=0, axis_index_groups=ACROSS)  16.8 us
    all_to_all x1, blocking collectives, body(): lax.all_to_all(out.reshape(8, BLOCK, DH), ('seq', 'dp'), 0, 0, tiled=True...  12 us
    pallas_call x7, Pallas kernels, call(): pl.pallas_call(kernel, name=name, out_shape=[jax.ShapeDtypeStruct(s, d) f...  8.97 us
    ppermute x1, starting transfers between devices, body(): got = lax.ppermute(give, 'seq', SIBLING)  8.79 us
    all_to_all x1, blocking collectives, body(): lax.all_to_all(parts, 'seq', 0, 0, tiled=True, axis_index_groups=QUAD)  8.7 us
    all_to_all x1, blocking collectives, body(): lax.all_to_all(chip, 'seq', 0, 0, tiled=True, axis_index_groups=QUAD)  8.08 us
    all_to_all x1, starting transfers between devices, body(): mine_t = lax.all_to_all(copies, 'dp', 0, 0, tiled=True)  3.71 us
  transfers between devices with their start and end apart: 3, of which 1 were waited for; matrix products, arithmetic and copies ran while one was open for 2% of the time, Pallas kernels for 4%

profile of v6, /device:TPU:1, one launch (start us, length us, event | category | flops | bytes accessed | tf_op | source)
XLA Modules:
  0.0 123.2 jit_solution(9305337285973279183)
XLA Ops:
  0.0 0.9 fusion
  0.9 0.1 reshape.22
  1.0 0.3 fusion.1
  1.3 0.2 broadcast_select_fusion
  1.5 8.8 %collective-permute-start = (f16[96,384]{1,0:T(8,128)(2,1)S(1)}, f16[96,384]{1,0:T(8,128)(2,1)S(1)}, u32[]{:S(2)}, u32[]{:S(2)}) collective-permute-start(f16[96,384]{1,0:T(8,128)(2,1)S(1)} %bitcast.32), channel_id=1, source_target_pairs={{0,16},{16,0},{32,48},{48,32},{64,80},{80,64},{96,112},{112,96},{1... | collective-permute-start | bytes 221192 | tf_op jit(solution)/shard_map/ppermute | solution.py:157
  10.3 2.8 %copies.1 = bf16[4,128,3072]{2,1,0:T(8,128)(2,1)} custom-call(bf16[128,3072]{1,0:T(8,128)(2,1)} %bitcast.29), custom_call_target="tpu_custom_call" | custom-call | tf_op jit(solution)/shard_map/copies/pallas_call | solution.py:136
  13.1 0.0 collective-permute-done
  13.2 3.7 %all-to-all-start = ((bf16[4,128,3072]{2,1,0:T(8,128)(2,1)}), bf16[4,128,3072]{2,1,0:T(8,128)(2,1)S(1)}, u32[]{:S(2)}, u32[]{:S(2)}) async-start(bf16[4,128,3072]{2,1,0:T(8,128)(2,1)} %copies.1), calls=%async_computation | async-start | bytes 6291456 | tf_op jit(solution)/shard_map/all_to_all | solution.py:163
  17.0 48.2 %all-gather.2 = f16[3072,384]{1,0:T(8,128)(2,1)} all-gather(f16[192,384]{1,0:T(8,128)(2,1)S(1)} %pad_maximum_fusion), channel_id=1, replica_groups={{0,48,64,112,144,160,208,224,256,304,320,368,400,416,464,480},{16,32,80..., dimensions={0}, use_global_device_ids=true | all-gather | bytes 2506752 | tf_op jit(solution)/shard_map/all_gather | solution.py:166
  65.2 0.0 all-to-all-done
  65.2 3.2 %collective-permute-start.1 = (bf16[4,128,3072]{2,1,0:T(8,128)(2,1)S(1)}, bf16[4,128,3072]{2,1,0:T(8,128)(2,1)S(1)}, u32[]{:S(2)}, u32[]{:S(2)}) collective-permute-start(bf16[4,128,3072]{2,1,0:T(8,128)(2,1)S(1)} %all-to-all-done), channel_id=1, source_target_pairs={{0,16},{16,0},{32,48},{48,32},{64,80},{80,64},{96,112},{112,96},{1... | collective-permute-start | bytes 9437192 | tf_op jit(solution)/shard_map/ppermute | solution.py:168
  68.4 2.2 %multiply_convert_fusion.w_ref = bf16[3072,384]{1,0:T(8,128)(2,1)S(1)} fusion(f16[3072,384]{1,0:T(8,128)(2,1)} %all-gather.2), kind=kLoop, calls=%fused_computation | loop fusion | flops 3538944 | bytes 4718592 | tf_op jit(solution)/shard_map/convert_element_type | solution.py:169
  70.6 2.2 %first.1 = (bf16[512,128]{1,0:T(8,128)(2,1)S(1)}, f32[512,128]{1,0:T(8,128)S(1)}, f32[4,128,128]{2,1,0:T(8,128)S(1)}) custom-call(bf16[512,3072]{1,0:T(8,128)(2,1)S(1)} %bitcast.24, bf16[3072,384]{1,0:T(8,128)(2,1)S(1)} %multiply_convert_fusion.w_ref), custom_call_target="tpu_custom_call" | custom-call | tf_op jit(solution)/shard_map/first/pallas_call | solution.py:136
  72.7 0.9 collective-permute-done.1
  73.6 0.0 copy-start
  73.6 2.8 %second.1 = (bf16[512,128]{1,0:T(8,128)(2,1)S(1)}, f32[512,128]{1,0:T(8,128)S(1)}, f32[4,128,128]{2,1,0:T(8,128)S(1)}, bf16[4,128,128]{2,1,0:T(8,128)(2,1)S(1)}) custom-call(bf16[512,3072]{1,0:T(8,128)(2,1)S(1)} %bitcast.25, bf16[3072,384]{1,0:T(8,128)(2,1)S(1)} %multiply_convert_fusion.w_ref, f32[4,128,128]{2,1,0:T(8,128)S(1)} %get-tuple-element.41.sa_ref), custom_call_target="tpu_custom_call" | custom-call | tf_op jit(solution)/shard_map/second/pallas_call | solution.py:136
  76.4 8.1 %all_to_all.20.r_ref = bf16[4,128,128]{2,1,0:T(8,128)(2,1)S(1)} all-to-all(bf16[4,128,128]{2,1,0:T(8,128)(2,1)S(1)} %get-tuple-element.40), channel_id=1, replica_groups={{0,48,64,112},{16,32,80,96},{144,160,208,224},{128,176,192,240},{256,30..., dimensions={0} | all-to-all | bytes 262144 | tf_op jit(solution)/shard_map/all_to_all | solution.py:182
  84.5 16.8 %all-gather = bf16[512,128]{1,0:T(8,128)(2,1)S(1)} all-gather(bf16[128,128]{1,0:T(8,128)(2,1)S(1)} %total.1), channel_id=2, replica_groups={{0,144,256,400},{16,128,272,384},{48,160,304,416},{32,176,288,432},{64,..., dimensions={0}, use_global_device_ids=true | all-gather | bytes 163840 | tf_op jit(solution)/shard_map/all_gather | solution.py:184
  101.4 8.7 %all_to_all.21.before_ref = bf16[4,128,128]{2,1,0:T(8,128)(2,1)S(1)} all-to-all(bf16[4,128,128]{2,1,0:T(8,128)(2,1)S(1)} %parts.1), channel_id=1, replica_groups={{0,48,64,112},{16,32,80,96},{144,160,208,224},{128,176,192,240},{256,30..., dimensions={0} | all-to-all | bytes 262144 | tf_op jit(solution)/shard_map/all_to_all | solution.py:186
  110.1 0.0 copy-done
  110.1 0.4 final.1
  110.5 12.0 %all_to_all.22.i_ref = bf16[8,128,128]{2,1,0:T(8,128)(2,1)S(1)} all-to-all(bf16[8,128,128]{2,1,0:T(8,128)(2,1)S(1)} %bitcast.26), channel_id=1, replica_groups={{0,16,1,17,2,18,3,19},{48,32,49,33,50,34,51,35},{64,80,65,81,66,82,67,8..., dimensions={0} | all-to-all | bytes 524288 | tf_op jit(solution)/shard_map/all_to_all | solution.py:191
  122.5 0.8 join.1
  (5 shorter events, 0.2 us)
Async XLA Ops:
  1.5 11.6 %collective-permute-start = (f16[96,384]{1,0:T(8,128)(2,1)S(1)}, f16[96,384]{1,0:T(8,128)(2,1)S(1)}, u32[]{:S(2)}, u32[]{:S(2)}) collective-permute-start(f16[96,384]{1,0:T(8,128)(2,1)S(1)} %bitcast.32), channel_id=1, source_target_pairs={{0,16},{16,0},{32,48},{48,32},{64,80},{80,64},{96,112},{112,96},{1... | collective-permute-start | bytes 221192 | tf_op jit(solution)/shard_map/ppermute | solution.py:157
  13.2 52.0 %all-to-all-start = ((bf16[4,128,3072]{2,1,0:T(8,128)(2,1)}), bf16[4,128,3072]{2,1,0:T(8,128)(2,1)S(1)}, u32[]{:S(2)}, u32[]{:S(2)}) async-start(bf16[4,128,3072]{2,1,0:T(8,128)(2,1)} %copies.1), calls=%async_computation | async-start | bytes 6291456 | tf_op jit(solution)/shard_map/all_to_all | solution.py:163
  65.2 8.4 %collective-permute-start.1 = (bf16[4,128,3072]{2,1,0:T(8,128)(2,1)S(1)}, bf16[4,128,3072]{2,1,0:T(8,128)(2,1)S(1)}, u32[]{:S(2)}, u32[]{:S(2)}) collective-permute-start(bf16[4,128,3072]{2,1,0:T(8,128)(2,1)S(1)} %all-to-all-done), channel_id=1, source_target_pairs={{0,16},{16,0},{32,48},{48,32},{64,80},{80,64},{96,112},{112,96},{1... | collective-permute-start | bytes 9437192 | tf_op jit(solution)/shard_map/ppermute | solution.py:168
  73.6 36.5 %copy-start = (f32[256]{0:T(256)S(1)}, f32[256]{0:T(256)}, u32[]{:S(2)}) copy-start(f32[256]{0:T(256)} %param.5) | copy-start | bytes 3076

commit v7 on v6

--- a/solution.py
+++ b/solution.py
@@ -63,22 +63,22 @@
     block_work(jnp.dot(t_ref[...], w_ref[...], preferred_element_type=F32), q_ref, l_ref, s_ref)
 
 
-def second_kernel(t_ref, w_ref, sa_ref, q_ref, l_ref, s_ref, chip_ref, piece, acc, sem):
-    count, _, width = piece.shape
-    span = [slice(i * width, (i + 1) * width) for i in range(count)]
-    copies = [pltpu.make_async_copy(t_ref.at[:, span[i]], piece.at[i], sem.at[i]) for i in range(count)]
-    for c in copies:
-        c.start()
-    for i in range(count):
-        copies[i].wait()
-        part = jnp.dot(piece[i], w_ref[span[i]], preferred_element_type=F32)
-        if i == 0:
-            acc[...] = part
-        else:
-            acc[...] += part
-    block_work(acc[...], q_ref, l_ref, s_ref)
+def second_kernel(t_ref, w_ref, sa_ref, q_ref, l_ref, s_ref, chip_ref):
+    block_work(jnp.dot(t_ref[...], w_ref[...], preferred_element_type=F32), q_ref, l_ref, s_ref)
     for s in range(SEQS):
         chip_ref[s] = (sa_ref[s] + s_ref[s]).astype(B16)
+
+
+def heads_kernel(spot_ref, w_ref, keep_ref, give_ref):
+    mine = head_of(spot_ref[0]) == 0
+    for j in range(3):
+        low, high = w_ref[j, :, :DH], w_ref[j, :, DH:]
+        keep_ref[:, j * DH : (j + 1) * DH] = jnp.where(mine, low, high)
+        give_ref[:, j * DH : (j + 1) * DH] = jnp.where(mine, high, low)
+
+
+def to_half(w):
+    return (w.astype(F32) * WSCALE).astype(jnp.float16)
 
 
 def total_kernel(r_ref, o_ref):
@@ -147,14 +147,11 @@
 def body(tokens, proj_weights, norm_gain):
     place = lax.axis_index("seq")
     core = place & 1
-    head = head_of(place)
     spot = place.reshape(1)
-    wh = (proj_weights.astype(F32) * WSCALE).astype(jnp.float16)
-    wh = jnp.transpose(wh, (1, 0, 2)).reshape(-1, 3, 2, DH)
-    head0, head1 = wh[:, :, 0].reshape(-1, 3 * DH), wh[:, :, 1].reshape(-1, 3 * DH)
-    keep = jnp.where(head == 0, head0, head1)
-    give = jnp.where(head == 0, head1, head0)
-    got = lax.ppermute(give, "seq", SIBLING)
+    own = ((proj_weights.shape[1], 3 * DH), B16)
+    keep, give = call(heads_kernel, "heads", [own, own], spot, proj_weights)
+    keep = to_half(keep)
+    got = lax.ppermute(to_half(give), "seq", SIBLING)
     (copies,) = call(
         copies_kernel, "copies", [((SEQS,) + tokens.shape[1:], B16)], tokens[0], out_away=True, params=False,
         scratch=[pltpu.SemaphoreType.DMA((SEQS,))],
@@ -164,18 +161,14 @@
     first = core == 0
     pair = jnp.concatenate([jnp.where(first, keep, got), jnp.where(first, got, keep)], axis=0)
     full = lax.all_gather(pair, "seq", axis=0, tiled=True, axis_index_groups=SAME_HEAD)
-    mine_t, full = lax.optimization_barrier((mine_t, full))
+    weights = (full.astype(F32) * (1.0 / WSCALE)).astype(B16)
+    mine_t, weights = lax.optimization_barrier((mine_t, weights))
     other_t = lax.ppermute(mine_t, "seq", SIBLING)
-    weights = (full.astype(F32) * (1.0 / WSCALE)).astype(B16)
     n = SEQS * BLOCK
     ta, tb = mine_t.reshape(n, -1), other_t.reshape(n, -1)
     outs = [((n, DH), B16), ((n, DH), F32), ((SEQS, DH, DH), F32)]
     qa, la, sa = call(first_kernel, "first", outs, ta, weights)
-    width = tb.shape[1] // 4
-    qb, lb, sb, chip = call(
-        second_kernel, "second", outs + [((SEQS, DH, DH), B16)], tb, weights, sa, away=(0,),
-        scratch=[pltpu.VMEM((4, n, width), B16), pltpu.VMEM((n, 3 * DH), F32), pltpu.SemaphoreType.DMA((4,))],
-    )
+    qb, lb, sb, chip = call(second_kernel, "second", outs + [((SEQS, DH, DH), B16)], tb, weights, sa)
     chip, qa, la, sa, qb, lb, sb, spot = lax.optimization_barrier((chip, qa, la, sa, qb, lb, sb, spot))
 
     square = (DH, DH)

time: 124 us -> 122 us (0.984)
  other arithmetic: 3.44 us -> 0.71 us
  blocking collectives: 93.8 us -> 92.1 us
  Pallas kernels: 8.97 us -> 10.3 us
    convert_element_type x1, other arithmetic: 2.2 us -> 0.6 us  [body(): weights = (full.astype(F32) * (1.0 / WSCALE)).astype(B16)]
    all_gather x1, blocking collectives: 48.2 us -> 46.8 us  [body(): lax.all_gather(pair, 'seq', axis=0, tiled=True, axis_index_groups=SAME_HEAD)]
    pallas_call x7 -> x8, Pallas kernels: 8.97 us -> 10.3 us  [call(): pl.pallas_call(kernel, name=name, out_shape=[jax.ShapeDtypeStruct(s, d) f...]
    all_to_all x1, blocking collectives: 12 us -> 10.7 us  [body(): lax.all_to_all(out.reshape(8, BLOCK, DH), ('seq', 'dp'), 0, 0, tiled=True...]
  transfers between devices with their start and end apart: 3 -> 3, of which waited for: 1 -> 1; matrix products, arithmetic and copies ran while one was open for 2% -> 1% of each run, Pallas kernels for 4% -> 6%
where the time goes in v7:
time: 122 us
  blocking collectives  92.1 us (75%)
  starting transfers between devices  16.4 us (13%)
  Pallas kernels  10.3 us (8%)
  waiting for transfers between devices  1.42 us (1%)
    all_gather x1, blocking collectives, body(): lax.all_gather(pair, 'seq', axis=0, tiled=True, axis_index_groups=SAME_HEAD)  46.8 us
    all_gather x1, blocking collectives, body(): totals = lax.all_gather(total, 'seq', axis=0, axis_index_groups=ACROSS)  17.2 us
    all_to_all x1, blocking collectives, body(): lax.all_to_all(out.reshape(8, BLOCK, DH), ('seq', 'dp'), 0, 0, tiled=True...  10.7 us
    pallas_call x8, Pallas kernels, call(): pl.pallas_call(kernel, name=name, out_shape=[jax.ShapeDtypeStruct(s, d) f...  10.3 us
    all_to_all x1, blocking collectives, body(): lax.all_to_all(parts, 'seq', 0, 0, tiled=True, axis_index_groups=QUAD)  9.36 us
    ppermute x1, starting transfers between devices, body(): got = lax.ppermute(to_half(give), 'seq', SIBLING)  8.79 us
    all_to_all x1, blocking collectives, body(): lax.all_to_all(chip, 'seq', 0, 0, tiled=True, axis_index_groups=QUAD)  8.08 us
    all_to_all x1, starting transfers between devices, body(): mine_t = lax.all_to_all(copies, 'dp', 0, 0, tiled=True)  4.65 us
  transfers between devices with their start and end apart: 3, of which 1 were waited for; matrix products, arithmetic and copies ran while one was open for 1% of the time, Pallas kernels for 6%

profile of v7, /device:TPU:1, one launch (start us, length us, event | category | flops | bytes accessed | tf_op | source)
XLA Modules:
  0.0 122.0 jit_solution(1037898743474610051)
XLA Ops:
  0.0 0.0 copy-start
  0.0 0.9 copy-done
  1.0 8.8 %collective-permute-start = (f16[96,384]{1,0:T(8,128)(2,1)S(1)}, f16[96,384]{1,0:T(8,128)(2,1)S(1)}, u32[]{:S(2)}, u32[]{:S(2)}) collective-permute-start(f16[96,384]{1,0:T(8,128)(2,1)S(1)} %multiply_convert_fusion.2), channel_id=1, source_target_pairs={{0,16},{16,0},{32,48},{48,32},{64,80},{80,64},{96,112},{112,96},{1... | collective-permute-start | bytes 221192 | tf_op jit(solution)/shard_map/ppermute | solution.py:154
  9.8 2.9 %copies.1 = bf16[4,128,3072]{2,1,0:T(8,128)(2,1)} custom-call(bf16[128,3072]{1,0:T(8,128)(2,1)} %bitcast.12), custom_call_target="tpu_custom_call" | custom-call | tf_op jit(solution)/shard_map/copies/pallas_call | solution.py:136
  12.6 0.0 collective-permute-done
  12.6 4.7 %all-to-all-start = ((bf16[4,128,3072]{2,1,0:T(8,128)(2,1)}), bf16[4,128,3072]{2,1,0:T(8,128)(2,1)}, u32[]{:S(2)}, u32[]{:S(2)}) async-start(bf16[4,128,3072]{2,1,0:T(8,128)(2,1)} %copies.1), calls=%async_computation | async-start | bytes 6291456 | tf_op jit(solution)/shard_map/all_to_all | solution.py:160
  17.4 46.8 %all-gather.2 = f16[3072,384]{1,0:T(8,128)(2,1)S(1)} all-gather(f16[192,384]{1,0:T(8,128)(2,1)S(1)} %pad_maximum_fusion), channel_id=1, replica_groups={{0,48,64,112,144,160,208,224,256,304,320,368,400,416,464,480},{16,32,80..., dimensions={0}, use_global_device_ids=true | all-gather | bytes 2506752 | tf_op jit(solution)/shard_map/all_gather | solution.py:163
  64.2 0.6 multiply_convert_fusion.w_ref
  64.8 0.0 all-to-all-done
  64.8 2.9 %collective-permute-start.1 = (bf16[4,128,3072]{2,1,0:T(8,128)(2,1)}, bf16[4,128,3072]{2,1,0:T(8,128)(2,1)S(1)}, u32[]{:S(2)}, u32[]{:S(2)}) collective-permute-start(bf16[4,128,3072]{2,1,0:T(8,128)(2,1)} %all-to-all-done), channel_id=1, source_target_pairs={{0,16},{16,0},{32,48},{48,32},{64,80},{80,64},{96,112},{112,96},{1... | collective-permute-start | bytes 9437192 | tf_op jit(solution)/shard_map/ppermute | solution.py:166
  67.7 4.1 %first.1 = (bf16[512,128]{1,0:T(8,128)(2,1)S(1)}, f32[512,128]{1,0:T(8,128)S(1)}, f32[4,128,128]{2,1,0:T(8,128)S(1)}) custom-call(bf16[512,3072]{1,0:T(8,128)(2,1)} %bitcast.3.t_ref, bf16[3072,384]{1,0:T(8,128)(2,1)S(1)} %multiply_convert_fusion.w_ref), custom_call_target="tpu_custom_call" | custom-call | tf_op jit(solution)/shard_map/first/pallas_call | solution.py:136
  71.8 1.4 %collective-permute-done.1 = bf16[4,128,3072]{2,1,0:T(8,128)(2,1)S(1)} collective-permute-done((bf16[4,128,3072]{2,1,0:T(8,128)(2,1)}, bf16[4,128,3072]{2,1,0:T(8,128)(2,1)S(1)}, u32[]{:S(2)}, u32[]{:S(2)}) %collective-permute-start.1) | collective-permute-done | bytes 3145760 | tf_op jit(solution)/shard_map/ppermute | solution.py:166
  73.2 0.0 copy-start.1
  73.2 2.2 %second.1 = (bf16[512,128]{1,0:T(8,128)(2,1)S(1)}, f32[512,128]{1,0:T(8,128)S(1)}, f32[4,128,128]{2,1,0:T(8,128)S(1)}, bf16[4,128,128]{2,1,0:T(8,128)(2,1)S(1)}) custom-call(bf16[512,3072]{1,0:T(8,128)(2,1)S(1)} %bitcast.8, bf16[3072,384]{1,0:T(8,128)(2,1)S(1)} %multiply_convert_fusion.w_ref, f32[4,128,128]{2,1,0:T(8,128)S(1)} %get-tuple-element.45.sa_ref), custom_call_target="tpu_custom_call" | custom-call | tf_op jit(solution)/shard_map/second/pallas_call | solution.py:136
  75.4 8.1 %all_to_all.20.r_ref = bf16[4,128,128]{2,1,0:T(8,128)(2,1)S(1)} all-to-all(bf16[4,128,128]{2,1,0:T(8,128)(2,1)S(1)} %get-tuple-element.44), channel_id=1, replica_groups={{0,48,64,112},{16,32,80,96},{144,160,208,224},{128,176,192,240},{256,30..., dimensions={0} | all-to-all | bytes 262144 | tf_op jit(solution)/shard_map/all_to_all | solution.py:175
  83.5 17.2 %all-gather = bf16[512,128]{1,0:T(8,128)(2,1)S(1)} all-gather(bf16[128,128]{1,0:T(8,128)(2,1)S(1)} %total.1), channel_id=2, replica_groups={{0,144,256,400},{16,128,272,384},{48,160,304,416},{32,176,288,432},{64,..., dimensions={0}, use_global_device_ids=true | all-gather | bytes 163840 | tf_op jit(solution)/shard_map/all_gather | solution.py:177
  100.7 9.4 %all_to_all.21.before_ref = bf16[4,128,128]{2,1,0:T(8,128)(2,1)S(1)} all-to-all(bf16[4,128,128]{2,1,0:T(8,128)(2,1)S(1)} %parts.1), channel_id=1, replica_groups={{0,48,64,112},{16,32,80,96},{144,160,208,224},{128,176,192,240},{256,30..., dimensions={0} | all-to-all | bytes 262144 | tf_op jit(solution)/shard_map/all_to_all | solution.py:179
  110.1 0.0 copy-done.1
  110.1 0.4 final.1
  110.5 10.7 %all_to_all.22.i_ref = bf16[8,128,128]{2,1,0:T(8,128)(2,1)S(1)} all-to-all(bf16[8,128,128]{2,1,0:T(8,128)(2,1)S(1)} %bitcast.9), channel_id=1, replica_groups={{0,16,1,17,2,18,3,19},{48,32,49,33,50,34,51,35},{64,80,65,81,66,82,67,8..., dimensions={0} | all-to-all | bytes 524288 | tf_op jit(solution)/shard_map/all_to_all | solution.py:184
  121.2 0.8 join.1
  (6 shorter events, 0.2 us)
Async XLA Ops:
  0.0 0.9 copy-start
  1.0 11.7 %collective-permute-start = (f16[96,384]{1,0:T(8,128)(2,1)S(1)}, f16[96,384]{1,0:T(8,128)(2,1)S(1)}, u32[]{:S(2)}, u32[]{:S(2)}) collective-permute-start(f16[96,384]{1,0:T(8,128)(2,1)S(1)} %multiply_convert_fusion.2), channel_id=1, source_target_pairs={{0,16},{16,0},{32,48},{48,32},{64,80},{80,64},{96,112},{112,96},{1... | collective-permute-start | bytes 221192 | tf_op jit(solution)/shard_map/ppermute | solution.py:154
  12.6 52.1 %all-to-all-start = ((bf16[4,128,3072]{2,1,0:T(8,128)(2,1)}), bf16[4,128,3072]{2,1,0:T(8,128)(2,1)}, u32[]{:S(2)}, u32[]{:S(2)}) async-start(bf16[4,128,3072]{2,1,0:T(8,128)(2,1)} %copies.1), calls=%async_computation | async-start | bytes 6291456 | tf_op jit(solution)/shard_map/all_to_all | solution.py:160
  64.8 8.4 %collective-permute-start.1 = (bf16[4,128,3072]{2,1,0:T(8,128)(2,1)}, bf16[4,128,3072]{2,1,0:T(8,128)(2,1)S(1)}, u32[]{:S(2)}, u32[]{:S(2)}) collective-permute-start(bf16[4,128,3072]{2,1,0:T(8,128)(2,1)} %all-to-all-done), channel_id=1, source_target_pairs={{0,16},{16,0},{32,48},{48,32},{64,80},{80,64},{96,112},{112,96},{1... | collective-permute-start | bytes 9437192 | tf_op jit(solution)/shard_map/ppermute | solution.py:166
  73.2 36.9 %copy-start.1 = (f32[256]{0:T(256)S(1)}, f32[256]{0:T(256)}, u32[]{:S(2)}) copy-start(f32[256]{0:T(256)} %param.5) | copy-start | bytes 3076

commit v8 on v7

--- a/solution.py
+++ b/solution.py
@@ -161,9 +161,9 @@
     first = core == 0
     pair = jnp.concatenate([jnp.where(first, keep, got), jnp.where(first, got, keep)], axis=0)
     full = lax.all_gather(pair, "seq", axis=0, tiled=True, axis_index_groups=SAME_HEAD)
+    mine_t, full = lax.optimization_barrier((mine_t, full))
+    other_t = lax.ppermute(mine_t, "seq", SIBLING)
     weights = (full.astype(F32) * (1.0 / WSCALE)).astype(B16)
-    mine_t, weights = lax.optimization_barrier((mine_t, weights))
-    other_t = lax.ppermute(mine_t, "seq", SIBLING)
     n = SEQS * BLOCK
     ta, tb = mine_t.reshape(n, -1), other_t.reshape(n, -1)
     outs = [((n, DH), B16), ((n, DH), F32), ((SEQS, DH, DH), F32)]

time: 122 us -> 122 us (level)
  Pallas kernels: 10.3 us -> 8.37 us
  blocking collectives: 92.1 us -> 93.8 us
  other arithmetic: 0.71 us -> 2.31 us
    pallas_call x8, Pallas kernels: 10.3 us -> 8.37 us  [call(): pl.pallas_call(kernel, name=name, out_shape=[jax.ShapeDtypeStruct(s, d) f...]
    convert_element_type x1, other arithmetic: 0.6 us -> 2.2 us  [body(): weights = (full.astype(F32) * (1.0 / WSCALE)).astype(B16)]
    all_gather x1, blocking collectives: 46.8 us -> 48.2 us  [body(): lax.all_gather(pair, 'seq', axis=0, tiled=True, axis_index_groups=SAME_HEAD)]
    all_to_all x1, blocking collectives: 10.7 us -> 12 us  [body(): lax.all_to_all(out.reshape(8, BLOCK, DH), ('seq', 'dp'), 0, 0, tiled=True...]
  transfers between devices with their start and end apart: 3 -> 3, of which waited for: 1 -> 1; matrix products, arithmetic and copies ran while one was open for 1% -> 2% of each run, Pallas kernels for 6% -> 4%
where the time goes in v8:
time: 122 us
  blocking collectives  93.8 us (77%)
  starting transfers between devices  15.7 us (13%)
  Pallas kernels  8.37 us (7%)
  other arithmetic  2.31 us (2%)
    all_gather x1, blocking collectives, body(): lax.all_gather(pair, 'seq', axis=0, tiled=True, axis_index_groups=SAME_HEAD)  48.2 us
    all_gather x1, blocking collectives, body(): totals = lax.all_gather(total, 'seq', axis=0, axis_index_groups=ACROSS)  16.8 us
    all_to_all x1, blocking collectives, body(): lax.all_to_all(out.reshape(8, BLOCK, DH), ('seq', 'dp'), 0, 0, tiled=True...  12 us
    ppermute x1, starting transfers between devices, body(): got = lax.ppermute(to_half(give), 'seq', SIBLING)  8.79 us
    all_to_all x1, blocking collectives, body(): lax.all_to_all(parts, 'seq', 0, 0, tiled=True, axis_index_groups=QUAD)  8.7 us
    pallas_call x8, Pallas kernels, call(): pl.pallas_call(kernel, name=name, out_shape=[jax.ShapeDtypeStruct(s, d) f...  8.37 us
    all_to_all x1, blocking collectives, body(): lax.all_to_all(chip, 'seq', 0, 0, tiled=True, axis_index_groups=QUAD)  8.08 us
    all_to_all x1, starting transfers between devices, body(): mine_t = lax.all_to_all(copies, 'dp', 0, 0, tiled=True)  3.71 us
  transfers between devices with their start and end apart: 3, of which 1 were waited for; matrix products, arithmetic and copies ran while one was open for 2% of the time, Pallas kernels for 4%

profile of v8, /device:TPU:1, one launch (start us, length us, event | category | flops | bytes accessed | tf_op | source)
XLA Modules:
  0.0 122.0 jit_solution(12467075170051401182)
XLA Ops:
  0.0 0.0 copy-start
  0.0 0.9 copy-done
  1.0 8.8 %collective-permute-start = (f16[96,384]{1,0:T(8,128)(2,1)S(1)}, f16[96,384]{1,0:T(8,128)(2,1)S(1)}, u32[]{:S(2)}, u32[]{:S(2)}) collective-permute-start(f16[96,384]{1,0:T(8,128)(2,1)S(1)} %multiply_convert_fusion.2), channel_id=1, source_target_pairs={{0,16},{16,0},{32,48},{48,32},{64,80},{80,64},{96,112},{112,96},{1... | collective-permute-start | bytes 221192 | tf_op jit(solution)/shard_map/ppermute | solution.py:154
  9.8 2.8 %copies.1 = bf16[4,128,3072]{2,1,0:T(8,128)(2,1)} custom-call(bf16[128,3072]{1,0:T(8,128)(2,1)} %bitcast.13), custom_call_target="tpu_custom_call" | custom-call | tf_op jit(solution)/shard_map/copies/pallas_call | solution.py:136
  12.6 0.0 collective-permute-done
  12.6 3.7 %all-to-all-start = ((bf16[4,128,3072]{2,1,0:T(8,128)(2,1)}), bf16[4,128,3072]{2,1,0:T(8,128)(2,1)S(1)}, u32[]{:S(2)}, u32[]{:S(2)}) async-start(bf16[4,128,3072]{2,1,0:T(8,128)(2,1)} %copies.1), calls=%async_computation | async-start | bytes 6291456 | tf_op jit(solution)/shard_map/all_to_all | solution.py:160
  16.4 48.2 %all-gather.2 = f16[3072,384]{1,0:T(8,128)(2,1)} all-gather(f16[192,384]{1,0:T(8,128)(2,1)S(1)} %pad_maximum_fusion), channel_id=1, replica_groups={{0,48,64,112,144,160,208,224,256,304,320,368,400,416,464,480},{16,32,80..., dimensions={0}, use_global_device_ids=true | all-gather | bytes 2506752 | tf_op jit(solution)/shard_map/all_gather | solution.py:163
  64.6 0.0 all-to-all-done
  64.6 3.2 %collective-permute-start.1 = (bf16[4,128,3072]{2,1,0:T(8,128)(2,1)S(1)}, bf16[4,128,3072]{2,1,0:T(8,128)(2,1)S(1)}, u32[]{:S(2)}, u32[]{:S(2)}) collective-permute-start(bf16[4,128,3072]{2,1,0:T(8,128)(2,1)S(1)} %all-to-all-done), channel_id=1, source_target_pairs={{0,16},{16,0},{32,48},{48,32},{64,80},{80,64},{96,112},{112,96},{1... | collective-permute-start | bytes 9437192 | tf_op jit(solution)/shard_map/ppermute | solution.py:165
  67.8 2.2 %multiply_convert_fusion.w_ref = bf16[3072,384]{1,0:T(8,128)(2,1)S(1)} fusion(f16[3072,384]{1,0:T(8,128)(2,1)} %all-gather.2), kind=kLoop, calls=%fused_computation | loop fusion | flops 3538944 | bytes 4718592 | tf_op jit(solution)/shard_map/convert_element_type | solution.py:166
  70.0 2.2 %first.1 = (bf16[512,128]{1,0:T(8,128)(2,1)S(1)}, f32[512,128]{1,0:T(8,128)S(1)}, f32[4,128,128]{2,1,0:T(8,128)S(1)}) custom-call(bf16[512,3072]{1,0:T(8,128)(2,1)S(1)} %bitcast.8, bf16[3072,384]{1,0:T(8,128)(2,1)S(1)} %multiply_convert_fusion.w_ref), custom_call_target="tpu_custom_call" | custom-call | tf_op jit(solution)/shard_map/first/pallas_call | solution.py:136
  72.2 0.9 collective-permute-done.1
  73.0 0.0 copy-start.1
  73.1 2.2 %second.1 = (bf16[512,128]{1,0:T(8,128)(2,1)S(1)}, f32[512,128]{1,0:T(8,128)S(1)}, f32[4,128,128]{2,1,0:T(8,128)S(1)}, bf16[4,128,128]{2,1,0:T(8,128)(2,1)S(1)}) custom-call(bf16[512,3072]{1,0:T(8,128)(2,1)S(1)} %bitcast.9, bf16[3072,384]{1,0:T(8,128)(2,1)S(1)} %multiply_convert_fusion.w_ref, f32[4,128,128]{2,1,0:T(8,128)S(1)} %get-tuple-element.45.sa_ref), custom_call_target="tpu_custom_call" | custom-call | tf_op jit(solution)/shard_map/second/pallas_call | solution.py:136
  75.2 8.1 %all_to_all.20.r_ref = bf16[4,128,128]{2,1,0:T(8,128)(2,1)S(1)} all-to-all(bf16[4,128,128]{2,1,0:T(8,128)(2,1)S(1)} %get-tuple-element.44), channel_id=1, replica_groups={{0,48,64,112},{16,32,80,96},{144,160,208,224},{128,176,192,240},{256,30..., dimensions={0} | all-to-all | bytes 262144 | tf_op jit(solution)/shard_map/all_to_all | solution.py:175
  83.3 16.8 %all-gather = bf16[512,128]{1,0:T(8,128)(2,1)S(1)} all-gather(bf16[128,128]{1,0:T(8,128)(2,1)S(1)} %total.1), channel_id=2, replica_groups={{0,144,256,400},{16,128,272,384},{48,160,304,416},{32,176,288,432},{64,..., dimensions={0}, use_global_device_ids=true | all-gather | bytes 163840 | tf_op jit(solution)/shard_map/all_gather | solution.py:177
  100.2 8.7 %all_to_all.21.before_ref = bf16[4,128,128]{2,1,0:T(8,128)(2,1)S(1)} all-to-all(bf16[4,128,128]{2,1,0:T(8,128)(2,1)S(1)} %parts.1), channel_id=1, replica_groups={{0,48,64,112},{16,32,80,96},{144,160,208,224},{128,176,192,240},{256,30..., dimensions={0} | all-to-all | bytes 262144 | tf_op jit(solution)/shard_map/all_to_all | solution.py:179
  108.9 0.0 copy-done.1
  108.9 0.4 final.1
  109.3 12.0 %all_to_all.22.i_ref = bf16[8,128,128]{2,1,0:T(8,128)(2,1)S(1)} all-to-all(bf16[8,128,128]{2,1,0:T(8,128)(2,1)S(1)} %bitcast.10), channel_id=1, replica_groups={{0,16,1,17,2,18,3,19},{48,32,49,33,50,34,51,35},{64,80,65,81,66,82,67,8..., dimensions={0} | all-to-all | bytes 524288 | tf_op jit(solution)/shard_map/all_to_all | solution.py:184
  121.3 0.8 join.1
  (6 shorter events, 0.2 us)
Async XLA Ops:
  0.0 0.9 copy-start
  1.0 11.6 %collective-permute-start = (f16[96,384]{1,0:T(8,128)(2,1)S(1)}, f16[96,384]{1,0:T(8,128)(2,1)S(1)}, u32[]{:S(2)}, u32[]{:S(2)}) collective-permute-start(f16[96,384]{1,0:T(8,128)(2,1)S(1)} %multiply_convert_fusion.2), channel_id=1, source_target_pairs={{0,16},{16,0},{32,48},{48,32},{64,80},{80,64},{96,112},{112,96},{1... | collective-permute-start | bytes 221192 | tf_op jit(solution)/shard_map/ppermute | solution.py:154
  12.6 52.0 %all-to-all-start = ((bf16[4,128,3072]{2,1,0:T(8,128)(2,1)}), bf16[4,128,3072]{2,1,0:T(8,128)(2,1)S(1)}, u32[]{:S(2)}, u32[]{:S(2)}) async-start(bf16[4,128,3072]{2,1,0:T(8,128)(2,1)} %copies.1), calls=%async_computation | async-start | bytes 6291456 | tf_op jit(solution)/shard_map/all_to_all | solution.py:160
  64.6 8.4 %collective-permute-start.1 = (bf16[4,128,3072]{2,1,0:T(8,128)(2,1)S(1)}, bf16[4,128,3072]{2,1,0:T(8,128)(2,1)S(1)}, u32[]{:S(2)}, u32[]{:S(2)}) collective-permute-start(bf16[4,128,3072]{2,1,0:T(8,128)(2,1)S(1)} %all-to-all-done), channel_id=1, source_target_pairs={{0,16},{16,0},{32,48},{48,32},{64,80},{80,64},{96,112},{112,96},{1... | collective-permute-start | bytes 9437192 | tf_op jit(solution)/shard_map/ppermute | solution.py:165
  73.0 35.8 %copy-start.1 = (f32[256]{0:T(256)S(1)}, f32[256]{0:T(256)}, u32[]{:S(2)}) copy-start(f32[256]{0:T(256)} %param.5) | copy-start | bytes 3076

commit v9 on v7

--- a/solution.py
+++ b/solution.py
@@ -25,7 +25,7 @@
 
 
 SAME_HEAD = [[holder(z, h) for z in range(16)] for h in range(2)]
-ACROSS = [[holder(4 * a + b, h) for a in range(4)] for b in range(4) for h in range(2)]
+FORWARD = [[(holder(z, h), holder(z + d, h)) for z in range(16 - d) for h in range(2)] for d in (4, 8, 12)]
 OWNERS = [[holder(z, h) * 4 + y for y in range(4) for h in range(2)] for z in range(16)]
 VMEM = pl.BlockSpec(memory_space=pltpu.VMEM)
 SMEM = pl.BlockSpec(memory_space=pltpu.SMEM)
@@ -63,10 +63,24 @@
     block_work(jnp.dot(t_ref[...], w_ref[...], preferred_element_type=F32), q_ref, l_ref, s_ref)
 
 
-def second_kernel(t_ref, w_ref, sa_ref, q_ref, l_ref, s_ref, chip_ref):
-    block_work(jnp.dot(t_ref[...], w_ref[...], preferred_element_type=F32), q_ref, l_ref, s_ref)
-    for s in range(SEQS):
-        chip_ref[s] = (sa_ref[s] + s_ref[s]).astype(B16)
+def second_kernel(t_ref, w_ref, sa_ref, k_ref, v_ref, s_ref, chip_ref):
+    kv = jnp.dot(t_ref[...], w_ref[:, DH:], preferred_element_type=F32)
+    k, v = silu_b(kv[:, :DH]), kv[:, DH:].astype(B16)
+    k_ref[...] = k
+    v_ref[...] = v
+    for s in range(SEQS):
+        r = rows(s)
+        state = outer(k[r], v[r])
+        s_ref[s] = state
+        chip_ref[s] = (sa_ref[s] + state).astype(B16)
+
+
+def late_kernel(t_ref, w_ref, k_ref, v_ref, q_ref, l_ref):
+    q = silu_b(jnp.dot(t_ref[...], w_ref[:, :DH], preferred_element_type=F32))
+    q_ref[...] = q
+    for s in range(SEQS):
+        r = rows(s)
+        l_ref[r] = local(q[r], k_ref[r], v_ref[r])
 
 
 def heads_kernel(spot_ref, w_ref, keep_ref, give_ref):
@@ -85,11 +99,8 @@
     o_ref[...] = (r_ref[0].astype(F32) + r_ref[1].astype(F32) + r_ref[2].astype(F32) + r_ref[3].astype(F32)).astype(B16)
 
 
-def parts_kernel(spot_ref, r_ref, totals_ref, o_ref):
-    quad = spot_ref[0] >> 3
-    before = jnp.zeros((DH, DH), F32)
-    for a in range(3):
-        before = before + jnp.where(a < quad, totals_ref[a].astype(F32), 0.0)
+def parts_kernel(r_ref, one_ref, two_ref, three_ref, o_ref):
+    before = one_ref[...].astype(F32) + two_ref[...].astype(F32) + three_ref[...].astype(F32)
     o_ref[0] = before.astype(B16)
     for j in range(3):
         before = before + r_ref[j].astype(F32)
@@ -168,14 +179,18 @@
     ta, tb = mine_t.reshape(n, -1), other_t.reshape(n, -1)
     outs = [((n, DH), B16), ((n, DH), F32), ((SEQS, DH, DH), F32)]
     qa, la, sa = call(first_kernel, "first", outs, ta, weights)
-    qb, lb, sb, chip = call(second_kernel, "second", outs + [((SEQS, DH, DH), B16)], tb, weights, sa)
-    chip, qa, la, sa, qb, lb, sb, spot = lax.optimization_barrier((chip, qa, la, sa, qb, lb, sb, spot))
-
     square = (DH, DH)
+    kb, vb, sb, chip = call(
+        second_kernel, "second", [((n, DH), B16), ((n, DH), B16), ((SEQS, DH, DH), F32), ((SEQS, DH, DH), B16)], tb, weights, sa
+    )
+    chip, qa, la, sa, kb, vb, sb, tb, weights, spot = lax.optimization_barrier((chip, qa, la, sa, kb, vb, sb, tb, weights, spot))
     by_chip = lax.all_to_all(chip, "seq", 0, 0, tiled=True, axis_index_groups=QUAD)
+    by_chip, tb = lax.optimization_barrier((by_chip, tb))
     (total,) = call(total_kernel, "total", [(square, B16)], by_chip)
-    totals = lax.all_gather(total, "seq", axis=0, axis_index_groups=ACROSS)
-    (parts,) = call(parts_kernel, "parts", [((4,) + square, B16)], spot, by_chip, totals)
+    earlier = [lax.ppermute(total, "seq", route) for route in FORWARD]
+    qb, lb = call(late_kernel, "late", [((n, DH), B16), ((n, DH), F32)], tb, weights, kb, vb)
+    earlier, qb, lb = lax.optimization_barrier((earlier, qb, lb))
+    (parts,) = call(parts_kernel, "parts", [((4,) + square, B16)], by_chip, *earlier)
     back = lax.all_to_all(parts, "seq", 0, 0, tiled=True, axis_index_groups=QUAD)
     (out,) = call(
         final_kernel, "final", [((SEQS, 2, BLOCK, DH), B16)],

time: 122 us -> 122 us (level)
  blocking collectives: 92.1 us -> 74.8 us
  starting transfers between devices: 16.4 us -> 29.5 us
  waiting for transfers between devices: 1.42 us -> 4.4 us
    all_gather x1 -> x0, blocking collectives: 17.2 us -> none  [body(): totals = lax.all_gather(total, 'seq', axis=0, axis_index_groups=ACROSS)]
    ppermute x0 -> x3, starting transfers between devices: none -> 13.1 us  [body(): earlier = [lax.ppermute(total, 'seq', route) for route in FORWARD]]
    ppermute x0 -> x3, waiting for transfers between devices: none -> 2.98 us  [body(): earlier = [lax.ppermute(total, 'seq', route) for route in FORWARD]]
    pallas_call x8 -> x9, Pallas kernels: 10.3 us -> 11 us  [call(): pl.pallas_call(kernel, name=name, out_shape=[jax.ShapeDtypeStruct(s, d) f...]
  transfers between devices with their start and end apart: 3 -> 6, of which waited for: 1 -> 2; matrix products, arithmetic and copies ran while one was open for 1% -> 1% of each run, Pallas kernels for 6% -> 7%
where the time goes in v9:
time: 122 us; the launch traced here: 121 us
  blocking collectives  74.8 us (61%)
  starting transfers between devices  29.5 us (24%)
  Pallas kernels  11 us (9%)
  waiting for transfers between devices  4.4 us (4%)
    all_gather x1, blocking collectives, body(): lax.all_gather(pair, 'seq', axis=0, tiled=True, axis_index_groups=SAME_HEAD)  46.8 us
    ppermute x3, starting transfers between devices, body(): earlier = [lax.ppermute(total, 'seq', route) for route in FORWARD]  13.1 us
    all_to_all x1, blocking collectives, body(): lax.all_to_all(out.reshape(8, BLOCK, DH), ('seq', 'dp'), 0, 0, tiled=True...  11.8 us
    pallas_call x9, Pallas kernels, call(): pl.pallas_call(kernel, name=name, out_shape=[jax.ShapeDtypeStruct(s, d) f...  11 us
    ppermute x1, starting transfers between devices, body(): got = lax.ppermute(to_half(give), 'seq', SIBLING)  8.79 us
    all_to_all x1, blocking collectives, body(): lax.all_to_all(parts, 'seq', 0, 0, tiled=True, axis_index_groups=QUAD)  8.17 us
    all_to_all x1, blocking collectives, body(): lax.all_to_all(chip, 'seq', 0, 0, tiled=True, axis_index_groups=QUAD)  8.09 us
    all_to_all x1, starting transfers between devices, body(): mine_t = lax.all_to_all(copies, 'dp', 0, 0, tiled=True)  4.67 us
  transfers between devices with their start and end apart: 6, of which 2 were waited for; matrix products, arithmetic and copies ran while one was open for 1% of the time, Pallas kernels for 7%

profile of v9, /device:TPU:1, one launch (start us, length us, event | category | flops | bytes accessed | tf_op | source)
XLA Modules:
  0.0 121.5 jit_solution(8749373350081735419)
XLA Ops:
  0.0 0.0 copy-start
  0.0 0.9 copy-done
  1.0 8.8 %collective-permute-start = (f16[96,384]{1,0:T(8,128)(2,1)S(1)}, f16[96,384]{1,0:T(8,128)(2,1)S(1)}, u32[]{:S(2)}, u32[]{:S(2)}) collective-permute-start(f16[96,384]{1,0:T(8,128)(2,1)S(1)} %multiply_convert_fusion.2), channel_id=1, source_target_pairs={{0,16},{16,0},{32,48},{48,32},{64,80},{80,64},{96,112},{112,96},{1... | collective-permute-start | bytes 221192 | tf_op jit(solution)/shard_map/ppermute | solution.py:165
  9.8 2.8 %copies.1 = bf16[4,128,3072]{2,1,0:T(8,128)(2,1)} custom-call(bf16[128,3072]{1,0:T(8,128)(2,1)} %bitcast.11), custom_call_target="tpu_custom_call" | custom-call | tf_op jit(solution)/shard_map/copies/pallas_call | solution.py:147
  12.6 0.0 collective-permute-done
  12.6 4.7 %all-to-all-start = ((bf16[4,128,3072]{2,1,0:T(8,128)(2,1)}), bf16[4,128,3072]{2,1,0:T(8,128)(2,1)}, u32[]{:S(2)}, u32[]{:S(2)}) async-start(bf16[4,128,3072]{2,1,0:T(8,128)(2,1)} %copies.1), calls=%async_computation | async-start | bytes 6291456 | tf_op jit(solution)/shard_map/all_to_all | solution.py:171
  17.4 46.8 %all-gather.1 = f16[3072,384]{1,0:T(8,128)(2,1)S(1)} all-gather(f16[192,384]{1,0:T(8,128)(2,1)S(1)} %pad_maximum_fusion), channel_id=1, replica_groups={{0,48,64,112,144,160,208,224,256,304,320,368,400,416,464,480},{16,32,80..., dimensions={0}, use_global_device_ids=true | all-gather | bytes 2506752 | tf_op jit(solution)/shard_map/all_gather | solution.py:174
  64.2 0.6 multiply_convert_fusion.w_ref
  64.8 0.0 all-to-all-done
  64.8 2.9 %collective-permute-start.1 = (bf16[4,128,3072]{2,1,0:T(8,128)(2,1)}, bf16[4,128,3072]{2,1,0:T(8,128)(2,1)S(1)}, u32[]{:S(2)}, u32[]{:S(2)}) collective-permute-start(bf16[4,128,3072]{2,1,0:T(8,128)(2,1)} %all-to-all-done), channel_id=1, source_target_pairs={{0,16},{16,0},{32,48},{48,32},{64,80},{80,64},{96,112},{112,96},{1... | collective-permute-start | bytes 9437192 | tf_op jit(solution)/shard_map/ppermute | solution.py:177
  67.7 4.1 %first.1 = (bf16[512,128]{1,0:T(8,128)(2,1)S(1)}, f32[512,128]{1,0:T(8,128)S(1)}, f32[4,128,128]{2,1,0:T(8,128)S(1)}) custom-call(bf16[512,3072]{1,0:T(8,128)(2,1)} %bitcast.3.t_ref, bf16[3072,384]{1,0:T(8,128)(2,1)S(1)} %multiply_convert_fusion.w_ref), custom_call_target="tpu_custom_call" | custom-call | tf_op jit(solution)/shard_map/first/pallas_call | solution.py:147
  71.8 1.4 %collective-permute-done.1 = bf16[4,128,3072]{2,1,0:T(8,128)(2,1)S(1)} collective-permute-done((bf16[4,128,3072]{2,1,0:T(8,128)(2,1)}, bf16[4,128,3072]{2,1,0:T(8,128)(2,1)S(1)}, u32[]{:S(2)}, u32[]{:S(2)}) %collective-permute-start.1) | collective-permute-done | bytes 3145760 | tf_op jit(solution)/shard_map/ppermute | solution.py:177
  73.2 1.2 second.1
  74.4 8.1 %all_to_all.20.r_ref = bf16[4,128,128]{2,1,0:T(8,128)(2,1)S(1)} all-to-all(bf16[4,128,128]{2,1,0:T(8,128)(2,1)S(1)} %get-tuple-element.52), channel_id=1, replica_groups={{0,48,64,112},{16,32,80,96},{144,160,208,224},{128,176,192,240},{256,30..., dimensions={0} | all-to-all | bytes 262144 | tf_op jit(solution)/shard_map/all_to_all | solution.py:187
  82.5 0.0 copy-start.1
  82.5 4.9 %collective-permute-start.2 = (bf16[128,128]{1,0:T(8,128)(2,1)S(1)}, bf16[128,128]{1,0:T(8,128)(2,1)S(1)}, u32[]{:S(2)}, u32[]{:S(2)}) collective-permute-start(bf16[128,128]{1,0:T(8,128)(2,1)S(1)} %total.1), channel_id=1, source_target_pairs={{0,144},{16,128},{48,160},{32,176},{64,208},{80,192},{112,224},{96... | collective-permute-start | bytes 98312 | tf_op jit(solution)/shard_map/ppermute | solution.py:190
  87.4 6.9 %collective-permute-start.3 = (bf16[128,128]{1,0:T(8,128)(2,1)S(1)}, bf16[128,128]{1,0:T(8,128)(2,1)S(1)}, u32[]{:S(2)}, u32[]{:S(2)}) collective-permute-start(bf16[128,128]{1,0:T(8,128)(2,1)S(1)} %total.1), channel_id=1, source_target_pairs={{0,256},{16,272},{48,304},{32,288},{64,320},{80,336},{112,368},{96... | collective-permute-start | bytes 98312 | tf_op jit(solution)/shard_map/ppermute | solution.py:190
  94.4 1.3 %collective-permute-start.4 = (bf16[128,128]{1,0:T(8,128)(2,1)S(1)}, bf16[128,128]{1,0:T(8,128)(2,1)S(1)}, u32[]{:S(2)}, u32[]{:S(2)}) collective-permute-start(bf16[128,128]{1,0:T(8,128)(2,1)S(1)} %total.1), channel_id=1, source_target_pairs={{0,400},{16,384},{48,416},{32,432},{64,464},{80,448},{112,480},{96... | collective-permute-start | bytes 98312 | tf_op jit(solution)/shard_map/ppermute | solution.py:190
  95.7 1.6 %late.1 = (bf16[512,128]{1,0:T(8,128)(2,1)S(1)}, f32[512,128]{1,0:T(8,128)S(1)}) custom-call(bf16[512,3072]{1,0:T(8,128)(2,1)S(1)} %bitcast.8, bf16[3072,384]{1,0:T(8,128)(2,1)S(1)} %multiply_convert_fusion.w_ref, bf16[512,128]{1,0:T(8,128)(2,1)S(1)} %get-tuple-element.57.k_ref, bf16[512,128]{1,0:T(8,128)(2,1)S(1)} %get-tuple-element.58.v_ref), custom_call_target="tpu_custom_call" | custom-call | tf_op jit(solution)/shard_map/late/pallas_call | solution.py:147
  97.3 0.0 collective-permute-done.2.one_ref
  97.3 0.0 collective-permute-done.3.two_ref
  97.3 3.0 %collective-permute-done.4.three_ref = bf16[128,128]{1,0:T(8,128)(2,1)S(1)} collective-permute-done((bf16[128,128]{1,0:T(8,128)(2,1)S(1)}, bf16[128,128]{1,0:T(8,128)(2,1)S(1)}, u32[]{:S(2)}, u32[]{:S(2)}) %collective-permute-start.4) | collective-permute-done | bytes 32800 | tf_op jit(solution)/shard_map/ppermute | solution.py:190
  100.3 8.2 %all_to_all.21.before_ref = bf16[4,128,128]{2,1,0:T(8,128)(2,1)S(1)} all-to-all(bf16[4,128,128]{2,1,0:T(8,128)(2,1)S(1)} %parts.1), channel_id=1, replica_groups={{0,48,64,112},{16,32,80,96},{144,160,208,224},{128,176,192,240},{256,30..., dimensions={0} | all-to-all | bytes 262144 | tf_op jit(solution)/shard_map/all_to_all | solution.py:194
  108.5 0.0 copy-done.1
  108.5 0.4 final.1
  108.9 11.8 %all_to_all.22.i_ref = bf16[8,128,128]{2,1,0:T(8,128)(2,1)S(1)} all-to-all(bf16[8,128,128]{2,1,0:T(8,128)(2,1)S(1)} %bitcast.9), channel_id=1, replica_groups={{0,16,1,17,2,18,3,19},{48,32,49,33,50,34,51,35},{64,80,65,81,66,82,67,8..., dimensions={0} | all-to-all | bytes 524288 | tf_op jit(solution)/shard_map/all_to_all | solution.py:199
  120.7 0.8 join.1
  (6 shorter events, 0.2 us)
Async XLA Ops:
  0.0 0.9 copy-start
  1.0 11.6 %collective-permute-start = (f16[96,384]{1,0:T(8,128)(2,1)S(1)}, f16[96,384]{1,0:T(8,128)(2,1)S(1)}, u32[]{:S(2)}, u32[]{:S(2)}) collective-permute-start(f16[96,384]{1,0:T(8,128)(2,1)S(1)} %multiply_convert_fusion.2), channel_id=1, source_target_pairs={{0,16},{16,0},{32,48},{48,32},{64,80},{80,64},{96,112},{112,96},{1... | collective-permute-start | bytes 221192 | tf_op jit(solution)/shard_map/ppermute | solution.py:165
  12.6 52.2 %all-to-all-start = ((bf16[4,128,3072]{2,1,0:T(8,128)(2,1)}), bf16[4,128,3072]{2,1,0:T(8,128)(2,1)}, u32[]{:S(2)}, u32[]{:S(2)}) async-start(bf16[4,128,3072]{2,1,0:T(8,128)(2,1)} %copies.1), calls=%async_computation | async-start | bytes 6291456 | tf_op jit(solution)/shard_map/all_to_all | solution.py:171
  64.8 8.4 %collective-permute-start.1 = (bf16[4,128,3072]{2,1,0:T(8,128)(2,1)}, bf16[4,128,3072]{2,1,0:T(8,128)(2,1)S(1)}, u32[]{:S(2)}, u32[]{:S(2)}) collective-permute-start(bf16[4,128,3072]{2,1,0:T(8,128)(2,1)} %all-to-all-done), channel_id=1, source_target_pairs={{0,16},{16,0},{32,48},{48,32},{64,80},{80,64},{96,112},{112,96},{1... | collective-permute-start | bytes 9437192 | tf_op jit(solution)/shard_map/ppermute | solution.py:177
  82.5 26.0 %copy-start.1 = (f32[256]{0:T(256)S(1)}, f32[256]{0:T(256)}, u32[]{:S(2)}) copy-start(f32[256]{0:T(256)} %param.5) | copy-start | bytes 3076
  82.5 14.8 %collective-permute-start.2 = (bf16[128,128]{1,0:T(8,128)(2,1)S(1)}, bf16[128,128]{1,0:T(8,128)(2,1)S(1)}, u32[]{:S(2)}, u32[]{:S(2)}) collective-permute-start(bf16[128,128]{1,0:T(8,128)(2,1)S(1)} %total.1), channel_id=1, source_target_pairs={{0,144},{16,128},{48,160},{32,176},{64,208},{80,192},{112,224},{96... | collective-permute-start | bytes 98312 | tf_op jit(solution)/shard_map/ppermute | solution.py:190
  87.4 9.9 %collective-permute-start.3 = (bf16[128,128]{1,0:T(8,128)(2,1)S(1)}, bf16[128,128]{1,0:T(8,128)(2,1)S(1)}, u32[]{:S(2)}, u32[]{:S(2)}) collective-permute-start(bf16[128,128]{1,0:T(8,128)(2,1)S(1)} %total.1), channel_id=1, source_target_pairs={{0,256},{16,272},{48,304},{32,288},{64,320},{80,336},{112,368},{96... | collective-permute-start | bytes 98312 | tf_op jit(solution)/shard_map/ppermute | solution.py:190
  94.4 5.9 %collective-permute-start.4 = (bf16[128,128]{1,0:T(8,128)(2,1)S(1)}, bf16[128,128]{1,0:T(8,128)(2,1)S(1)}, u32[]{:S(2)}, u32[]{:S(2)}) collective-permute-start(bf16[128,128]{1,0:T(8,128)(2,1)S(1)} %total.1), channel_id=1, source_target_pairs={{0,400},{16,384},{48,416},{32,432},{64,464},{80,448},{112,480},{96... | collective-permute-start | bytes 98312 | tf_op jit(solution)/shard_map/ppermute | solution.py:190

commit v10 on v9

--- a/solution.py
+++ b/solution.py
@@ -25,7 +25,7 @@
 
 
 SAME_HEAD = [[holder(z, h) for z in range(16)] for h in range(2)]
-FORWARD = [[(holder(z, h), holder(z + d, h)) for z in range(16 - d) for h in range(2)] for d in (4, 8, 12)]
+FORWARD = [[(holder(z, h), holder(z + d, h)) for z in range(16 - d) for h in range(2)] for d in (8, 12, 4)]
 OWNERS = [[holder(z, h) * 4 + y for y in range(4) for h in range(2)] for z in range(16)]
 VMEM = pl.BlockSpec(memory_space=pltpu.VMEM)
 SMEM = pl.BlockSpec(memory_space=pltpu.SMEM)

time: 122 us -> 119 us (0.975)
  waiting for transfers between devices: 4.4 us -> 1.43 us
    ppermute x3, waiting for transfers between devices: 2.98 us -> 0.01 us  [body(): earlier = [lax.ppermute(total, 'seq', route) for route in FORWARD]]
  transfers between devices with their start and end apart: 6 -> 6, of which waited for: 2 -> 1; matrix products, arithmetic and copies ran while one was open for 1% -> 1% of each run, Pallas kernels for 7% -> 7%
where the time goes in v10:
time: 119 us
  blocking collectives  75.2 us (63%)
  starting transfers between devices  29.1 us (24%)
  Pallas kernels  11 us (9%)
  waiting for transfers between devices  1.43 us (1%)
    all_gather x1, blocking collectives, body(): lax.all_gather(pair, 'seq', axis=0, tiled=True, axis_index_groups=SAME_HEAD)  46.8 us
    ppermute x3, starting transfers between devices, body(): earlier = [lax.ppermute(total, 'seq', route) for route in FORWARD]  12.8 us
    all_to_all x1, blocking collectives, body(): lax.all_to_all(out.reshape(8, BLOCK, DH), ('seq', 'dp'), 0, 0, tiled=True...  11.8 us
    pallas_call x9, Pallas kernels, call(): pl.pallas_call(kernel, name=name, out_shape=[jax.ShapeDtypeStruct(s, d) f...  11 us
    ppermute x1, starting transfers between devices, body(): got = lax.ppermute(to_half(give), 'seq', SIBLING)  8.79 us
    all_to_all x1, blocking collectives, body(): lax.all_to_all(parts, 'seq', 0, 0, tiled=True, axis_index_groups=QUAD)  8.55 us
    all_to_all x1, blocking collectives, body(): lax.all_to_all(chip, 'seq', 0, 0, tiled=True, axis_index_groups=QUAD)  8.09 us
    all_to_all x1, starting transfers between devices, body(): mine_t = lax.all_to_all(copies, 'dp', 0, 0, tiled=True)  4.67 us
  transfers between devices with their start and end apart: 6, of which 1 were waited for; matrix products, arithmetic and copies ran while one was open for 1% of the time, Pallas kernels for 7%

profile of v10, /device:TPU:1, one launch (start us, length us, event | category | flops | bytes accessed | tf_op | source)
XLA Modules:
  0.0 118.5 jit_solution(17206585738248680325)
XLA Ops:
  0.0 0.0 copy-start
  0.0 0.9 copy-done
  1.0 8.8 %collective-permute-start = (f16[96,384]{1,0:T(8,128)(2,1)S(1)}, f16[96,384]{1,0:T(8,128)(2,1)S(1)}, u32[]{:S(2)}, u32[]{:S(2)}) collective-permute-start(f16[96,384]{1,0:T(8,128)(2,1)S(1)} %multiply_convert_fusion.2), channel_id=1, source_target_pairs={{0,16},{16,0},{32,48},{48,32},{64,80},{80,64},{96,112},{112,96},{1... | collective-permute-start | bytes 221192 | tf_op jit(solution)/shard_map/ppermute | solution.py:165
  9.8 2.8 %copies.1 = bf16[4,128,3072]{2,1,0:T(8,128)(2,1)} custom-call(bf16[128,3072]{1,0:T(8,128)(2,1)} %bitcast.11), custom_call_target="tpu_custom_call" | custom-call | tf_op jit(solution)/shard_map/copies/pallas_call | solution.py:147
  12.6 0.0 collective-permute-done
  12.6 4.7 %all-to-all-start = ((bf16[4,128,3072]{2,1,0:T(8,128)(2,1)}), bf16[4,128,3072]{2,1,0:T(8,128)(2,1)}, u32[]{:S(2)}, u32[]{:S(2)}) async-start(bf16[4,128,3072]{2,1,0:T(8,128)(2,1)} %copies.1), calls=%async_computation | async-start | bytes 6291456 | tf_op jit(solution)/shard_map/all_to_all | solution.py:171
  17.4 46.8 %all-gather.1 = f16[3072,384]{1,0:T(8,128)(2,1)S(1)} all-gather(f16[192,384]{1,0:T(8,128)(2,1)S(1)} %pad_maximum_fusion), channel_id=1, replica_groups={{0,48,64,112,144,160,208,224,256,304,320,368,400,416,464,480},{16,32,80..., dimensions={0}, use_global_device_ids=true | all-gather | bytes 2506752 | tf_op jit(solution)/shard_map/all_gather | solution.py:174
  64.2 0.6 multiply_convert_fusion.w_ref
  64.8 0.0 all-to-all-done
  64.8 2.9 %collective-permute-start.1 = (bf16[4,128,3072]{2,1,0:T(8,128)(2,1)}, bf16[4,128,3072]{2,1,0:T(8,128)(2,1)S(1)}, u32[]{:S(2)}, u32[]{:S(2)}) collective-permute-start(bf16[4,128,3072]{2,1,0:T(8,128)(2,1)} %all-to-all-done), channel_id=1, source_target_pairs={{0,16},{16,0},{32,48},{48,32},{64,80},{80,64},{96,112},{112,96},{1... | collective-permute-start | bytes 9437192 | tf_op jit(solution)/shard_map/ppermute | solution.py:177
  67.7 4.1 %first.1 = (bf16[512,128]{1,0:T(8,128)(2,1)S(1)}, f32[512,128]{1,0:T(8,128)S(1)}, f32[4,128,128]{2,1,0:T(8,128)S(1)}) custom-call(bf16[512,3072]{1,0:T(8,128)(2,1)} %bitcast.3.t_ref, bf16[3072,384]{1,0:T(8,128)(2,1)S(1)} %multiply_convert_fusion.w_ref), custom_call_target="tpu_custom_call" | custom-call | tf_op jit(solution)/shard_map/first/pallas_call | solution.py:147
  71.8 1.4 %collective-permute-done.1 = bf16[4,128,3072]{2,1,0:T(8,128)(2,1)S(1)} collective-permute-done((bf16[4,128,3072]{2,1,0:T(8,128)(2,1)}, bf16[4,128,3072]{2,1,0:T(8,128)(2,1)S(1)}, u32[]{:S(2)}, u32[]{:S(2)}) %collective-permute-start.1) | collective-permute-done | bytes 3145760 | tf_op jit(solution)/shard_map/ppermute | solution.py:177
  73.2 1.2 %second.1 = (bf16[512,128]{1,0:T(8,128)(2,1)S(1)}, bf16[512,128]{1,0:T(8,128)(2,1)S(1)}, f32[4,128,128]{2,1,0:T(8,128)S(1)}, bf16[4,128,128]{2,1,0:T(8,128)(2,1)S(1)}) custom-call(bf16[512,3072]{1,0:T(8,128)(2,1)S(1)} %bitcast.7, bf16[3072,384]{1,0:T(8,128)(2,1)S(1)} %multiply_convert_fusion.w_ref, f32[4,128,128]{2,1,0:T(8,128)S(1)} %get-tuple-element.67.sa_ref), custom_call_target="tpu_custom_call" | custom-call | tf_op jit(solution)/shard_map/second/pallas_call | solution.py:147
  74.4 8.1 %all_to_all.20.r_ref = bf16[4,128,128]{2,1,0:T(8,128)(2,1)S(1)} all-to-all(bf16[4,128,128]{2,1,0:T(8,128)(2,1)S(1)} %get-tuple-element.52), channel_id=1, replica_groups={{0,48,64,112},{16,32,80,96},{144,160,208,224},{128,176,192,240},{256,30..., dimensions={0} | all-to-all | bytes 262144 | tf_op jit(solution)/shard_map/all_to_all | solution.py:187
  82.5 0.0 copy-start.1
  82.5 7.1 %collective-permute-start.2 = (bf16[128,128]{1,0:T(8,128)(2,1)S(1)}, bf16[128,128]{1,0:T(8,128)(2,1)S(1)}, u32[]{:S(2)}, u32[]{:S(2)}) collective-permute-start(bf16[128,128]{1,0:T(8,128)(2,1)S(1)} %total.1), channel_id=1, source_target_pairs={{0,256},{16,272},{48,304},{32,288},{64,320},{80,336},{112,368},{96... | collective-permute-start | bytes 98312 | tf_op jit(solution)/shard_map/ppermute | solution.py:190
  89.6 1.3 %collective-permute-start.3 = (bf16[128,128]{1,0:T(8,128)(2,1)S(1)}, bf16[128,128]{1,0:T(8,128)(2,1)S(1)}, u32[]{:S(2)}, u32[]{:S(2)}) collective-permute-start(bf16[128,128]{1,0:T(8,128)(2,1)S(1)} %total.1), channel_id=1, source_target_pairs={{0,400},{16,384},{48,416},{32,432},{64,464},{80,448},{112,480},{96... | collective-permute-start | bytes 98312 | tf_op jit(solution)/shard_map/ppermute | solution.py:190
  90.9 4.4 %collective-permute-start.4 = (bf16[128,128]{1,0:T(8,128)(2,1)S(1)}, bf16[128,128]{1,0:T(8,128)(2,1)S(1)}, u32[]{:S(2)}, u32[]{:S(2)}) collective-permute-start(bf16[128,128]{1,0:T(8,128)(2,1)S(1)} %total.1), channel_id=1, source_target_pairs={{0,144},{16,128},{48,160},{32,176},{64,208},{80,192},{112,224},{96... | collective-permute-start | bytes 98312 | tf_op jit(solution)/shard_map/ppermute | solution.py:190
  95.3 1.7 %late.1 = (bf16[512,128]{1,0:T(8,128)(2,1)S(1)}, f32[512,128]{1,0:T(8,128)S(1)}) custom-call(bf16[512,3072]{1,0:T(8,128)(2,1)S(1)} %bitcast.8, bf16[3072,384]{1,0:T(8,128)(2,1)S(1)} %multiply_convert_fusion.w_ref, bf16[512,128]{1,0:T(8,128)(2,1)S(1)} %get-tuple-element.57.k_ref, bf16[512,128]{1,0:T(8,128)(2,1)S(1)} %get-tuple-element.58.v_ref), custom_call_target="tpu_custom_call" | custom-call | tf_op jit(solution)/shard_map/late/pallas_call | solution.py:147
  97.0 0.0 collective-permute-done.2.one_ref
  97.0 0.0 collective-permute-done.3.two_ref
  97.0 0.0 collective-permute-done.4.three_ref
  97.0 8.6 %all_to_all.21.before_ref = bf16[4,128,128]{2,1,0:T(8,128)(2,1)S(1)} all-to-all(bf16[4,128,128]{2,1,0:T(8,128)(2,1)S(1)} %parts.1), channel_id=1, replica_groups={{0,48,64,112},{16,32,80,96},{144,160,208,224},{128,176,192,240},{256,30..., dimensions={0} | all-to-all | bytes 262144 | tf_op jit(solution)/shard_map/all_to_all | solution.py:194
  105.6 0.0 copy-done.1
  105.6 0.4 final.1
  106.0 11.8 %all_to_all.22.i_ref = bf16[8,128,128]{2,1,0:T(8,128)(2,1)S(1)} all-to-all(bf16[8,128,128]{2,1,0:T(8,128)(2,1)S(1)} %bitcast.9), channel_id=1, replica_groups={{0,16,1,17,2,18,3,19},{48,32,49,33,50,34,51,35},{64,80,65,81,66,82,67,8..., dimensions={0} | all-to-all | bytes 524288 | tf_op jit(solution)/shard_map/all_to_all | solution.py:199
  117.8 0.8 join.1
  (6 shorter events, 0.2 us)
Async XLA Ops:
  0.0 0.9 copy-start
  1.0 11.6 %collective-permute-start = (f16[96,384]{1,0:T(8,128)(2,1)S(1)}, f16[96,384]{1,0:T(8,128)(2,1)S(1)}, u32[]{:S(2)}, u32[]{:S(2)}) collective-permute-start(f16[96,384]{1,0:T(8,128)(2,1)S(1)} %multiply_convert_fusion.2), channel_id=1, source_target_pairs={{0,16},{16,0},{32,48},{48,32},{64,80},{80,64},{96,112},{112,96},{1... | collective-permute-start | bytes 221192 | tf_op jit(solution)/shard_map/ppermute | solution.py:165
  12.6 52.2 %all-to-all-start = ((bf16[4,128,3072]{2,1,0:T(8,128)(2,1)}), bf16[4,128,3072]{2,1,0:T(8,128)(2,1)}, u32[]{:S(2)}, u32[]{:S(2)}) async-start(bf16[4,128,3072]{2,1,0:T(8,128)(2,1)} %copies.1), calls=%async_computation | async-start | bytes 6291456 | tf_op jit(solution)/shard_map/all_to_all | solution.py:171
  64.8 8.4 %collective-permute-start.1 = (bf16[4,128,3072]{2,1,0:T(8,128)(2,1)}, bf16[4,128,3072]{2,1,0:T(8,128)(2,1)S(1)}, u32[]{:S(2)}, u32[]{:S(2)}) collective-permute-start(bf16[4,128,3072]{2,1,0:T(8,128)(2,1)} %all-to-all-done), channel_id=1, source_target_pairs={{0,16},{16,0},{32,48},{48,32},{64,80},{80,64},{96,112},{112,96},{1... | collective-permute-start | bytes 9437192 | tf_op jit(solution)/shard_map/ppermute | solution.py:177
  82.5 23.1 %copy-start.1 = (f32[256]{0:T(256)S(1)}, f32[256]{0:T(256)}, u32[]{:S(2)}) copy-start(f32[256]{0:T(256)} %param.5) | copy-start | bytes 3076
  82.5 14.4 %collective-permute-start.2 = (bf16[128,128]{1,0:T(8,128)(2,1)S(1)}, bf16[128,128]{1,0:T(8,128)(2,1)S(1)}, u32[]{:S(2)}, u32[]{:S(2)}) collective-permute-start(bf16[128,128]{1,0:T(8,128)(2,1)S(1)} %total.1), channel_id=1, source_target_pairs={{0,256},{16,272},{48,304},{32,288},{64,320},{80,336},{112,368},{96... | collective-permute-start | bytes 98312 | tf_op jit(solution)/shard_map/ppermute | solution.py:190
  89.6 7.3 %collective-permute-start.3 = (bf16[128,128]{1,0:T(8,128)(2,1)S(1)}, bf16[128,128]{1,0:T(8,128)(2,1)S(1)}, u32[]{:S(2)}, u32[]{:S(2)}) collective-permute-start(bf16[128,128]{1,0:T(8,128)(2,1)S(1)} %total.1), channel_id=1, source_target_pairs={{0,400},{16,384},{48,416},{32,432},{64,464},{80,448},{112,480},{96... | collective-permute-start | bytes 98312 | tf_op jit(solution)/shard_map/ppermute | solution.py:190
  90.9 6.0 %collective-permute-start.4 = (bf16[128,128]{1,0:T(8,128)(2,1)S(1)}, bf16[128,128]{1,0:T(8,128)(2,1)S(1)}, u32[]{:S(2)}, u32[]{:S(2)}) collective-permute-start(bf16[128,128]{1,0:T(8,128)(2,1)S(1)} %total.1), channel_id=1, source_target_pairs={{0,144},{16,128},{48,160},{32,176},{64,208},{80,192},{112,224},{96... | collective-permute-start | bytes 98312 | tf_op jit(solution)/shard_map/ppermute | solution.py:190

commit v11 on v10

--- a/solution.py
+++ b/solution.py
@@ -25,7 +25,7 @@
 
 
 SAME_HEAD = [[holder(z, h) for z in range(16)] for h in range(2)]
-FORWARD = [[(holder(z, h), holder(z + d, h)) for z in range(16 - d) for h in range(2)] for d in (8, 12, 4)]
+FORWARD = [[(holder(z, h), holder(z + d, h)) for z in range(16 - d) for h in range(2)] for d in (12, 8, 4)]
 OWNERS = [[holder(z, h) * 4 + y for y in range(4) for h in range(2)] for z in range(16)]
 VMEM = pl.BlockSpec(memory_space=pltpu.VMEM)
 SMEM = pl.BlockSpec(memory_space=pltpu.SMEM)

time: 119 us -> 120 us (level)
  no operation moved by 1% of the time
where the time goes in v11:
time: 120 us; the launch traced here: 119 us
  blocking collectives  75.2 us (63%)
  starting transfers between devices  29.8 us (25%)
  Pallas kernels  11 us (9%)
  waiting for transfers between devices  1.43 us (1%)
    all_gather x1, blocking collectives, body(): lax.all_gather(pair, 'seq', axis=0, tiled=True, axis_index_groups=SAME_HEAD)  46.8 us
    ppermute x3, starting transfers between devices, body(): earlier = [lax.ppermute(total, 'seq', route) for route in FORWARD]  13.4 us
    all_to_all x1, blocking collectives, body(): lax.all_to_all(out.reshape(8, BLOCK, DH), ('seq', 'dp'), 0, 0, tiled=True...  11.8 us
    pallas_call x9, Pallas kernels, call(): pl.pallas_call(kernel, name=name, out_shape=[jax.ShapeDtypeStruct(s, d) f...  11 us
    ppermute x1, starting transfers between devices, body(): got = lax.ppermute(to_half(give), 'seq', SIBLING)  8.79 us
    all_to_all x1, blocking collectives, body(): lax.all_to_all(parts, 'seq', 0, 0, tiled=True, axis_index_groups=QUAD)  8.55 us
    all_to_all x1, blocking collectives, body(): lax.all_to_all(chip, 'seq', 0, 0, tiled=True, axis_index_groups=QUAD)  8.09 us
    all_to_all x1, starting transfers between devices, body(): mine_t = lax.all_to_all(copies, 'dp', 0, 0, tiled=True)  4.67 us
  transfers between devices with their start and end apart: 6, of which 1 were waited for; matrix products, arithmetic and copies ran while one was open for 1% of the time, Pallas kernels for 7%

profile of v11, /device:TPU:1, one launch (start us, length us, event | category | flops | bytes accessed | tf_op | source)
XLA Modules:
  0.0 119.2 jit_solution(392097428414319041)
XLA Ops:
  0.0 0.0 copy-start
  0.0 0.9 copy-done
  1.0 8.8 %collective-permute-start = (f16[96,384]{1,0:T(8,128)(2,1)S(1)}, f16[96,384]{1,0:T(8,128)(2,1)S(1)}, u32[]{:S(2)}, u32[]{:S(2)}) collective-permute-start(f16[96,384]{1,0:T(8,128)(2,1)S(1)} %multiply_convert_fusion.2), channel_id=1, source_target_pairs={{0,16},{16,0},{32,48},{48,32},{64,80},{80,64},{96,112},{112,96},{1... | collective-permute-start | bytes 221192 | tf_op jit(solution)/shard_map/ppermute | solution.py:165
  9.8 2.8 %copies.1 = bf16[4,128,3072]{2,1,0:T(8,128)(2,1)} custom-call(bf16[128,3072]{1,0:T(8,128)(2,1)} %bitcast.11), custom_call_target="tpu_custom_call" | custom-call | tf_op jit(solution)/shard_map/copies/pallas_call | solution.py:147
  12.6 0.0 collective-permute-done
  12.6 4.7 %all-to-all-start = ((bf16[4,128,3072]{2,1,0:T(8,128)(2,1)}), bf16[4,128,3072]{2,1,0:T(8,128)(2,1)}, u32[]{:S(2)}, u32[]{:S(2)}) async-start(bf16[4,128,3072]{2,1,0:T(8,128)(2,1)} %copies.1), calls=%async_computation | async-start | bytes 6291456 | tf_op jit(solution)/shard_map/all_to_all | solution.py:171
  17.4 46.8 %all-gather.1 = f16[3072,384]{1,0:T(8,128)(2,1)S(1)} all-gather(f16[192,384]{1,0:T(8,128)(2,1)S(1)} %pad_maximum_fusion), channel_id=1, replica_groups={{0,48,64,112,144,160,208,224,256,304,320,368,400,416,464,480},{16,32,80..., dimensions={0}, use_global_device_ids=true | all-gather | bytes 2506752 | tf_op jit(solution)/shard_map/all_gather | solution.py:174
  64.2 0.6 multiply_convert_fusion.w_ref
  64.8 0.0 all-to-all-done
  64.8 2.9 %collective-permute-start.1 = (bf16[4,128,3072]{2,1,0:T(8,128)(2,1)}, bf16[4,128,3072]{2,1,0:T(8,128)(2,1)S(1)}, u32[]{:S(2)}, u32[]{:S(2)}) collective-permute-start(bf16[4,128,3072]{2,1,0:T(8,128)(2,1)} %all-to-all-done), channel_id=1, source_target_pairs={{0,16},{16,0},{32,48},{48,32},{64,80},{80,64},{96,112},{112,96},{1... | collective-permute-start | bytes 9437192 | tf_op jit(solution)/shard_map/ppermute | solution.py:177
  67.7 4.1 %first.1 = (bf16[512,128]{1,0:T(8,128)(2,1)S(1)}, f32[512,128]{1,0:T(8,128)S(1)}, f32[4,128,128]{2,1,0:T(8,128)S(1)}) custom-call(bf16[512,3072]{1,0:T(8,128)(2,1)} %bitcast.3.t_ref, bf16[3072,384]{1,0:T(8,128)(2,1)S(1)} %multiply_convert_fusion.w_ref), custom_call_target="tpu_custom_call" | custom-call | tf_op jit(solution)/shard_map/first/pallas_call | solution.py:147
  71.8 1.4 %collective-permute-done.1 = bf16[4,128,3072]{2,1,0:T(8,128)(2,1)S(1)} collective-permute-done((bf16[4,128,3072]{2,1,0:T(8,128)(2,1)}, bf16[4,128,3072]{2,1,0:T(8,128)(2,1)S(1)}, u32[]{:S(2)}, u32[]{:S(2)}) %collective-permute-start.1) | collective-permute-done | bytes 3145760 | tf_op jit(solution)/shard_map/ppermute | solution.py:177
  73.2 1.2 %second.1 = (bf16[512,128]{1,0:T(8,128)(2,1)S(1)}, bf16[512,128]{1,0:T(8,128)(2,1)S(1)}, f32[4,128,128]{2,1,0:T(8,128)S(1)}, bf16[4,128,128]{2,1,0:T(8,128)(2,1)S(1)}) custom-call(bf16[512,3072]{1,0:T(8,128)(2,1)S(1)} %bitcast.7, bf16[3072,384]{1,0:T(8,128)(2,1)S(1)} %multiply_convert_fusion.w_ref, f32[4,128,128]{2,1,0:T(8,128)S(1)} %get-tuple-element.67.sa_ref), custom_call_target="tpu_custom_call" | custom-call | tf_op jit(solution)/shard_map/second/pallas_call | solution.py:147
  74.4 8.1 %all_to_all.20.r_ref = bf16[4,128,128]{2,1,0:T(8,128)(2,1)S(1)} all-to-all(bf16[4,128,128]{2,1,0:T(8,128)(2,1)S(1)} %get-tuple-element.52), channel_id=1, replica_groups={{0,48,64,112},{16,32,80,96},{144,160,208,224},{128,176,192,240},{256,30..., dimensions={0} | all-to-all | bytes 262144 | tf_op jit(solution)/shard_map/all_to_all | solution.py:187
  82.5 0.0 copy-start.1
  82.5 4.8 %collective-permute-start.2 = (bf16[128,128]{1,0:T(8,128)(2,1)S(1)}, bf16[128,128]{1,0:T(8,128)(2,1)S(1)}, u32[]{:S(2)}, u32[]{:S(2)}) collective-permute-start(bf16[128,128]{1,0:T(8,128)(2,1)S(1)} %total.1), channel_id=1, source_target_pairs={{0,400},{16,384},{48,416},{32,432},{64,464},{80,448},{112,480},{96... | collective-permute-start | bytes 98312 | tf_op jit(solution)/shard_map/ppermute | solution.py:190
  87.4 3.0 %collective-permute-start.3 = (bf16[128,128]{1,0:T(8,128)(2,1)S(1)}, bf16[128,128]{1,0:T(8,128)(2,1)S(1)}, u32[]{:S(2)}, u32[]{:S(2)}) collective-permute-start(bf16[128,128]{1,0:T(8,128)(2,1)S(1)} %total.1), channel_id=1, source_target_pairs={{0,256},{16,272},{48,304},{32,288},{64,320},{80,336},{112,368},{96... | collective-permute-start | bytes 98312 | tf_op jit(solution)/shard_map/ppermute | solution.py:190
  90.3 5.6 %collective-permute-start.4 = (bf16[128,128]{1,0:T(8,128)(2,1)S(1)}, bf16[128,128]{1,0:T(8,128)(2,1)S(1)}, u32[]{:S(2)}, u32[]{:S(2)}) collective-permute-start(bf16[128,128]{1,0:T(8,128)(2,1)S(1)} %total.1), channel_id=1, source_target_pairs={{0,144},{16,128},{48,160},{32,176},{64,208},{80,192},{112,224},{96... | collective-permute-start | bytes 98312 | tf_op jit(solution)/shard_map/ppermute | solution.py:190
  95.9 1.6 %late.1 = (bf16[512,128]{1,0:T(8,128)(2,1)S(1)}, f32[512,128]{1,0:T(8,128)S(1)}) custom-call(bf16[512,3072]{1,0:T(8,128)(2,1)S(1)} %bitcast.8, bf16[3072,384]{1,0:T(8,128)(2,1)S(1)} %multiply_convert_fusion.w_ref, bf16[512,128]{1,0:T(8,128)(2,1)S(1)} %get-tuple-element.57.k_ref, bf16[512,128]{1,0:T(8,128)(2,1)S(1)} %get-tuple-element.58.v_ref), custom_call_target="tpu_custom_call" | custom-call | tf_op jit(solution)/shard_map/late/pallas_call | solution.py:147
  97.6 0.0 collective-permute-done.2.one_ref
  97.6 0.0 collective-permute-done.3.two_ref
  97.6 0.0 collective-permute-done.4.three_ref
  97.7 8.6 %all_to_all.21.before_ref = bf16[4,128,128]{2,1,0:T(8,128)(2,1)S(1)} all-to-all(bf16[4,128,128]{2,1,0:T(8,128)(2,1)S(1)} %parts.1), channel_id=1, replica_groups={{0,48,64,112},{16,32,80,96},{144,160,208,224},{128,176,192,240},{256,30..., dimensions={0} | all-to-all | bytes 262144 | tf_op jit(solution)/shard_map/all_to_all | solution.py:194
  106.2 0.0 copy-done.1
  106.2 0.4 final.1
  106.6 11.8 %all_to_all.22.i_ref = bf16[8,128,128]{2,1,0:T(8,128)(2,1)S(1)} all-to-all(bf16[8,128,128]{2,1,0:T(8,128)(2,1)S(1)} %bitcast.9), channel_id=1, replica_groups={{0,16,1,17,2,18,3,19},{48,32,49,33,50,34,51,35},{64,80,65,81,66,82,67,8..., dimensions={0} | all-to-all | bytes 524288 | tf_op jit(solution)/shard_map/all_to_all | solution.py:199
  118.4 0.8 join.1
  (6 shorter events, 0.2 us)
Async XLA Ops:
  0.0 0.9 copy-start
  1.0 11.6 %collective-permute-start = (f16[96,384]{1,0:T(8,128)(2,1)S(1)}, f16[96,384]{1,0:T(8,128)(2,1)S(1)}, u32[]{:S(2)}, u32[]{:S(2)}) collective-permute-start(f16[96,384]{1,0:T(8,128)(2,1)S(1)} %multiply_convert_fusion.2), channel_id=1, source_target_pairs={{0,16},{16,0},{32,48},{48,32},{64,80},{80,64},{96,112},{112,96},{1... | collective-permute-start | bytes 221192 | tf_op jit(solution)/shard_map/ppermute | solution.py:165
  12.6 52.2 %all-to-all-start = ((bf16[4,128,3072]{2,1,0:T(8,128)(2,1)}), bf16[4,128,3072]{2,1,0:T(8,128)(2,1)}, u32[]{:S(2)}, u32[]{:S(2)}) async-start(bf16[4,128,3072]{2,1,0:T(8,128)(2,1)} %copies.1), calls=%async_computation | async-start | bytes 6291456 | tf_op jit(solution)/shard_map/all_to_all | solution.py:171
  64.8 8.4 %collective-permute-start.1 = (bf16[4,128,3072]{2,1,0:T(8,128)(2,1)}, bf16[4,128,3072]{2,1,0:T(8,128)(2,1)S(1)}, u32[]{:S(2)}, u32[]{:S(2)}) collective-permute-start(bf16[4,128,3072]{2,1,0:T(8,128)(2,1)} %all-to-all-done), channel_id=1, source_target_pairs={{0,16},{16,0},{32,48},{48,32},{64,80},{80,64},{96,112},{112,96},{1... | collective-permute-start | bytes 9437192 | tf_op jit(solution)/shard_map/ppermute | solution.py:177
  82.5 23.7 %copy-start.1 = (f32[256]{0:T(256)S(1)}, f32[256]{0:T(256)}, u32[]{:S(2)}) copy-start(f32[256]{0:T(256)} %param.5) | copy-start | bytes 3076
  82.5 15.1 %collective-permute-start.2 = (bf16[128,128]{1,0:T(8,128)(2,1)S(1)}, bf16[128,128]{1,0:T(8,128)(2,1)S(1)}, u32[]{:S(2)}, u32[]{:S(2)}) collective-permute-start(bf16[128,128]{1,0:T(8,128)(2,1)S(1)} %total.1), channel_id=1, source_target_pairs={{0,400},{16,384},{48,416},{32,432},{64,464},{80,448},{112,480},{96... | collective-permute-start | bytes 98312 | tf_op jit(solution)/shard_map/ppermute | solution.py:190
  87.4 10.2 %collective-permute-start.3 = (bf16[128,128]{1,0:T(8,128)(2,1)S(1)}, bf16[128,128]{1,0:T(8,128)(2,1)S(1)}, u32[]{:S(2)}, u32[]{:S(2)}) collective-permute-start(bf16[128,128]{1,0:T(8,128)(2,1)S(1)} %total.1), channel_id=1, source_target_pairs={{0,256},{16,272},{48,304},{32,288},{64,320},{80,336},{112,368},{96... | collective-permute-start | bytes 98312 | tf_op jit(solution)/shard_map/ppermute | solution.py:190
  90.3 7.3 %collective-permute-start.4 = (bf16[128,128]{1,0:T(8,128)(2,1)S(1)}, bf16[128,128]{1,0:T(8,128)(2,1)S(1)}, u32[]{:S(2)}, u32[]{:S(2)}) collective-permute-start(bf16[128,128]{1,0:T(8,128)(2,1)S(1)} %total.1), channel_id=1, source_target_pairs={{0,144},{16,128},{48,160},{32,176},{64,208},{80,192},{112,224},{96... | collective-permute-start | bytes 98312 | tf_op jit(solution)/shard_map/ppermute | solution.py:190

commit v12 on v11

--- a/solution.py
+++ b/solution.py
@@ -25,7 +25,7 @@
 
 
 SAME_HEAD = [[holder(z, h) for z in range(16)] for h in range(2)]
-FORWARD = [[(holder(z, h), holder(z + d, h)) for z in range(16 - d) for h in range(2)] for d in (12, 8, 4)]
+FORWARD = [[(holder(z, h), holder(z + d, h)) for z in range(16 - d) for h in range(2)] for d in (8, 4, 12)]
 OWNERS = [[holder(z, h) * 4 + y for y in range(4) for h in range(2)] for z in range(16)]
 VMEM = pl.BlockSpec(memory_space=pltpu.VMEM)
 SMEM = pl.BlockSpec(memory_space=pltpu.SMEM)

time: 120 us -> 121 us (level)
  waiting for transfers between devices: 1.43 us -> 2.71 us
    ppermute x3, waiting for transfers between devices: 0.01 us -> 1.29 us  [body(): earlier = [lax.ppermute(total, 'seq', route) for route in FORWARD]]
  transfers between devices with their start and end apart: 6 -> 6, of which waited for: 1 -> 2; matrix products, arithmetic and copies ran while one was open for 1% -> 1% of each run, Pallas kernels for 7% -> 7%
where the time goes in v12:
time: 121 us; the launch traced here: 120 us
  blocking collectives  75.2 us (62%)
  starting transfers between devices  29.8 us (25%)
  Pallas kernels  11 us (9%)
  waiting for transfers between devices  2.71 us (2%)
    all_gather x1, blocking collectives, body(): lax.all_gather(pair, 'seq', axis=0, tiled=True, axis_index_groups=SAME_HEAD)  46.8 us
    ppermute x3, starting transfers between devices, body(): earlier = [lax.ppermute(total, 'seq', route) for route in FORWARD]  13.4 us
    all_to_all x1, blocking collectives, body(): lax.all_to_all(out.reshape(8, BLOCK, DH), ('seq', 'dp'), 0, 0, tiled=True...  11.5 us
    pallas_call x9, Pallas kernels, call(): pl.pallas_call(kernel, name=name, out_shape=[jax.ShapeDtypeStruct(s, d) f...  11 us
    all_to_all x1, blocking collectives, body(): lax.all_to_all(parts, 'seq', 0, 0, tiled=True, axis_index_groups=QUAD)  8.9 us
    ppermute x1, starting transfers between devices, body(): got = lax.ppermute(to_half(give), 'seq', SIBLING)  8.79 us
    all_to_all x1, blocking collectives, body(): lax.all_to_all(chip, 'seq', 0, 0, tiled=True, axis_index_groups=QUAD)  8.09 us
    all_to_all x1, starting transfers between devices, body(): mine_t = lax.all_to_all(copies, 'dp', 0, 0, tiled=True)  4.67 us
  transfers between devices with their start and end apart: 6, of which 2 were waited for; matrix products, arithmetic and copies ran while one was open for 1% of the time, Pallas kernels for 7%

profile of v12, /device:TPU:1, one launch (start us, length us, event | category | flops | bytes accessed | tf_op | source)
XLA Modules:
  0.0 120.4 jit_solution(7888023203916157427)
XLA Ops:
  0.0 0.0 copy-start
  0.0 0.9 copy-done
  1.0 8.8 %collective-permute-start = (f16[96,384]{1,0:T(8,128)(2,1)S(1)}, f16[96,384]{1,0:T(8,128)(2,1)S(1)}, u32[]{:S(2)}, u32[]{:S(2)}) collective-permute-start(f16[96,384]{1,0:T(8,128)(2,1)S(1)} %multiply_convert_fusion.2), channel_id=1, source_target_pairs={{0,16},{16,0},{32,48},{48,32},{64,80},{80,64},{96,112},{112,96},{1... | collective-permute-start | bytes 221192 | tf_op jit(solution)/shard_map/ppermute | solution.py:165
  9.8 2.8 %copies.1 = bf16[4,128,3072]{2,1,0:T(8,128)(2,1)} custom-call(bf16[128,3072]{1,0:T(8,128)(2,1)} %bitcast.11), custom_call_target="tpu_custom_call" | custom-call | tf_op jit(solution)/shard_map/copies/pallas_call | solution.py:147
  12.6 0.0 collective-permute-done
  12.6 4.7 %all-to-all-start = ((bf16[4,128,3072]{2,1,0:T(8,128)(2,1)}), bf16[4,128,3072]{2,1,0:T(8,128)(2,1)}, u32[]{:S(2)}, u32[]{:S(2)}) async-start(bf16[4,128,3072]{2,1,0:T(8,128)(2,1)} %copies.1), calls=%async_computation | async-start | bytes 6291456 | tf_op jit(solution)/shard_map/all_to_all | solution.py:171
  17.4 46.8 %all-gather.1 = f16[3072,384]{1,0:T(8,128)(2,1)S(1)} all-gather(f16[192,384]{1,0:T(8,128)(2,1)S(1)} %pad_maximum_fusion), channel_id=1, replica_groups={{0,48,64,112,144,160,208,224,256,304,320,368,400,416,464,480},{16,32,80..., dimensions={0}, use_global_device_ids=true | all-gather | bytes 2506752 | tf_op jit(solution)/shard_map/all_gather | solution.py:174
  64.2 0.6 multiply_convert_fusion.w_ref
  64.8 0.0 all-to-all-done
  64.8 2.9 %collective-permute-start.1 = (bf16[4,128,3072]{2,1,0:T(8,128)(2,1)}, bf16[4,128,3072]{2,1,0:T(8,128)(2,1)S(1)}, u32[]{:S(2)}, u32[]{:S(2)}) collective-permute-start(bf16[4,128,3072]{2,1,0:T(8,128)(2,1)} %all-to-all-done), channel_id=1, source_target_pairs={{0,16},{16,0},{32,48},{48,32},{64,80},{80,64},{96,112},{112,96},{1... | collective-permute-start | bytes 9437192 | tf_op jit(solution)/shard_map/ppermute | solution.py:177
  67.7 4.1 %first.1 = (bf16[512,128]{1,0:T(8,128)(2,1)S(1)}, f32[512,128]{1,0:T(8,128)S(1)}, f32[4,128,128]{2,1,0:T(8,128)S(1)}) custom-call(bf16[512,3072]{1,0:T(8,128)(2,1)} %bitcast.3.t_ref, bf16[3072,384]{1,0:T(8,128)(2,1)S(1)} %multiply_convert_fusion.w_ref), custom_call_target="tpu_custom_call" | custom-call | tf_op jit(solution)/shard_map/first/pallas_call | solution.py:147
  71.8 1.4 %collective-permute-done.1 = bf16[4,128,3072]{2,1,0:T(8,128)(2,1)S(1)} collective-permute-done((bf16[4,128,3072]{2,1,0:T(8,128)(2,1)}, bf16[4,128,3072]{2,1,0:T(8,128)(2,1)S(1)}, u32[]{:S(2)}, u32[]{:S(2)}) %collective-permute-start.1) | collective-permute-done | bytes 3145760 | tf_op jit(solution)/shard_map/ppermute | solution.py:177
  73.2 1.2 second.1
  74.4 8.1 %all_to_all.20.r_ref = bf16[4,128,128]{2,1,0:T(8,128)(2,1)S(1)} all-to-all(bf16[4,128,128]{2,1,0:T(8,128)(2,1)S(1)} %get-tuple-element.52), channel_id=1, replica_groups={{0,48,64,112},{16,32,80,96},{144,160,208,224},{128,176,192,240},{256,30..., dimensions={0} | all-to-all | bytes 262144 | tf_op jit(solution)/shard_map/all_to_all | solution.py:187
  82.5 0.0 copy-start.1
  82.5 7.1 %collective-permute-start.2 = (bf16[128,128]{1,0:T(8,128)(2,1)S(1)}, bf16[128,128]{1,0:T(8,128)(2,1)S(1)}, u32[]{:S(2)}, u32[]{:S(2)}) collective-permute-start(bf16[128,128]{1,0:T(8,128)(2,1)S(1)} %total.1), channel_id=1, source_target_pairs={{0,256},{16,272},{48,304},{32,288},{64,320},{80,336},{112,368},{96... | collective-permute-start | bytes 98312 | tf_op jit(solution)/shard_map/ppermute | solution.py:190
  89.6 5.0 %collective-permute-start.3 = (bf16[128,128]{1,0:T(8,128)(2,1)S(1)}, bf16[128,128]{1,0:T(8,128)(2,1)S(1)}, u32[]{:S(2)}, u32[]{:S(2)}) collective-permute-start(bf16[128,128]{1,0:T(8,128)(2,1)S(1)} %total.1), channel_id=1, source_target_pairs={{0,144},{16,128},{48,160},{32,176},{64,208},{80,192},{112,224},{96... | collective-permute-start | bytes 98312 | tf_op jit(solution)/shard_map/ppermute | solution.py:190
  94.6 1.3 %collective-permute-start.4 = (bf16[128,128]{1,0:T(8,128)(2,1)S(1)}, bf16[128,128]{1,0:T(8,128)(2,1)S(1)}, u32[]{:S(2)}, u32[]{:S(2)}) collective-permute-start(bf16[128,128]{1,0:T(8,128)(2,1)S(1)} %total.1), channel_id=1, source_target_pairs={{0,400},{16,384},{48,416},{32,432},{64,464},{80,448},{112,480},{96... | collective-permute-start | bytes 98312 | tf_op jit(solution)/shard_map/ppermute | solution.py:190
  95.9 1.6 %late.1 = (bf16[512,128]{1,0:T(8,128)(2,1)S(1)}, f32[512,128]{1,0:T(8,128)S(1)}) custom-call(bf16[512,3072]{1,0:T(8,128)(2,1)S(1)} %bitcast.8, bf16[3072,384]{1,0:T(8,128)(2,1)S(1)} %multiply_convert_fusion.w_ref, bf16[512,128]{1,0:T(8,128)(2,1)S(1)} %get-tuple-element.57.k_ref, bf16[512,128]{1,0:T(8,128)(2,1)S(1)} %get-tuple-element.58.v_ref), custom_call_target="tpu_custom_call" | custom-call | tf_op jit(solution)/shard_map/late/pallas_call | solution.py:147
  97.6 0.0 collective-permute-done.2.one_ref
  97.6 0.0 collective-permute-done.3.two_ref
  97.6 1.3 %collective-permute-done.4.three_ref = bf16[128,128]{1,0:T(8,128)(2,1)S(1)} collective-permute-done((bf16[128,128]{1,0:T(8,128)(2,1)S(1)}, bf16[128,128]{1,0:T(8,128)(2,1)S(1)}, u32[]{:S(2)}, u32[]{:S(2)}) %collective-permute-start.4) | collective-permute-done | bytes 32800 | tf_op jit(solution)/shard_map/ppermute | solution.py:190
  98.9 8.9 %all_to_all.21.before_ref = bf16[4,128,128]{2,1,0:T(8,128)(2,1)S(1)} all-to-all(bf16[4,128,128]{2,1,0:T(8,128)(2,1)S(1)} %parts.1), channel_id=1, replica_groups={{0,48,64,112},{16,32,80,96},{144,160,208,224},{128,176,192,240},{256,30..., dimensions={0} | all-to-all | bytes 262144 | tf_op jit(solution)/shard_map/all_to_all | solution.py:194
  107.8 0.0 copy-done.1
  107.8 0.4 final.1
  108.2 11.5 %all_to_all.22.i_ref = bf16[8,128,128]{2,1,0:T(8,128)(2,1)S(1)} all-to-all(bf16[8,128,128]{2,1,0:T(8,128)(2,1)S(1)} %bitcast.9), channel_id=1, replica_groups={{0,16,1,17,2,18,3,19},{48,32,49,33,50,34,51,35},{64,80,65,81,66,82,67,8..., dimensions={0} | all-to-all | bytes 524288 | tf_op jit(solution)/shard_map/all_to_all | solution.py:199
  119.7 0.8 join.1
  (6 shorter events, 0.2 us)
Async XLA Ops:
  0.0 0.9 copy-start
  1.0 11.6 %collective-permute-start = (f16[96,384]{1,0:T(8,128)(2,1)S(1)}, f16[96,384]{1,0:T(8,128)(2,1)S(1)}, u32[]{:S(2)}, u32[]{:S(2)}) collective-permute-start(f16[96,384]{1,0:T(8,128)(2,1)S(1)} %multiply_convert_fusion.2), channel_id=1, source_target_pairs={{0,16},{16,0},{32,48},{48,32},{64,80},{80,64},{96,112},{112,96},{1... | collective-permute-start | bytes 221192 | tf_op jit(solution)/shard_map/ppermute | solution.py:165
  12.6 52.2 %all-to-all-start = ((bf16[4,128,3072]{2,1,0:T(8,128)(2,1)}), bf16[4,128,3072]{2,1,0:T(8,128)(2,1)}, u32[]{:S(2)}, u32[]{:S(2)}) async-start(bf16[4,128,3072]{2,1,0:T(8,128)(2,1)} %copies.1), calls=%async_computation | async-start | bytes 6291456 | tf_op jit(solution)/shard_map/all_to_all | solution.py:171
  64.8 8.4 %collective-permute-start.1 = (bf16[4,128,3072]{2,1,0:T(8,128)(2,1)}, bf16[4,128,3072]{2,1,0:T(8,128)(2,1)S(1)}, u32[]{:S(2)}, u32[]{:S(2)}) collective-permute-start(bf16[4,128,3072]{2,1,0:T(8,128)(2,1)} %all-to-all-done), channel_id=1, source_target_pairs={{0,16},{16,0},{32,48},{48,32},{64,80},{80,64},{96,112},{112,96},{1... | collective-permute-start | bytes 9437192 | tf_op jit(solution)/shard_map/ppermute | solution.py:177
  82.5 25.3 %copy-start.1 = (f32[256]{0:T(256)S(1)}, f32[256]{0:T(256)}, u32[]{:S(2)}) copy-start(f32[256]{0:T(256)} %param.5) | copy-start | bytes 3076
  82.5 15.1 %collective-permute-start.2 = (bf16[128,128]{1,0:T(8,128)(2,1)S(1)}, bf16[128,128]{1,0:T(8,128)(2,1)S(1)}, u32[]{:S(2)}, u32[]{:S(2)}) collective-permute-start(bf16[128,128]{1,0:T(8,128)(2,1)S(1)} %total.1), channel_id=1, source_target_pairs={{0,256},{16,272},{48,304},{32,288},{64,320},{80,336},{112,368},{96... | collective-permute-start | bytes 98312 | tf_op jit(solution)/shard_map/ppermute | solution.py:190
  89.6 8.0 %collective-permute-start.3 = (bf16[128,128]{1,0:T(8,128)(2,1)S(1)}, bf16[128,128]{1,0:T(8,128)(2,1)S(1)}, u32[]{:S(2)}, u32[]{:S(2)}) collective-permute-start(bf16[128,128]{1,0:T(8,128)(2,1)S(1)} %total.1), channel_id=1, source_target_pairs={{0,144},{16,128},{48,160},{32,176},{64,208},{80,192},{112,224},{96... | collective-permute-start | bytes 98312 | tf_op jit(solution)/shard_map/ppermute | solution.py:190
  94.6 4.3 %collective-permute-start.4 = (bf16[128,128]{1,0:T(8,128)(2,1)S(1)}, bf16[128,128]{1,0:T(8,128)(2,1)S(1)}, u32[]{:S(2)}, u32[]{:S(2)}) collective-permute-start(bf16[128,128]{1,0:T(8,128)(2,1)S(1)} %total.1), channel_id=1, source_target_pairs={{0,400},{16,384},{48,416},{32,432},{64,464},{80,448},{112,480},{96... | collective-permute-start | bytes 98312 | tf_op jit(solution)/shard_map/ppermute | solution.py:190

commit v13 on v10

--- a/solution.py
+++ b/solution.py
@@ -16,12 +16,12 @@
 
 
 def holder(z, head):
-    return 2 * z + (head ^ ((z ^ (z >> 2)) & 1))
+    return 2 * z + head
 
 
 QUAD = [[holder(4 * a + b, h) for b in range(4)] for a in range(4) for h in range(2)]
 def head_of(place):
-    return (place ^ (place >> 1) ^ (place >> 3)) & 1
+    return place & 1
 
 
 SAME_HEAD = [[holder(z, h) for z in range(16)] for h in range(2)]

time: 119 us -> 120 us (level)
  starting transfers between devices: 29.1 us -> 33.4 us
  blocking collectives: 75.2 us -> 71.5 us
    all_gather x1, blocking collectives: 46.8 us -> 40.3 us  [body(): lax.all_gather(pair, 'seq', axis=0, tiled=True, axis_index_groups=SAME_HEAD)]
    ppermute x1, starting transfers between devices: 2.93 us -> 7.14 us  [body(): other_t = lax.ppermute(mine_t, 'seq', SIBLING)]
    all_to_all x1, blocking collectives: 11.8 us -> 15.9 us  [body(): lax.all_to_all(out.reshape(8, BLOCK, DH), ('seq', 'dp'), 0, 0, tiled=True...]
where the time goes in v13:
time: 120 us; the launch traced here: 119 us
  blocking collectives  71.5 us (60%)
  starting transfers between devices  33.4 us (28%)
  Pallas kernels  11 us (9%)
  waiting for transfers between devices  1.43 us (1%)
    all_gather x1, blocking collectives, body(): lax.all_gather(pair, 'seq', axis=0, tiled=True, axis_index_groups=SAME_HEAD)  40.3 us
    all_to_all x1, blocking collectives, body(): lax.all_to_all(out.reshape(8, BLOCK, DH), ('seq', 'dp'), 0, 0, tiled=True...  15.9 us
    ppermute x3, starting transfers between devices, body(): earlier = [lax.ppermute(total, 'seq', route) for route in FORWARD]  12.8 us
    pallas_call x9, Pallas kernels, call(): pl.pallas_call(kernel, name=name, out_shape=[jax.ShapeDtypeStruct(s, d) f...  11 us
    ppermute x1, starting transfers between devices, body(): got = lax.ppermute(to_half(give), 'seq', SIBLING)  8.79 us
    all_to_all x1, blocking collectives, body(): lax.all_to_all(parts, 'seq', 0, 0, tiled=True, axis_index_groups=QUAD)  8.16 us
    all_to_all x1, blocking collectives, body(): lax.all_to_all(chip, 'seq', 0, 0, tiled=True, axis_index_groups=QUAD)  7.19 us
    ppermute x1, starting transfers between devices, body(): other_t = lax.ppermute(mine_t, 'seq', SIBLING)  7.14 us
  transfers between devices with their start and end apart: 6, of which 1 were waited for; matrix products, arithmetic and copies ran while one was open for 1% of the time, Pallas kernels for 7%

profile of v13, /device:TPU:1, one launch (start us, length us, event | category | flops | bytes accessed | tf_op | source)
XLA Modules:
  0.0 119.1 jit_solution(4140665939561069508)
XLA Ops:
  0.0 0.0 copy-start
  0.0 0.9 copy-done
  1.0 8.8 %collective-permute-start = (f16[96,384]{1,0:T(8,128)(2,1)S(1)}, f16[96,384]{1,0:T(8,128)(2,1)S(1)}, u32[]{:S(2)}, u32[]{:S(2)}) collective-permute-start(f16[96,384]{1,0:T(8,128)(2,1)S(1)} %multiply_convert_fusion.2), channel_id=1, source_target_pairs={{0,16},{16,0},{32,48},{48,32},{64,80},{80,64},{96,112},{112,96},{1... | collective-permute-start | bytes 221192 | tf_op jit(solution)/shard_map/ppermute | solution.py:165
  9.8 2.8 %copies.1 = bf16[4,128,3072]{2,1,0:T(8,128)(2,1)} custom-call(bf16[128,3072]{1,0:T(8,128)(2,1)} %bitcast.11), custom_call_target="tpu_custom_call" | custom-call | tf_op jit(solution)/shard_map/copies/pallas_call | solution.py:147
  12.6 0.0 collective-permute-done
  12.6 4.7 %all-to-all-start = ((bf16[4,128,3072]{2,1,0:T(8,128)(2,1)}), bf16[4,128,3072]{2,1,0:T(8,128)(2,1)}, u32[]{:S(2)}, u32[]{:S(2)}) async-start(bf16[4,128,3072]{2,1,0:T(8,128)(2,1)} %copies.1), calls=%async_computation | async-start | bytes 6291456 | tf_op jit(solution)/shard_map/all_to_all | solution.py:171
  17.4 40.3 %all-gather.1 = f16[3072,384]{1,0:T(8,128)(2,1)S(1)} all-gather(f16[192,384]{1,0:T(8,128)(2,1)S(1)} %pad_maximum_fusion), channel_id=1, replica_groups={{0,32,64,96,128,160,192,224,256,288,320,352,384,416,448,480},{16,48,80,..., dimensions={0}, use_global_device_ids=true | all-gather | bytes 2506752 | tf_op jit(solution)/shard_map/all_gather | solution.py:174
  57.7 0.6 multiply_convert_fusion.w_ref
  58.3 0.0 all-to-all-done
  58.4 7.1 %collective-permute-start.1 = (bf16[4,128,3072]{2,1,0:T(8,128)(2,1)}, bf16[4,128,3072]{2,1,0:T(8,128)(2,1)S(1)}, u32[]{:S(2)}, u32[]{:S(2)}) collective-permute-start(bf16[4,128,3072]{2,1,0:T(8,128)(2,1)} %all-to-all-done), channel_id=1, source_target_pairs={{0,16},{16,0},{32,48},{48,32},{64,80},{80,64},{96,112},{112,96},{1... | collective-permute-start | bytes 9437192 | tf_op jit(solution)/shard_map/ppermute | solution.py:177
  65.5 4.1 %first.1 = (bf16[512,128]{1,0:T(8,128)(2,1)S(1)}, f32[512,128]{1,0:T(8,128)S(1)}, f32[4,128,128]{2,1,0:T(8,128)S(1)}) custom-call(bf16[512,3072]{1,0:T(8,128)(2,1)} %bitcast.3.t_ref, bf16[3072,384]{1,0:T(8,128)(2,1)S(1)} %multiply_convert_fusion.w_ref), custom_call_target="tpu_custom_call" | custom-call | tf_op jit(solution)/shard_map/first/pallas_call | solution.py:147
  69.6 1.4 %collective-permute-done.1 = bf16[4,128,3072]{2,1,0:T(8,128)(2,1)S(1)} collective-permute-done((bf16[4,128,3072]{2,1,0:T(8,128)(2,1)}, bf16[4,128,3072]{2,1,0:T(8,128)(2,1)S(1)}, u32[]{:S(2)}, u32[]{:S(2)}) %collective-permute-start.1) | collective-permute-done | bytes 3145760 | tf_op jit(solution)/shard_map/ppermute | solution.py:177
  71.0 1.2 %second.1 = (bf16[512,128]{1,0:T(8,128)(2,1)S(1)}, bf16[512,128]{1,0:T(8,128)(2,1)S(1)}, f32[4,128,128]{2,1,0:T(8,128)S(1)}, bf16[4,128,128]{2,1,0:T(8,128)(2,1)S(1)}) custom-call(bf16[512,3072]{1,0:T(8,128)(2,1)S(1)} %bitcast.7, bf16[3072,384]{1,0:T(8,128)(2,1)S(1)} %multiply_convert_fusion.w_ref, f32[4,128,128]{2,1,0:T(8,128)S(1)} %get-tuple-element.67.sa_ref), custom_call_target="tpu_custom_call" | custom-call | tf_op jit(solution)/shard_map/second/pallas_call | solution.py:147
  72.2 7.2 %all_to_all.20.r_ref = bf16[4,128,128]{2,1,0:T(8,128)(2,1)S(1)} all-to-all(bf16[4,128,128]{2,1,0:T(8,128)(2,1)S(1)} %get-tuple-element.52), channel_id=1, replica_groups={{0,32,64,96},{16,48,80,112},{128,160,192,224},{144,176,208,240},{256,28..., dimensions={0} | all-to-all | bytes 262144 | tf_op jit(solution)/shard_map/all_to_all | solution.py:187
  79.4 0.0 copy-start.1
  79.4 7.5 %collective-permute-start.2 = (bf16[128,128]{1,0:T(8,128)(2,1)S(1)}, bf16[128,128]{1,0:T(8,128)(2,1)S(1)}, u32[]{:S(2)}, u32[]{:S(2)}) collective-permute-start(bf16[128,128]{1,0:T(8,128)(2,1)S(1)} %total.1), channel_id=1, source_target_pairs={{0,256},{16,272},{32,288},{48,304},{64,320},{80,336},{96,352},{112... | collective-permute-start | bytes 98312 | tf_op jit(solution)/shard_map/ppermute | solution.py:190
  86.9 1.3 %collective-permute-start.3 = (bf16[128,128]{1,0:T(8,128)(2,1)S(1)}, bf16[128,128]{1,0:T(8,128)(2,1)S(1)}, u32[]{:S(2)}, u32[]{:S(2)}) collective-permute-start(bf16[128,128]{1,0:T(8,128)(2,1)S(1)} %total.1), channel_id=1, source_target_pairs={{0,384},{16,400},{32,416},{48,432},{64,448},{80,464},{96,480},{112... | collective-permute-start | bytes 98312 | tf_op jit(solution)/shard_map/ppermute | solution.py:190
  88.2 4.0 %collective-permute-start.4 = (bf16[128,128]{1,0:T(8,128)(2,1)S(1)}, bf16[128,128]{1,0:T(8,128)(2,1)S(1)}, u32[]{:S(2)}, u32[]{:S(2)}) collective-permute-start(bf16[128,128]{1,0:T(8,128)(2,1)S(1)} %total.1), channel_id=1, source_target_pairs={{0,128},{16,144},{32,160},{48,176},{64,192},{80,208},{96,224},{112... | collective-permute-start | bytes 98312 | tf_op jit(solution)/shard_map/ppermute | solution.py:190
  92.2 1.7 %late.1 = (bf16[512,128]{1,0:T(8,128)(2,1)S(1)}, f32[512,128]{1,0:T(8,128)S(1)}) custom-call(bf16[512,3072]{1,0:T(8,128)(2,1)S(1)} %bitcast.8, bf16[3072,384]{1,0:T(8,128)(2,1)S(1)} %multiply_convert_fusion.w_ref, bf16[512,128]{1,0:T(8,128)(2,1)S(1)} %get-tuple-element.57.k_ref, bf16[512,128]{1,0:T(8,128)(2,1)S(1)} %get-tuple-element.58.v_ref), custom_call_target="tpu_custom_call" | custom-call | tf_op jit(solution)/shard_map/late/pallas_call | solution.py:147
  93.9 0.0 collective-permute-done.2.one_ref
  93.9 0.0 collective-permute-done.3.two_ref
  93.9 0.0 collective-permute-done.4.three_ref
  94.0 8.2 %all_to_all.21.before_ref = bf16[4,128,128]{2,1,0:T(8,128)(2,1)S(1)} all-to-all(bf16[4,128,128]{2,1,0:T(8,128)(2,1)S(1)} %parts.1), channel_id=1, replica_groups={{0,32,64,96},{16,48,80,112},{128,160,192,224},{144,176,208,240},{256,28..., dimensions={0} | all-to-all | bytes 262144 | tf_op jit(solution)/shard_map/all_to_all | solution.py:194
  102.1 0.0 copy-done.1
  102.1 0.4 final.1
  102.5 15.9 %all_to_all.22.i_ref = bf16[8,128,128]{2,1,0:T(8,128)(2,1)S(1)} all-to-all(bf16[8,128,128]{2,1,0:T(8,128)(2,1)S(1)} %bitcast.9), channel_id=1, replica_groups={{0,16,1,17,2,18,3,19},{32,48,33,49,34,50,35,51},{64,80,65,81,66,82,67,8..., dimensions={0} | all-to-all | bytes 524288 | tf_op jit(solution)/shard_map/all_to_all | solution.py:199
  118.4 0.8 join.1
  (6 shorter events, 0.2 us)
Async XLA Ops:
  0.0 0.9 copy-start
  1.0 11.6 %collective-permute-start = (f16[96,384]{1,0:T(8,128)(2,1)S(1)}, f16[96,384]{1,0:T(8,128)(2,1)S(1)}, u32[]{:S(2)}, u32[]{:S(2)}) collective-permute-start(f16[96,384]{1,0:T(8,128)(2,1)S(1)} %multiply_convert_fusion.2), channel_id=1, source_target_pairs={{0,16},{16,0},{32,48},{48,32},{64,80},{80,64},{96,112},{112,96},{1... | collective-permute-start | bytes 221192 | tf_op jit(solution)/shard_map/ppermute | solution.py:165
  12.6 45.7 %all-to-all-start = ((bf16[4,128,3072]{2,1,0:T(8,128)(2,1)}), bf16[4,128,3072]{2,1,0:T(8,128)(2,1)}, u32[]{:S(2)}, u32[]{:S(2)}) async-start(bf16[4,128,3072]{2,1,0:T(8,128)(2,1)} %copies.1), calls=%async_computation | async-start | bytes 6291456 | tf_op jit(solution)/shard_map/all_to_all | solution.py:171
  58.4 12.6 %collective-permute-start.1 = (bf16[4,128,3072]{2,1,0:T(8,128)(2,1)}, bf16[4,128,3072]{2,1,0:T(8,128)(2,1)S(1)}, u32[]{:S(2)}, u32[]{:S(2)}) collective-permute-start(bf16[4,128,3072]{2,1,0:T(8,128)(2,1)} %all-to-all-done), channel_id=1, source_target_pairs={{0,16},{16,0},{32,48},{48,32},{64,80},{80,64},{96,112},{112,96},{1... | collective-permute-start | bytes 9437192 | tf_op jit(solution)/shard_map/ppermute | solution.py:177
  79.4 22.7 %copy-start.1 = (f32[256]{0:T(256)S(1)}, f32[256]{0:T(256)}, u32[]{:S(2)}) copy-start(f32[256]{0:T(256)} %param.5) | copy-start | bytes 3076
  79.4 14.5 %collective-permute-start.2 = (bf16[128,128]{1,0:T(8,128)(2,1)S(1)}, bf16[128,128]{1,0:T(8,128)(2,1)S(1)}, u32[]{:S(2)}, u32[]{:S(2)}) collective-permute-start(bf16[128,128]{1,0:T(8,128)(2,1)S(1)} %total.1), channel_id=1, source_target_pairs={{0,256},{16,272},{32,288},{48,304},{64,320},{80,336},{96,352},{112... | collective-permute-start | bytes 98312 | tf_op jit(solution)/shard_map/ppermute | solution.py:190
  86.9 7.0 %collective-permute-start.3 = (bf16[128,128]{1,0:T(8,128)(2,1)S(1)}, bf16[128,128]{1,0:T(8,128)(2,1)S(1)}, u32[]{:S(2)}, u32[]{:S(2)}) collective-permute-start(bf16[128,128]{1,0:T(8,128)(2,1)S(1)} %total.1), channel_id=1, source_target_pairs={{0,384},{16,400},{32,416},{48,432},{64,448},{80,464},{96,480},{112... | collective-permute-start | bytes 98312 | tf_op jit(solution)/shard_map/ppermute | solution.py:190
  88.2 5.7 %collective-permute-start.4 = (bf16[128,128]{1,0:T(8,128)(2,1)S(1)}, bf16[128,128]{1,0:T(8,128)(2,1)S(1)}, u32[]{:S(2)}, u32[]{:S(2)}) collective-permute-start(bf16[128,128]{1,0:T(8,128)(2,1)S(1)} %total.1), channel_id=1, source_target_pairs={{0,128},{16,144},{32,160},{48,176},{64,192},{80,208},{96,224},{112... | collective-permute-start | bytes 98312 | tf_op jit(solution)/shard_map/ppermute | solution.py:190
